TPU v7x, 128 devices: a whole 4x4x4 slice. The times are simulated.
128 devices in a mesh: brick: 64 (over z_lo, x, y, core), vec: 2 (over z_hi).
Axes of the slice: x: 4, y: 4, z: 4 (z_hi: 2, z_lo: 2; z = z_hi * 2 + z_lo), core: 2. Of those that a mesh axis runs over, the one named last changes fastest.
Arguments:
- levels: int32 [12, 2048, 16, 128], P(None, 'brick'), may hold values from 0 to 255
- start_block: int32 [16, 2048, 16, 128], P('vec', 'brick'), may hold values from -8 to 8
Outputs:
- alpha_blocks: float32 [1, 16, 16], replicated
- beta_blocks: float32 [1, 16, 16], replicated
- basis: float32 [16, 2048, 16, 128], P('vec', 'brick')
All inputs are finite; a program needn't handle non-finite values.
Results may differ from a plain program's by a relative error of at most 0.00026.
Values sent between devices are 32-bit elements; how exact they have to be, the bound alone decides.
No kernel may reach another device: no remote copies, remote signals or barrier semaphores. Data moves between devices by JAX's collectives and lax.ppermute only.
A program may use at most 128 MiB of HBM per device.

v0:
```python
import functools
import math

import jax
import jax.numpy as jnp
from jax import lax
from jax.experimental import pallas as pl
from jax.experimental.pallas import tpu as pltpu
from jax.sharding import PartitionSpec as P


offsets_cube = (1, 3, 9, 27)
deepest = 27
highest = lax.Precision.HIGHEST
chunk = 4
f32 = jnp.float32


ANY = pl.BlockSpec(memory_space=pl.ANY)
SMEM = pl.BlockSpec(memory_space=pltpu.SMEM)
VMEM = pl.BlockSpec(memory_space=pltpu.VMEM)


def params(mib):
    return pltpu.CompilerParams(vmem_limit_bytes=mib << 20)


def shift_rows(value, by):
    length = value.shape[-2]
    if abs(by) >= length:
        return jnp.zeros_like(value)
    rolled = pltpu.roll(value, (-by) % length, value.ndim - 2)
    row = lax.broadcasted_iota(jnp.int32, value.shape, value.ndim - 2) + by
    return jnp.where((row >= 0) & (row < length), rolled, 0.0)


def shift_lanes(value, by):
    length = value.shape[-1]
    if abs(by) >= length:
        return jnp.zeros_like(value)
    rolled = pltpu.roll(value, (-by) % length, value.ndim - 1)
    lane = lax.broadcasted_iota(jnp.int32, value.shape, value.ndim - 1) + by
    return jnp.where((lane >= 0) & (lane < length), rolled, 0.0)


def inverse_root(value):
    guess = lax.rsqrt(value)
    return guess * (1.5 - 0.5 * value * guess * guess)


def to_weight(level):
    return (level.astype(f32) + 0.5) / 256.0


def halo_start(position):
    return sum(offsets_cube[:position])


def tail_kernel(levels_ref, out_ref, raw_ref, sem):
    planes = levels_ref.shape[1]
    copies = []
    for position, offset in enumerate(offsets_cube):
        place = pl.ds(halo_start(position), offset)
        copies.append(
            pltpu.make_async_copy(
                levels_ref.at[position, pl.ds(planes - offset, offset)], raw_ref.at[place], sem.at[position]
            )
        )
    for copy in copies:
        copy.start()
    for copy in copies:
        copy.wait()
    out_ref[...] = to_weight(raw_ref[...])


def degree_kernel(flag_ref, levels_ref, halo_ref, root_ref):
    planes = levels_ref.shape[1]
    inside_above = flag_ref[0].astype(f32)

    def plane(x, _):
        total = jnp.ones(levels_ref.shape[2:], f32)
        for position, offset in enumerate(offsets_cube):
            weight = to_weight(levels_ref[position, x])
            total = total + jnp.where(x + offset < planes, 1.0, inside_above) * weight
            own = to_weight(levels_ref[position, jnp.maximum(x - offset, 0)])
            base = halo_start(position)
            far = halo_ref[base + jnp.minimum(x, offset - 1)]
            total = total + jnp.where(x >= offset, own, far)
            for axis, shift in ((1, shift_rows), (2, shift_lanes)):
                weight = to_weight(levels_ref[4 * axis + position, x])
                ones = shift(jnp.ones_like(weight), offset)
                total = total + ones * weight + shift(weight, -offset)
        root_ref[x] = inverse_root(total)
        return 0

    lax.fori_loop(0, planes, plane, 0, unroll=4)


def weights_kernel(levels_ref, halo_ref, root_ref, above_ref, below_ref, out_ref):
    planes = levels_ref.shape[1]

    def plane(x, _):
        root = root_ref[x]
        half = 0.5 * root
        slot = 0
        for position, offset in enumerate(offsets_cube):
            ahead = jnp.where(
                x + offset < planes,
                root_ref[jnp.minimum(x + offset, planes - 1)],
                above_ref[jnp.maximum(x + offset - planes, 0)],
            )
            out_ref[slot, x] = to_weight(levels_ref[position, x]) * half * ahead
            back = jnp.maximum(x - offset, 0)
            base = halo_start(position)
            weight = jnp.where(
                x >= offset, to_weight(levels_ref[position, back]), halo_ref[base + jnp.minimum(x, offset - 1)]
            )
            behind = jnp.where(
                x >= offset, root_ref[back], below_ref[jnp.clip(deepest + x - offset, 0, deepest - 1)]
            )
            out_ref[slot + 1, x] = weight * half * behind
            slot += 2
        for axis, shift in ((1, shift_rows), (2, shift_lanes)):
            for position, offset in enumerate(offsets_cube):
                if offset >= root.shape[axis - 1]:
                    continue
                weight = to_weight(levels_ref[4 * axis + position, x])
                forward = weight * half * shift(root, offset)
                out_ref[slot, x] = forward
                out_ref[slot + 1, x] = shift(forward, -offset)
                slot += 2
        return 0

    lax.fori_loop(0, planes, plane, 0, unroll=2)


def terms_of(rows, lanes):
    found = [("x", o * s) for o in offsets_cube for s in (1, -1)]
    found += [("y", o * s) for o in offsets_cube if o < rows for s in (1, -1)]
    found += [("z", o * s) for o in offsets_cube if o < lanes for s in (1, -1)]
    return found


def filter_plane(ext_ref, weight_ref, x_local, x_plane, terms, rows, lanes, put):
    for first in range(0, rows, 8):
        base = pl.multiple_of((x_plane + deepest) * rows + first, 8)
        here = ext_ref[:, pl.ds(base, 8), :]
        total = 0.5 * here
        for slot, (kind, by) in enumerate(terms):
            weight = weight_ref[slot, x_local, pl.ds(first, 8)]
            if kind == "x":
                moved = ext_ref[:, pl.ds(base + by * rows, 8), :]
            elif kind == "y":
                moved = ext_ref[:, pl.ds(base + by, 8), :]
            else:
                moved = pltpu.roll(here, (-by) % lanes, 2)
            total = total + weight[None] * moved
        put(first, total)


def load_extended(own_ref, below_ref, above_ref, ext_ref, first, rows):
    count = ext_ref.shape[0]
    edge = deepest * rows
    own_rows = own_ref.shape[1]
    ext_ref[:, pl.ds(0, edge)] = below_ref[...]
    ext_ref[:, pl.ds(edge, own_rows)] = own_ref[pl.ds(first, count)]
    ext_ref[:, pl.ds(edge + own_rows, edge)] = above_ref[...]


def first_filter_kernel(first, terms, rows, lanes, weight_ref, own_ref, below_ref, above_ref,
                        out_ref, low_ref, high_ref, ext_ref):
    planes = weight_ref.shape[1]
    load_extended(own_ref, below_ref, above_ref, ext_ref, first, rows)

    def plane(x, _):
        def put(row, total):
            out_ref[:, x, pl.ds(row, 8)] = total

        filter_plane(ext_ref, weight_ref, x, x, terms, rows, lanes, put)
        return 0

    lax.fori_loop(0, planes, plane, 0, unroll=4)
    low_ref[...] = out_ref[:, :deepest]
    high_ref[...] = out_ref[:, planes - deepest :]


def second_filter_kernel(terms, rows, lanes, vec_ref, weight_ref, own_ref, below_ref, above_ref,
                         theirs_ref, mine_ref, ext_ref):
    halves = theirs_ref.shape[1]
    load_extended(own_ref, below_ref, above_ref, ext_ref, 0, rows)
    for target_ref, start in ((theirs_ref, (1 - vec_ref[0]) * halves), (mine_ref, vec_ref[0] * halves)):

        def plane(i, _, target_ref=target_ref, start=start):
            def put(row, total):
                target_ref[:, i, pl.ds(row, 8)] = total

            filter_plane(ext_ref, weight_ref, start + i, start + i, terms, rows, lanes, put)
            return 0

        lax.fori_loop(0, halves, plane, 0, unroll=4)


def gram_kernel(early, vec_ref, own_x_ref, other_x_ref, *refs):
    if early:
        ys, (out_ref, late_ref, acc_ref) = refs[:2], refs[2:]
        for place, ref in enumerate(ys):
            late_ref[pl.ds(place * chunk, chunk)] = ref[...]
    else:
        ys, (before_ref, out_ref, acc_ref) = refs[:4], refs[4:]
    cols = own_x_ref.shape[0]
    tiles = own_x_ref.shape[1] // 2
    group = chunk
    vec = vec_ref[0]
    acc_ref[...] = jnp.zeros_like(acc_ref)

    def load(kind, number, t):
        if kind == "x":
            ref = own_x_ref if number < 2 else other_x_ref
            return [ref[(number % 2) * group + k, vec * tiles + t] for k in range(group)]
        return [ys[number][k, t] for k in range(group)]

    def block_of_pairs(slot, left_kind, left, right_kind, right):
        same = left == right
        pairs = [(i, j) for i in range(group) for j in range(group) if not (same and j < i)]

        def step(t, accs):
            a = load(left_kind, left, t)
            b = a if same and left_kind == right_kind else load(right_kind, right, t)
            return tuple(acc + a[i] * b[j] for (i, j), acc in zip(pairs, accs))

        zero = tuple(jnp.zeros((8, 128), f32) for _ in pairs)
        accs = lax.fori_loop(0, tiles, step, zero, unroll=4)
        for (i, j), acc in zip(pairs, accs):
            row = jnp.sum(acc, axis=0, keepdims=True)
            gi = lax.rem(left * group + i + cols * vec, 2 * cols)
            gj = lax.rem(right * group + j + cols * vec, 2 * cols)
            acc_ref[slot, pl.ds(gi * 16 + gj, 1), :] = row
            acc_ref[slot, pl.ds(gj * 16 + gi, 1), :] = row

    for left in range(4):
        for right in range(left, 4):
            if early:
                block_of_pairs(0, "x", left, "x", right)
            if (right < 2) == early:
                block_of_pairs(2, "y", left, "y", right)
                if left // 2 == right // 2:
                    block_of_pairs(1, "y", left, "x", right)
            if left // 2 != right // 2:
                if early:

                    @pl.when(vec == 0)
                    def _(left=left, right=right):
                        block_of_pairs(1, "y", left, "x", right)

                else:

                    @pl.when(vec == 1)
                    def _(left=left, right=right):
                        block_of_pairs(1, "y", right, "x", left)

    lane = lax.broadcasted_iota(jnp.int32, (256, 128), 1)
    inner = lax.rem(lax.broadcasted_iota(jnp.int32, (256, 128), 0), 16)
    total = jnp.zeros((16, 128), f32) if early else before_ref[...]
    for slot in range(0 if early else 1, 3):
        sums = jnp.sum(acc_ref[slot], axis=1, keepdims=True)
        placed = jnp.where(lane == inner + 16 * slot, sums, 0.0)
        total = total + jnp.sum(placed.reshape(16, 16, 128), axis=1)
    out_ref[...] = total


def eliminate(square):
    n = square.shape[0]
    row = lax.broadcasted_iota(jnp.int32, (n, n), 0)
    col = lax.broadcasted_iota(jnp.int32, (n, n), 1)
    work = square
    inverse = jnp.where(row == col, 1.0, 0.0).astype(f32)
    columns = jnp.zeros((n, n), f32)
    pivots = jnp.zeros((n, n), f32)
    across = jnp.zeros((n, n), f32)
    for j in range(n):
        column = jnp.broadcast_to(work[:, j : j + 1], (n, n))
        pivot = jnp.broadcast_to(column[j : j + 1, :], (n, n))
        factor = jnp.where(row > j, column, 0.0) / pivot
        columns = jnp.where((col == j) & (row >= j), column, columns)
        pivots = jnp.where(row == j, pivot, pivots)
        across = jnp.where(col == j, pivot, across)
        inverse = inverse - factor * jnp.broadcast_to(inverse[j : j + 1, :], (n, n))
        work = work - factor * jnp.broadcast_to(work[j : j + 1, :], (n, n))
    return columns * inverse_root(across), inverse * inverse_root(pivots)


def times(a, b):
    return jnp.dot(a, b, precision=highest, preferred_element_type=f32)


def times_t(a, b):
    return lax.dot_general(a, b, (((1,), (1,)), ((), ())), precision=highest, preferred_element_type=f32)


def algebra_kernel(scale, vec_ref, gram_ref, alpha_ref, beta_ref, table_ref):
    grams = [gram_ref[:, 16 * k : 16 * k + 16] for k in range(3)]
    _, inverse = eliminate(grams[0])
    coeffs = times_t(times(inverse, grams[1]), inverse)
    image = times_t(times(inverse, grams[2]), inverse)
    factor, second = eliminate(image - times_t(coeffs, coeffs))
    alpha_ref[...] = coeffs
    beta_ref[...] = factor
    of_image = scale * times(second, inverse)
    of_start = -scale * times(times(second, coeffs), inverse)
    first = vec_ref[0] == 0
    for place, mix in ((0, of_start), (16, of_image)):
        mine = jnp.where(first, mix[:8], mix[8:])
        table_ref[:, place : place + 8] = jnp.where(first, mine[:, :8], mine[:, 8:])
        table_ref[:, place + 8 : place + 16] = jnp.where(first, mine[:, 8:], mine[:, :8])


def combine_kernel(vec_ref, table_ref, own_x_ref, other_x_ref, *refs):
    fields = [own_x_ref, other_x_ref]
    for ref in refs:
        if sum(field.shape[0] for field in fields) < table_ref.shape[1]:
            fields.append(ref)
    out_ref = refs[-1]
    sources = [(ref, k) for ref in fields for k in range(ref.shape[0])]
    for i in range(out_ref.shape[0]):
        acc = None
        for j, (ref, k) in enumerate(sources):
            term = table_ref[i, j] * ref[k]
            acc = term if acc is None else acc + term
        out_ref[i] = acc


def brick_of(zl, x, y, c):
    return ((zl * 4 + x) * 4 + y) * 2 + c


def places():
    for zl in range(2):
        for x in range(4):
            for y in range(4):
                for c in range(2):
                    yield brick_of(zl, x, y, c), zl, x, y, c


def crowded(zl, x, y):
    return (zl, x, y) in ((0, 0, 0), (1, 3, 3))


def swap_tables(half):
    direct, first, second = [], [], []
    detour = {0: (1, 3), 1: (2, 0)}
    for brick, zl, x, y, c in places():
        for vec in range(2):
            here, there = brick * 2 + vec, brick * 2 + 1 - vec
            if not crowded(zl, x, y):
                direct.append((here, there))
                continue
            relay = brick_of(zl, (x + detour[c][half]) % 4, y, c) * 2 + 1 - vec
            first.append((here, relay))
            second.append((relay, there))
    return direct, first, second


def sum_everywhere(value):
    def moved(place, dim, by):
        _, zl, x, y, c = place
        if dim == "x":
            x = (x + by) % 4
        elif dim == "y":
            y = (y + by) % 4
        else:
            c = c ^ by
        return brick_of(zl, x, y, c)

    def permute(v, dim, by):
        return lax.ppermute(v, "brick", [(place[0], moved(place, dim, by)) for place in places()])

    value = value + permute(value, "core", 1)
    pairs = {}
    for by in (1, 2, 3):
        table = []
        for brick, zl, x, y, c in places():
            for vec in range(2):
                z = (2 * vec + zl + by) % 4
                table.append((brick * 2 + vec, brick_of(z % 2, x, y, c) * 2 + z // 2))
        pairs[by] = table
    near = [lax.ppermute(value, ("brick", "vec"), pairs[by]) for by in (1, 2, 3)]
    value = (value + near[0]) + (near[1] + near[2])
    for dim in ("y", "x"):
        near = [permute(value, dim, by) for by in (1, 2, 3)]
        value = (value + near[0]) + (near[1] + near[2])
    return value


def steps_of(levels, start_block):
    own_cols, planes, rows, lanes = start_block.shape
    bricks = lax.axis_size("brick")
    brick = lax.axis_index("brick")
    vec = lax.axis_index("vec").astype(jnp.int32)
    voxel_total = bricks * planes * rows * lanes
    halves = planes // 2
    upward = [(i, i + 1) for i in range(bricks - 1)]
    downward = [(i + 1, i) for i in range(bricks - 1)]
    swap = [(0, 1), (1, 0)]

    def up(value):
        return lax.ppermute(value, "brick", upward)

    def down(value):
        return lax.ppermute(value, "brick", downward)

    vec_scalar = vec.reshape(1)
    tail = pl.pallas_call(
        tail_kernel,
        out_shape=jax.ShapeDtypeStruct((sum(offsets_cube), rows, lanes), f32),
        in_specs=[ANY],
        out_specs=VMEM,
        scratch_shapes=[
            pltpu.VMEM((sum(offsets_cube), rows, lanes), jnp.int32),
            pltpu.SemaphoreType.DMA((len(offsets_cube),)),
        ],
        compiler_params=params(4),
        name="tail",
    )(levels)
    halo = up(tail)
    x_own = start_block.astype(f32)
    x_above, x_below = [], []
    numbers = range(own_cols // chunk)
    for number in numbers:
        part = start_block[number * chunk : (number + 1) * chunk]
        x_above.append(down(part[:, :deepest].astype(f32)))
        x_below.append(up(part[:, planes - deepest :].astype(f32)))
    both = ("brick", "vec")
    x_relayed = []
    for half in range(2):
        direct, first_pairs, second_pairs = swap_tables(half)
        part = start_block[half * chunk : (half + 1) * chunk].astype(f32)
        part = lax.ppermute(part, both, first_pairs)
        x_relayed.append(lax.ppermute(part, both, second_pairs))
    x_other = lax.ppermute(x_own, both, direct)
    x_other = x_other + jnp.concatenate(x_relayed, axis=0)

    inside_above = (brick < bricks - 1).astype(jnp.int32).reshape(1)
    root = pl.pallas_call(
        degree_kernel,
        out_shape=jax.ShapeDtypeStruct((planes, rows, lanes), f32),
        in_specs=[SMEM, VMEM, VMEM],
        out_specs=VMEM,
        compiler_params=params(4),
        name="degree",
    )(inside_above, levels, halo)
    root_above = down(root[:deepest])
    root_below = up(root[planes - deepest :])

    terms = terms_of(rows, lanes)
    slots = len(terms)
    weights = pl.pallas_call(
        weights_kernel,
        out_shape=jax.ShapeDtypeStruct((slots, planes, rows, lanes), f32),
        in_specs=[VMEM] * 5,
        out_specs=VMEM,
        compiler_params=params(4),
        name="weights",
    )(levels, halo, root, root_above, root_below)
    ext = pltpu.VMEM((chunk, (planes + 2 * deepest) * rows, lanes), f32)

    def flat(value):
        return value.reshape(value.shape[0], -1, lanes)

    x_flat = flat(x_own)

    def first_filter(number):
        edge = jax.ShapeDtypeStruct((chunk, deepest, rows, lanes), f32)
        return pl.pallas_call(
            functools.partial(first_filter_kernel, number * chunk, terms, rows, lanes),
            out_shape=[jax.ShapeDtypeStruct((chunk, planes, rows, lanes), f32), edge, edge],
            in_specs=[VMEM] * 4,
            out_specs=[VMEM] * 3,
            scratch_shapes=[ext],
            compiler_params=params(10),
        )(weights, x_flat, flat(x_below[number]), flat(x_above[number]))

    def second_filter(field, below, above):
        return pl.pallas_call(
            functools.partial(second_filter_kernel, terms, rows, lanes),
            out_shape=[jax.ShapeDtypeStruct((chunk, halves, rows, lanes), f32)] * 2,
            in_specs=[SMEM] + [VMEM] * 4,
            out_specs=[VMEM] * 2,
            scratch_shapes=[ext],
            compiler_params=params(10),
        )(vec_scalar, weights, flat(field), flat(below), flat(above))

    fields, belows, aboves = [], [], []
    for number in numbers:
        field, low, high = first_filter(number)
        fields.append(field)
        aboves.append(down(low))
        belows.append(up(high))
    y_theirs, y_mine, y_other_mine = [], [], []
    for number in numbers:
        theirs, mine = second_filter(fields[number], belows[number], aboves[number])
        y_theirs.append(theirs)
        y_mine.append(mine)
        y_other_mine.append(lax.ppermute(theirs, "vec", swap))

    def tiled(value):
        return value.reshape(value.shape[0], -1, 8, lanes) if value.shape[2] != 8 else value

    def gram_call(early, *operands):
        out = jax.ShapeDtypeStruct((2 * own_cols, 128), f32)
        late = jax.ShapeDtypeStruct((own_cols, halves * rows // 8, 8, lanes), f32)
        return pl.pallas_call(
            functools.partial(gram_kernel, early),
            out_shape=(out, late) if early else out,
            in_specs=[SMEM] + [VMEM] * len(operands),
            out_specs=(VMEM, VMEM) if early else VMEM,
            scratch_shapes=[pltpu.VMEM((3, 256, 128), f32)],
            compiler_params=params(4),
            name="gram_early" if early else "gram_late",
        )(vec_scalar, *operands)

    mine_tiled = [tiled(value) for value in (x_own, x_other, *y_mine)]
    partial_gram, outgoing = gram_call(True, *mine_tiled)
    late = lax.ppermute(outgoing, "vec", [(0, 1)])
    gram = gram_call(False, *mine_tiled, *map(tiled, y_other_mine), partial_gram)
    gram = sum_everywhere(gram)

    small = jax.ShapeDtypeStruct((16, 16), f32)
    alpha, beta, table = pl.pallas_call(
        functools.partial(algebra_kernel, math.sqrt(voxel_total)),
        out_shape=[small, small, jax.ShapeDtypeStruct((own_cols, 4 * own_cols), f32)],
        in_specs=[SMEM, VMEM],
        out_specs=[VMEM] * 3,
        compiler_params=params(4),
        name="algebra",
    )(vec_scalar, gram)

    def combine(mine, *fields, before=None):
        parts = 4
        block_tiles = halves * rows // 8 // parts

        def whole(g, vec_ref):
            half = vec_ref[0] if mine else 1 - vec_ref[0]
            return (0, half * parts + g, 0, 0)

        extra = [] if before is None else [before]
        specs = [pl.BlockSpec((own_cols, block_tiles, 8, lanes), whole)] * 2
        for value in fields[2:]:
            specs.append(pl.BlockSpec((value.shape[0], block_tiles, 8, lanes), lambda g, vec_ref: (0, g, 0, 0)))
        return pl.pallas_call(
            combine_kernel,
            grid_spec=pltpu.PrefetchScalarGridSpec(
                num_scalar_prefetch=1,
                grid=(parts,),
                in_specs=[SMEM] + specs + [ANY] * len(extra),
                out_specs=pl.BlockSpec((own_cols, block_tiles, 8, lanes), whole),
            ),
            out_shape=jax.ShapeDtypeStruct((own_cols, planes * rows // 8, 8, lanes), f32),
            input_output_aliases={2 + len(fields): 0} if extra else {},
            compiler_params=params(10),
            name="combine",
        )(vec_scalar, table, *map(tiled, fields), *extra)

    basis = combine(True, x_own, x_other, *y_mine, *y_other_mine)
    basis = combine(False, x_own, x_other, *y_theirs, late, before=basis)
    return alpha[None], beta[None], basis.reshape(start_block.shape)


def solution(mesh):
    return jax.shard_map(
        steps_of,
        mesh=mesh,
        in_specs=(P(None, "brick", None, None), P("vec", "brick", None, None)),
        out_specs=(P(), P(), P("vec", "brick", None, None)),
        check_vma=False,
    )
```

profile of v0, /device:TPU:1, one launch (start us, length us, event | category | flops | bytes accessed | tf_op | source)
XLA Modules:
  0.0 185.7 jit_solution(12470441664234745952)
XLA Ops:
  0.6 0.0 copy-start.2
  0.6 1.9 %copy-done.2 = s32[12,32,16,128]{3,2,1,0:T(8,128)S(1)} copy-done((s32[12,32,16,128]{3,2,1,0:T(8,128)S(1)}, s32[12,32,16,128]{3,2,1,0:T(8,128)}, u32[]{:S(2)}) %copy-start.2) | copy-done | bytes 3145752
  2.5 1.2 tail.1
  3.7 0.0 copy-start.3
  3.8 4.8 %collective-permute-start.5 = (f32[40,16,128]{2,1,0:T(8,128)}, f32[40,16,128]{2,1,0:T(8,128)S(1)}, u32[]{:S(2)}, u32[]{:S(2)}) collective-permute-start(f32[40,16,128]{2,1,0:T(8,128)} %tail.1), channel_id=1, source_target_pairs={{0,2},{2,4},{4,6},{6,8},{8,10},{10,12},{12,14},{14,16},{16,18},{18... | collective-permute-start | bytes 983048 | tf_op jit(solution)/shard_map/ppermute | solution.py:406
  8.6 2.0 %slice_convert_fusion.2 = (f32[4,27,16,128]{3,2,1,0:T(8,128)}, f32[4,27,16,128]{3,2,1,0:T(8,128)}, f32[4,27,16,128]{3,2,1,0:T(8,128)}, f32[4,27,16,128]{3,2,1,0:T(8,128)}) fusion(s32[8,32,16,128]{3,2,1,0:T(8,128)S(1)} %copy-done.11), kind=kLoop, calls=%fused_computation.3 | loop fusion | flops 884736 | bytes 7077888 | tf_op jit(solution)/shard_map/convert_element_type | solution.py:430
  10.6 1.9 %collective-permute-start.12 = (f32[4,27,16,128]{3,2,1,0:T(8,128)}, f32[4,27,16,128]{3,2,1,0:T(8,128)}, u32[]{:S(2)}, u32[]{:S(2)}) collective-permute-start(f32[4,27,16,128]{3,2,1,0:T(8,128)} %get-tuple-element.36), channel_id=1, source_target_pairs={{0,2},{2,4},{4,6},{6,8},{8,10},{10,12},{12,14},{14,16},{16,18},{18... | collective-permute-start | bytes 2654216 | tf_op jit(solution)/shard_map/ppermute | solution.py:406
  12.5 3.3 %collective-permute-start.13 = (f32[4,27,16,128]{3,2,1,0:T(8,128)}, f32[4,27,16,128]{3,2,1,0:T(8,128)}, u32[]{:S(2)}, u32[]{:S(2)}) collective-permute-start(f32[4,27,16,128]{3,2,1,0:T(8,128)} %get-tuple-element.33), channel_id=1, source_target_pairs={{2,0},{4,2},{6,4},{8,6},{10,8},{12,10},{14,12},{16,14},{18,16},{20... | collective-permute-start | bytes 2654216 | tf_op jit(solution)/shard_map/ppermute | solution.py:409
  15.8 2.2 %collective-permute-start.8 = (f32[4,27,16,128]{3,2,1,0:T(8,128)}, f32[4,27,16,128]{3,2,1,0:T(8,128)}, u32[]{:S(2)}, u32[]{:S(2)}) collective-permute-start(f32[4,27,16,128]{3,2,1,0:T(8,128)} %get-tuple-element.35), channel_id=1, source_target_pairs={{0,2},{2,4},{4,6},{6,8},{8,10},{10,12},{12,14},{14,16},{16,18},{18... | collective-permute-start | bytes 2654216 | tf_op jit(solution)/shard_map/ppermute | solution.py:406
  18.1 3.0 %collective-permute-start.9 = (f32[4,27,16,128]{3,2,1,0:T(8,128)}, f32[4,27,16,128]{3,2,1,0:T(8,128)}, u32[]{:S(2)}, u32[]{:S(2)}) collective-permute-start(f32[4,27,16,128]{3,2,1,0:T(8,128)} %get-tuple-element.34), channel_id=1, source_target_pairs={{2,0},{4,2},{6,4},{8,6},{10,8},{12,10},{14,12},{16,14},{18,16},{20... | collective-permute-start | bytes 2654216 | tf_op jit(solution)/shard_map/ppermute | solution.py:409
  21.2 0.0 copy-start.12
  21.2 1.1 degree.1.root_ref
  22.3 1.9 %collective-permute-start.6 = (f32[27,16,128]{2,1,0:T(8,128)S(1)}, f32[27,16,128]{2,1,0:T(8,128)S(1)}, u32[]{:S(2)}, u32[]{:S(2)}) collective-permute-start(f32[27,16,128]{2,1,0:T(8,128)S(1)} %get-tuple-element.40), channel_id=1, source_target_pairs={{2,0},{4,2},{6,4},{8,6},{10,8},{12,10},{14,12},{16,14},{18,16},{20... | collective-permute-start | bytes 663560 | tf_op jit(solution)/shard_map/ppermute | solution.py:409
  24.3 0.2 convert_element_type.22
  24.4 14.5 %collective-permute-done.6.above_ref = f32[27,16,128]{2,1,0:T(8,128)S(1)} collective-permute-done((f32[27,16,128]{2,1,0:T(8,128)S(1)}, f32[27,16,128]{2,1,0:T(8,128)S(1)}, u32[]{:S(2)}, u32[]{:S(2)}) %collective-permute-start.6) | collective-permute-done | bytes 221216 | tf_op jit(solution)/shard_map/ppermute | solution.py:409
  38.9 2.2 %collective-permute-start.7 = (f32[27,16,128]{2,1,0:T(8,128)S(1)}, f32[27,16,128]{2,1,0:T(8,128)S(1)}, u32[]{:S(2)}, u32[]{:S(2)}) collective-permute-start(f32[27,16,128]{2,1,0:T(8,128)S(1)} %get-tuple-element.39), channel_id=1, source_target_pairs={{0,2},{2,4},{4,6},{6,8},{8,10},{10,12},{12,14},{14,16},{16,18},{18... | collective-permute-start | bytes 663560 | tf_op jit(solution)/shard_map/ppermute | solution.py:406
  41.1 0.2 slice_convert_fusion.1
  41.3 2.7 %collective-permute-done.7.below_ref = f32[27,16,128]{2,1,0:T(8,128)S(1)} collective-permute-done((f32[27,16,128]{2,1,0:T(8,128)S(1)}, f32[27,16,128]{2,1,0:T(8,128)S(1)}, u32[]{:S(2)}, u32[]{:S(2)}) %collective-permute-start.7) | collective-permute-done | bytes 221216 | tf_op jit(solution)/shard_map/ppermute | solution.py:406
  44.0 2.0 %collective-permute-start = (f32[8,32,16,128]{3,2,1,0:T(8,128)S(1)}, f32[8,32,16,128]{3,2,1,0:T(8,128)}, u32[]{:S(2)}, u32[]{:S(2)}) collective-permute-start(f32[8,32,16,128]{3,2,1,0:T(8,128)S(1)} %convert_element_type.22), channel_id=1, source_target_pairs={{4,5},{5,4},{6,7},{7,6},{8,9},{9,8},{10,11},{11,10},{12,13},{13,12... | collective-permute-start | bytes 6291464 | tf_op jit(solution)/shard_map/ppermute | solution.py:439
  46.0 8.9 %collective-permute-start.1 = (f32[4,32,16,128]{3,2,1,0:T(8,128)S(1)}, f32[4,32,16,128]{3,2,1,0:T(8,128)}, u32[]{:S(2)}, u32[]{:S(2)}) collective-permute-start(f32[4,32,16,128]{3,2,1,0:T(8,128)S(1)} %get-tuple-element.37), channel_id=1, source_target_pairs={{0,17},{1,16},{2,35},{3,34},{124,77},{125,76},{126,95},{127,94}} | collective-permute-start | bytes 3145736 | tf_op jit(solution)/shard_map/ppermute | solution.py:437
  54.8 4.9 %collective-permute-start.3 = (f32[4,32,16,128]{3,2,1,0:T(8,128)S(1)}, f32[4,32,16,128]{3,2,1,0:T(8,128)}, u32[]{:S(2)}, u32[]{:S(2)}) collective-permute-start(f32[4,32,16,128]{3,2,1,0:T(8,128)S(1)} %get-tuple-element.38), channel_id=1, source_target_pairs={{0,49},{1,48},{2,3},{3,2},{124,109},{125,108},{126,127},{127,126}} | collective-permute-start | bytes 3145736 | tf_op jit(solution)/shard_map/ppermute | solution.py:437
  59.7 3.0 %weights.1.weight_ref = f32[22,32,16,128]{3,2,1,0:T(8,128)S(1)} custom-call(s32[12,32,16,128]{3,2,1,0:T(8,128)S(1)} %copy-done.4, f32[40,16,128]{2,1,0:T(8,128)S(1)} %collective-permute-done.5.halo_ref, f32[32,16,128]{2,1,0:T(8,128)S(1)} %degree.1.root_ref, f32[27,16,128]{2,1,0:T(8,128)S(1)} %collective-permute-done.6.above_ref, ...), custom_call_target="tpu_custom_call" | custom-call | tf_op jit(solution)/shard_map/weights/pallas_call | solution.py:456
  62.7 5.8 %shard_map.51 = (f32[4,32,16,128]{3,2,1,0:T(8,128)S(1)}, f32[4,27,16,128]{3,2,1,0:T(8,128)S(1)}, f32[4,27,16,128]{3,2,1,0:T(8,128)S(1)}) custom-call(f32[22,32,16,128]{3,2,1,0:T(8,128)S(1)} %weights.1.weight_ref, f32[8,512,128]{2,1,0:T(8,128)S(1)} %bitcast.24, f32[4,432,128]{2,1,0:T(8,128)} %bitcast.11.below_ref, f32[4,432,128]{2,1,0:T(8,128)} %bitcast.12.above_ref), custom_call_target="tpu_custom_call" | custom-call | tf_op jit(solution)/shard_map/pallas_call | solution.py:473
  68.5 1.9 %collective-permute-start.14 = (f32[4,27,16,128]{3,2,1,0:T(8,128)S(1)}, f32[4,27,16,128]{3,2,1,0:T(8,128)S(1)}, u32[]{:S(2)}, u32[]{:S(2)}) collective-permute-start(f32[4,27,16,128]{3,2,1,0:T(8,128)S(1)} %get-tuple-element.23), channel_id=1, source_target_pairs={{0,2},{2,4},{4,6},{6,8},{8,10},{10,12},{12,14},{14,16},{16,18},{18... | collective-permute-start | bytes 2654216 | tf_op jit(solution)/shard_map/ppermute | solution.py:406
  70.4 3.7 %collective-permute-start.15 = (f32[4,27,16,128]{3,2,1,0:T(8,128)S(1)}, f32[4,27,16,128]{3,2,1,0:T(8,128)S(1)}, u32[]{:S(2)}, u32[]{:S(2)}) collective-permute-start(f32[4,27,16,128]{3,2,1,0:T(8,128)S(1)} %get-tuple-element.24), channel_id=1, source_target_pairs={{2,0},{4,2},{6,4},{8,6},{10,8},{12,10},{14,12},{16,14},{18,16},{20... | collective-permute-start | bytes 2654216 | tf_op jit(solution)/shard_map/ppermute | solution.py:409
  74.2 1.3 collective-permute-start.2
  75.5 9.5 %collective-permute-start.4 = (f32[4,32,16,128]{3,2,1,0:T(8,128)}, f32[4,32,16,128]{3,2,1,0:T(8,128)}, u32[]{:S(2)}, u32[]{:S(2)}) collective-permute-start(f32[4,32,16,128]{3,2,1,0:T(8,128)} %collective-permute-done.3), channel_id=1, source_target_pairs={{49,1},{48,0},{3,3},{2,2},{109,125},{108,124},{127,127},{126,126}} | collective-permute-start | bytes 3145736 | tf_op jit(solution)/shard_map/ppermute | solution.py:438
  84.9 5.7 %shard_map.49 = (f32[4,32,16,128]{3,2,1,0:T(8,128)S(1)}, f32[4,27,16,128]{3,2,1,0:T(8,128)}, f32[4,27,16,128]{3,2,1,0:T(8,128)}) custom-call(f32[22,32,16,128]{3,2,1,0:T(8,128)S(1)} %weights.1.weight_ref, f32[8,512,128]{2,1,0:T(8,128)S(1)} %bitcast.25, f32[4,432,128]{2,1,0:T(8,128)} %bitcast.5.below_ref, f32[4,432,128]{2,1,0:T(8,128)} %bitcast.6.above_ref), custom_call_target="tpu_custom_call" | custom-call | tf_op jit(solution)/shard_map/pallas_call | solution.py:473
  90.6 1.0 copy-done.5
  91.6 0.9 copy-done.7
  92.5 1.9 %collective-permute-start.10 = (f32[4,27,16,128]{3,2,1,0:T(8,128)}, f32[4,27,16,128]{3,2,1,0:T(8,128)}, u32[]{:S(2)}, u32[]{:S(2)}) collective-permute-start(f32[4,27,16,128]{3,2,1,0:T(8,128)} %get-tuple-element.19), channel_id=1, source_target_pairs={{0,2},{2,4},{4,6},{6,8},{8,10},{10,12},{12,14},{14,16},{16,18},{18... | collective-permute-start | bytes 2654216 | tf_op jit(solution)/shard_map/ppermute | solution.py:406
  94.4 0.9 copy-done.9
  95.4 3.4 %collective-permute-start.11 = (f32[4,27,16,128]{3,2,1,0:T(8,128)}, f32[4,27,16,128]{3,2,1,0:T(8,128)}, u32[]{:S(2)}, u32[]{:S(2)}) collective-permute-start(f32[4,27,16,128]{3,2,1,0:T(8,128)} %get-tuple-element.20), channel_id=1, source_target_pairs={{2,0},{4,2},{6,4},{8,6},{10,8},{12,10},{14,12},{16,14},{18,16},{20... | collective-permute-start | bytes 2654216 | tf_op jit(solution)/shard_map/ppermute | solution.py:409
  98.7 2.6 %copy-done.1 = f32[22,32,16,128]{3,2,1,0:T(8,128)S(1)} copy-done((f32[22,32,16,128]{3,2,1,0:T(8,128)S(1)}, f32[22,32,16,128]{3,2,1,0:T(8,128)}, u32[]{:S(2)}) %copy-start.1) | copy-done | bytes 5767192
  101.4 1.2 copy-done.8
  102.5 1.2 copy-done.10
  103.7 2.9 %shard_map.52 = (f32[4,16,16,128]{3,2,1,0:T(8,128)S(1)}, f32[4,16,16,128]{3,2,1,0:T(8,128)S(1)}) custom-call(s32[1]{0:T(128)} %bitcast.vec_ref, f32[22,32,16,128]{3,2,1,0:T(8,128)S(1)} %copy-done.1, f32[4,512,128]{2,1,0:T(8,128)S(1)} %bitcast.44, f32[4,432,128]{2,1,0:T(8,128)S(1)} %bitcast.46, f32[4,432,128]{2,1,0:T(8,128)S(1)} %bitcast.47), custom_call_target="tpu_custom_call" | custom-call | tf_op jit(solution)/shard_map/pallas_call | solution.py:483
  106.6 3.3 %collective-permute-start.17 = (f32[4,16,16,128]{3,2,1,0:T(8,128)S(1)}, f32[4,16,16,128]{3,2,1,0:T(8,128)S(1)}, u32[]{:S(2)}, u32[]{:S(2)}) collective-permute-start(f32[4,16,16,128]{3,2,1,0:T(8,128)S(1)} %get-tuple-element.27), channel_id=1, source_target_pairs={{0,1},{1,0},{2,3},{3,2},{4,5},{5,4},{6,7},{7,6},{8,9},{9,8},{10,11... | collective-permute-start | bytes 1572872 | tf_op jit(solution)/shard_map/ppermute | solution.py:503
  109.9 0.1 collective-permute-done.11
  110.0 4.3 %shard_map.50 = (f32[4,16,16,128]{3,2,1,0:T(8,128)S(1)}, f32[4,16,16,128]{3,2,1,0:T(8,128)S(1)}) custom-call(s32[1]{0:T(128)} %bitcast.vec_ref, f32[22,32,16,128]{3,2,1,0:T(8,128)S(1)} %copy-done.1, f32[4,512,128]{2,1,0:T(8,128)S(1)} %bitcast.45, f32[4,432,128]{2,1,0:T(8,128)} %bitcast.8.below_ref, f32[4,432,128]{2,1,0:T(8,128)} %bitcast.9.above_ref), custom_call_target="tpu_custom_call" | custom-call | tf_op jit(solution)/shard_map/pallas_call | solution.py:483
  114.4 3.3 %collective-permute-start.16 = (f32[4,16,16,128]{3,2,1,0:T(8,128)S(1)}, f32[4,16,16,128]{3,2,1,0:T(8,128)S(1)}, u32[]{:S(2)}, u32[]{:S(2)}) collective-permute-start(f32[4,16,16,128]{3,2,1,0:T(8,128)S(1)} %get-tuple-element.26), channel_id=1, source_target_pairs={{0,1},{1,0},{2,3},{3,2},{4,5},{5,4},{6,7},{7,6},{8,9},{9,8},{10,11... | collective-permute-start | bytes 1572872 | tf_op jit(solution)/shard_map/ppermute | solution.py:503
  117.7 2.4 %maximum_add_fusion = f32[8,32,16,128]{3,2,1,0:T(8,128)S(1)} fusion(f32[8,32,16,128]{3,2,1,0:T(8,128)} %collective-permute-done, f32[4,32,16,128]{3,2,1,0:T(8,128)} %collective-permute-done.4, f32[4,32,16,128]{3,2,1,0:T(8,128)} %collective-permute-done.2), kind=kLoop, calls=%fused_computation | loop fusion | flops 1048576 | bytes 6291456 | tf_op jit(solution)/shard_map/add | solution.py:440
  120.2 4.3 %gram_early.1 = (f32[16,128]{1,0:T(8,128)S(1)}, f32[8,32,8,128]{3,2,1,0:T(8,128)S(1)}) custom-call(s32[1]{0:T(128)} %bitcast.vec_ref, f32[8,64,8,128]{3,2,1,0:T(8,128)S(1)} %bitcast.26, f32[8,64,8,128]{3,2,1,0:T(8,128)S(1)} %bitcast.30, f32[4,32,8,128]{3,2,1,0:T(8,128)S(1)} %bitcast.37, f32[4,32,8,128]{3,2,1,0:T(8,128)S(1)} %bitcast.34), custom_call_target="tpu_custom_call" | custom-call | tf_op jit(solution)/shard_map/gram_early/pallas_call | solution.py:511
  124.5 1.4 collective-permute-start.28
  125.9 7.8 %collective-permute-done.16 = f32[4,16,16,128]{3,2,1,0:T(8,128)S(1)} collective-permute-done((f32[4,16,16,128]{3,2,1,0:T(8,128)S(1)}, f32[4,16,16,128]{3,2,1,0:T(8,128)S(1)}, u32[]{:S(2)}, u32[]{:S(2)}) %collective-permute-start.16) | collective-permute-done | bytes 524320 | tf_op jit(solution)/shard_map/ppermute | solution.py:503
  133.6 2.2 %gram_late.1 = f32[16,128]{1,0:T(8,128)S(1)} custom-call(s32[1]{0:T(128)} %bitcast.vec_ref, f32[8,64,8,128]{3,2,1,0:T(8,128)S(1)} %bitcast.27, f32[8,64,8,128]{3,2,1,0:T(8,128)S(1)} %bitcast.31, f32[4,32,8,128]{3,2,1,0:T(8,128)S(1)} %bitcast.38, f32[4,32,8,128]{3,2,1,0:T(8,128)S(1)} %bitcast.35, f32[4,32,8,128]{3,2,1,0:T(8,128)S(1)} %bitcast.42, ...), custom_call_target="tpu_custom_call" | custom-call | tf_op jit(solution)/shard_map/gram_late/pallas_call | solution.py:511
  135.8 0.5 collective-permute-start.18
  136.3 0.8 collective-permute-done.18
  137.1 1.9 %collective-permute-start.19 = (f32[16,128]{1,0:T(8,128)S(1)}, f32[16,128]{1,0:T(8,128)S(1)}, u32[]{:S(2)}, u32[]{:S(2)}) collective-permute-start(f32[16,128]{1,0:T(8,128)S(1)} %add.34), channel_id=1, source_target_pairs={{0,64},{1,65},{2,66},{3,67},{4,68},{5,69},{6,70},{7,71},{8,72},{9,... | collective-permute-start | bytes 24584 | tf_op jit(solution)/shard_map/ppermute | solution.py:386
  139.1 5.2 %collective-permute-start.20 = (f32[16,128]{1,0:T(8,128)S(1)}, f32[16,128]{1,0:T(8,128)S(1)}, u32[]{:S(2)}, u32[]{:S(2)}) collective-permute-start(f32[16,128]{1,0:T(8,128)S(1)} %add.34), channel_id=1, source_target_pairs={{0,1},{1,0},{2,3},{3,2},{4,5},{5,4},{6,7},{7,6},{8,9},{9,8},{10,11... | collective-permute-start | bytes 24584 | tf_op jit(solution)/shard_map/ppermute | solution.py:386
  144.3 11.3 %collective-permute-done.19 = f32[16,128]{1,0:T(8,128)S(1)} collective-permute-done((f32[16,128]{1,0:T(8,128)S(1)}, f32[16,128]{1,0:T(8,128)S(1)}, u32[]{:S(2)}, u32[]{:S(2)}) %collective-permute-start.19) | collective-permute-done | bytes 8224 | tf_op jit(solution)/shard_map/ppermute | solution.py:386
  155.6 0.1 collective-permute-done.20
  155.7 0.1 collective-permute-start.22
  155.8 2.7 %collective-permute-start.23 = (f32[16,128]{1,0:T(8,128)S(1)}, f32[16,128]{1,0:T(8,128)S(1)}, u32[]{:S(2)}, u32[]{:S(2)}) collective-permute-start(f32[16,128]{1,0:T(8,128)S(1)} %add_add_fusion.2), channel_id=1, source_target_pairs={{0,8},{2,10},{4,12},{6,14},{8,0},{10,2},{12,4},{14,6},{16,24},{18,... | collective-permute-start | bytes 24584 | tf_op jit(solution)/shard_map/ppermute | solution.py:375
  158.5 1.0 collective-permute-done.22
  159.5 0.4 collective-permute-done.23
  159.8 1.2 collective-permute-done.24
  161.0 1.2 collective-permute-start.25
  162.2 8.0 %collective-permute-start.26 = (f32[16,128]{1,0:T(8,128)S(1)}, f32[16,128]{1,0:T(8,128)S(1)}, u32[]{:S(2)}, u32[]{:S(2)}) collective-permute-start(f32[16,128]{1,0:T(8,128)S(1)} %add_add_fusion.1), channel_id=1, source_target_pairs={{0,32},{2,34},{4,36},{6,38},{8,40},{10,42},{12,44},{14,46},{16,48}... | collective-permute-start | bytes 24584 | tf_op jit(solution)/shard_map/ppermute | solution.py:375
  170.2 1.1 collective-permute-done.26
  171.3 1.4 collective-permute-done.27
  172.7 4.8 %algebra.1 = (f32[16,16]{1,0:T(8,128)}, f32[16,16]{1,0:T(8,128)}, f32[8,32]{1,0:T(8,128)S(1)}) custom-call(s32[1]{0:T(128)} %bitcast.vec_ref, f32[16,128]{1,0:T(8,128)S(1)} %add_add_fusion.gram_ref), custom_call_target="tpu_custom_call" | custom-call | tf_op jit(solution)/shard_map/algebra/pallas_call | solution.py:528
  177.5 4.1 %combine.2.refs_3_ = f32[8,64,8,128]{3,2,1,0:T(8,128)} custom-call(s32[1]{0:T(128)} %bitcast.vec_ref, f32[8,32]{1,0:T(8,128)S(1)} %get-tuple-element.31.table_ref, f32[8,64,8,128]{3,2,1,0:T(8,128)S(1)} %bitcast.28, f32[8,64,8,128]{3,2,1,0:T(8,128)S(1)} %bitcast.32, f32[4,32,8,128]{3,2,1,0:T(8,128)S(1)} %bitcast.39, f32[4,32,8,128]{3,2,1,0:T(8,128)S(1)} %bitcast.36, ...), custom_call_target="tpu_custom_call" | custom-call | tf_op jit(solution)/shard_map/combine/pallas_call | solution.py:549
  181.6 4.1 %combine.3 = f32[8,64,8,128]{3,2,1,0:T(8,128)} custom-call(s32[1]{0:T(128)} %bitcast.vec_ref, f32[8,32]{1,0:T(8,128)S(1)} %get-tuple-element.31.table_ref, f32[8,64,8,128]{3,2,1,0:T(8,128)S(1)} %bitcast.29, f32[8,64,8,128]{3,2,1,0:T(8,128)S(1)} %bitcast.33, f32[4,32,8,128]{3,2,1,0:T(8,128)S(1)} %bitcast.49, ...), custom_call_target="tpu_custom_call", output_to_operand_aliasing={{}: (7, {})} | custom-call | tf_op jit(solution)/shard_map/combine/pallas_call | solution.py:549
  (41 shorter events, 0.1 us)
Async XLA Ops:
  0.6 1.9 %copy-start.2 = (s32[12,32,16,128]{3,2,1,0:T(8,128)S(1)}, s32[12,32,16,128]{3,2,1,0:T(8,128)}, u32[]{:S(2)}) copy-start(s32[12,32,16,128]{3,2,1,0:T(8,128)} %levels_ref.5) | copy-start | bytes 9437188
  2.5 6.1 %copy-start.11 = (s32[8,32,16,128]{3,2,1,0:T(8,128)S(1)}, s32[8,32,16,128]{3,2,1,0:T(8,128)}, u32[]{:S(2)}) copy-start(s32[8,32,16,128]{3,2,1,0:T(8,128)} %param.3) | copy-start | bytes 6291460
  3.7 17.4 %copy-start.3 = (s32[12,32,16,128]{3,2,1,0:T(8,128)S(1)}, s32[12,32,16,128]{3,2,1,0:T(8,128)}, u32[]{:S(2)}) copy-start(s32[12,32,16,128]{3,2,1,0:T(8,128)} %levels_ref.5) | copy-start | bytes 9437188
  3.8 17.4 %collective-permute-start.5 = (f32[40,16,128]{2,1,0:T(8,128)}, f32[40,16,128]{2,1,0:T(8,128)S(1)}, u32[]{:S(2)}, u32[]{:S(2)}) collective-permute-start(f32[40,16,128]{2,1,0:T(8,128)} %tail.1), channel_id=1, source_target_pairs={{0,2},{2,4},{4,6},{6,8},{8,10},{10,12},{12,14},{14,16},{16,18},{18... | collective-permute-start | bytes 983048 | tf_op jit(solution)/shard_map/ppermute | solution.py:406
  10.6 35.4 %collective-permute-start.12 = (f32[4,27,16,128]{3,2,1,0:T(8,128)}, f32[4,27,16,128]{3,2,1,0:T(8,128)}, u32[]{:S(2)}, u32[]{:S(2)}) collective-permute-start(f32[4,27,16,128]{3,2,1,0:T(8,128)} %get-tuple-element.36), channel_id=1, source_target_pairs={{0,2},{2,4},{4,6},{6,8},{8,10},{10,12},{12,14},{14,16},{16,18},{18... | collective-permute-start | bytes 2654216 | tf_op jit(solution)/shard_map/ppermute | solution.py:406
  12.5 42.4 %collective-permute-start.13 = (f32[4,27,16,128]{3,2,1,0:T(8,128)}, f32[4,27,16,128]{3,2,1,0:T(8,128)}, u32[]{:S(2)}, u32[]{:S(2)}) collective-permute-start(f32[4,27,16,128]{3,2,1,0:T(8,128)} %get-tuple-element.33), channel_id=1, source_target_pairs={{2,0},{4,2},{6,4},{8,6},{10,8},{12,10},{14,12},{16,14},{18,16},{20... | collective-permute-start | bytes 2654216 | tf_op jit(solution)/shard_map/ppermute | solution.py:409
  15.8 52.7 %collective-permute-start.8 = (f32[4,27,16,128]{3,2,1,0:T(8,128)}, f32[4,27,16,128]{3,2,1,0:T(8,128)}, u32[]{:S(2)}, u32[]{:S(2)}) collective-permute-start(f32[4,27,16,128]{3,2,1,0:T(8,128)} %get-tuple-element.35), channel_id=1, source_target_pairs={{0,2},{2,4},{4,6},{6,8},{8,10},{10,12},{12,14},{14,16},{16,18},{18... | collective-permute-start | bytes 2654216 | tf_op jit(solution)/shard_map/ppermute | solution.py:406
  18.1 52.4 %collective-permute-start.9 = (f32[4,27,16,128]{3,2,1,0:T(8,128)}, f32[4,27,16,128]{3,2,1,0:T(8,128)}, u32[]{:S(2)}, u32[]{:S(2)}) collective-permute-start(f32[4,27,16,128]{3,2,1,0:T(8,128)} %get-tuple-element.34), channel_id=1, source_target_pairs={{2,0},{4,2},{6,4},{8,6},{10,8},{12,10},{14,12},{16,14},{18,16},{20... | collective-permute-start | bytes 2654216 | tf_op jit(solution)/shard_map/ppermute | solution.py:409
  21.2 3.1 %copy-start.12 = (s32[8,32,16,128]{3,2,1,0:T(8,128)S(1)}, s32[8,32,16,128]{3,2,1,0:T(8,128)}, u32[]{:S(2)}) copy-start(s32[8,32,16,128]{3,2,1,0:T(8,128)} %param.3) | copy-start | bytes 6291460
  22.3 16.6 %collective-permute-start.6 = (f32[27,16,128]{2,1,0:T(8,128)S(1)}, f32[27,16,128]{2,1,0:T(8,128)S(1)}, u32[]{:S(2)}, u32[]{:S(2)}) collective-permute-start(f32[27,16,128]{2,1,0:T(8,128)S(1)} %get-tuple-element.40), channel_id=1, source_target_pairs={{2,0},{4,2},{6,4},{8,6},{10,8},{12,10},{14,12},{16,14},{18,16},{20... | collective-permute-start | bytes 663560 | tf_op jit(solution)/shard_map/ppermute | solution.py:409
  38.9 20.8 %copy-start.4 = (s32[12,32,16,128]{3,2,1,0:T(8,128)S(1)}, s32[12,32,16,128]{3,2,1,0:T(8,128)}, u32[]{:S(2)}) copy-start(s32[12,32,16,128]{3,2,1,0:T(8,128)} %levels_ref.5) | copy-start | bytes 9437188
  38.9 5.0 %collective-permute-start.7 = (f32[27,16,128]{2,1,0:T(8,128)S(1)}, f32[27,16,128]{2,1,0:T(8,128)S(1)}, u32[]{:S(2)}, u32[]{:S(2)}) collective-permute-start(f32[27,16,128]{2,1,0:T(8,128)S(1)} %get-tuple-element.39), channel_id=1, source_target_pairs={{0,2},{2,4},{4,6},{6,8},{8,10},{10,12},{12,14},{14,16},{16,18},{18... | collective-permute-start | bytes 663560 | tf_op jit(solution)/shard_map/ppermute | solution.py:406
  44.0 73.7 %collective-permute-start = (f32[8,32,16,128]{3,2,1,0:T(8,128)S(1)}, f32[8,32,16,128]{3,2,1,0:T(8,128)}, u32[]{:S(2)}, u32[]{:S(2)}) collective-permute-start(f32[8,32,16,128]{3,2,1,0:T(8,128)S(1)} %convert_element_type.22), channel_id=1, source_target_pairs={{4,5},{5,4},{6,7},{7,6},{8,9},{9,8},{10,11},{11,10},{12,13},{13,12... | collective-permute-start | bytes 6291464 | tf_op jit(solution)/shard_map/ppermute | solution.py:439
  46.0 28.2 %collective-permute-start.1 = (f32[4,32,16,128]{3,2,1,0:T(8,128)S(1)}, f32[4,32,16,128]{3,2,1,0:T(8,128)}, u32[]{:S(2)}, u32[]{:S(2)}) collective-permute-start(f32[4,32,16,128]{3,2,1,0:T(8,128)S(1)} %get-tuple-element.37), channel_id=1, source_target_pairs={{0,17},{1,16},{2,35},{3,34},{124,77},{125,76},{126,95},{127,94}} | collective-permute-start | bytes 3145736 | tf_op jit(solution)/shard_map/ppermute | solution.py:437
  54.8 20.6 %collective-permute-start.3 = (f32[4,32,16,128]{3,2,1,0:T(8,128)S(1)}, f32[4,32,16,128]{3,2,1,0:T(8,128)}, u32[]{:S(2)}, u32[]{:S(2)}) collective-permute-start(f32[4,32,16,128]{3,2,1,0:T(8,128)S(1)} %get-tuple-element.38), channel_id=1, source_target_pairs={{0,49},{1,48},{2,3},{3,2},{124,109},{125,108},{126,127},{127,126}} | collective-permute-start | bytes 3145736 | tf_op jit(solution)/shard_map/ppermute | solution.py:437
  62.7 22.2 %copy-start = (f32[22,32,16,128]{3,2,1,0:T(8,128)}, f32[22,32,16,128]{3,2,1,0:T(8,128)S(1)}, u32[]{:S(2)}) copy-start(f32[22,32,16,128]{3,2,1,0:T(8,128)S(1)} %weights.1.weight_ref) | copy-start | bytes 17301508
  68.5 23.1 %collective-permute-start.14 = (f32[4,27,16,128]{3,2,1,0:T(8,128)S(1)}, f32[4,27,16,128]{3,2,1,0:T(8,128)S(1)}, u32[]{:S(2)}, u32[]{:S(2)}) collective-permute-start(f32[4,27,16,128]{3,2,1,0:T(8,128)S(1)} %get-tuple-element.23), channel_id=1, source_target_pairs={{0,2},{2,4},{4,6},{6,8},{8,10},{10,12},{12,14},{14,16},{16,18},{18... | collective-permute-start | bytes 2654216 | tf_op jit(solution)/shard_map/ppermute | solution.py:406
  70.4 24.0 %collective-permute-start.15 = (f32[4,27,16,128]{3,2,1,0:T(8,128)S(1)}, f32[4,27,16,128]{3,2,1,0:T(8,128)S(1)}, u32[]{:S(2)}, u32[]{:S(2)}) collective-permute-start(f32[4,27,16,128]{3,2,1,0:T(8,128)S(1)} %get-tuple-element.24), channel_id=1, source_target_pairs={{2,0},{4,2},{6,4},{8,6},{10,8},{12,10},{14,12},{16,14},{18,16},{20... | collective-permute-start | bytes 2654216 | tf_op jit(solution)/shard_map/ppermute | solution.py:409
  74.2 43.5 %collective-permute-start.2 = (f32[4,32,16,128]{3,2,1,0:T(8,128)}, f32[4,32,16,128]{3,2,1,0:T(8,128)}, u32[]{:S(2)}, u32[]{:S(2)}) collective-permute-start(f32[4,32,16,128]{3,2,1,0:T(8,128)} %collective-permute-done.1), channel_id=1, source_target_pairs={{17,1},{16,0},{35,3},{34,2},{77,125},{76,124},{95,127},{94,126}} | collective-permute-start | bytes 3145736 | tf_op jit(solution)/shard_map/ppermute | solution.py:438
  75.5 42.2 %collective-permute-start.4 = (f32[4,32,16,128]{3,2,1,0:T(8,128)}, f32[4,32,16,128]{3,2,1,0:T(8,128)}, u32[]{:S(2)}, u32[]{:S(2)}) collective-permute-start(f32[4,32,16,128]{3,2,1,0:T(8,128)} %collective-permute-done.3), channel_id=1, source_target_pairs={{49,1},{48,0},{3,3},{2,2},{109,125},{108,124},{127,127},{126,126}} | collective-permute-start | bytes 3145736 | tf_op jit(solution)/shard_map/ppermute | solution.py:438
  90.6 1.0 copy-start.5
  91.6 0.9 copy-start.7
  92.5 14.1 %collective-permute-start.10 = (f32[4,27,16,128]{3,2,1,0:T(8,128)}, f32[4,27,16,128]{3,2,1,0:T(8,128)}, u32[]{:S(2)}, u32[]{:S(2)}) collective-permute-start(f32[4,27,16,128]{3,2,1,0:T(8,128)} %get-tuple-element.19), channel_id=1, source_target_pairs={{0,2},{2,4},{4,6},{6,8},{8,10},{10,12},{12,14},{14,16},{16,18},{18... | collective-permute-start | bytes 2654216 | tf_op jit(solution)/shard_map/ppermute | solution.py:406
  94.4 0.9 copy-start.9
  95.4 14.7 %collective-permute-start.11 = (f32[4,27,16,128]{3,2,1,0:T(8,128)}, f32[4,27,16,128]{3,2,1,0:T(8,128)}, u32[]{:S(2)}, u32[]{:S(2)}) collective-permute-start(f32[4,27,16,128]{3,2,1,0:T(8,128)} %get-tuple-element.20), channel_id=1, source_target_pairs={{2,0},{4,2},{6,4},{8,6},{10,8},{12,10},{14,12},{16,14},{18,16},{20... | collective-permute-start | bytes 2654216 | tf_op jit(solution)/shard_map/ppermute | solution.py:409
  98.7 2.6 %copy-start.1 = (f32[22,32,16,128]{3,2,1,0:T(8,128)S(1)}, f32[22,32,16,128]{3,2,1,0:T(8,128)}, u32[]{:S(2)}) copy-start(f32[22,32,16,128]{3,2,1,0:T(8,128)} %copy-done) | copy-start | bytes 17301508
  101.4 1.2 copy-start.8
  102.5 1.2 copy-start.10
  103.7 6.3 %copy-start.6 = (f32[4,32,16,128]{3,2,1,0:T(8,128)S(1)}, f32[4,32,16,128]{3,2,1,0:T(8,128)}, u32[]{:S(2)}) copy-start(f32[4,32,16,128]{3,2,1,0:T(8,128)} %copy-done.5) | copy-start | bytes 3145732
  106.6 19.2 %collective-permute-start.17 = (f32[4,16,16,128]{3,2,1,0:T(8,128)S(1)}, f32[4,16,16,128]{3,2,1,0:T(8,128)S(1)}, u32[]{:S(2)}, u32[]{:S(2)}) collective-permute-start(f32[4,16,16,128]{3,2,1,0:T(8,128)S(1)} %get-tuple-element.27), channel_id=1, source_target_pairs={{0,1},{1,0},{2,3},{3,2},{4,5},{5,4},{6,7},{7,6},{8,9},{9,8},{10,11... | collective-permute-start | bytes 1572872 | tf_op jit(solution)/shard_map/ppermute | solution.py:503
  114.4 19.2 %collective-permute-start.16 = (f32[4,16,16,128]{3,2,1,0:T(8,128)S(1)}, f32[4,16,16,128]{3,2,1,0:T(8,128)S(1)}, u32[]{:S(2)}, u32[]{:S(2)}) collective-permute-start(f32[4,16,16,128]{3,2,1,0:T(8,128)S(1)} %get-tuple-element.26), channel_id=1, source_target_pairs={{0,1},{1,0},{2,3},{3,2},{4,5},{5,4},{6,7},{7,6},{8,9},{9,8},{10,11... | collective-permute-start | bytes 1572872 | tf_op jit(solution)/shard_map/ppermute | solution.py:503
  124.5 57.1 %collective-permute-start.28 = (f32[8,32,8,128]{3,2,1,0:T(8,128)S(1)}, f32[8,32,8,128]{3,2,1,0:T(8,128)S(1)}, u32[]{:S(2)}, u32[]{:S(2)}) collective-permute-start(f32[8,32,8,128]{3,2,1,0:T(8,128)S(1)} %get-tuple-element.32), channel_id=1, source_target_pairs={{0,1},{2,3},{4,5},{6,7},{8,9},{10,11},{12,13},{14,15},{16,17},{18,... | collective-permute-start | bytes 3145736 | tf_op jit(solution)/shard_map/ppermute | solution.py:523
  135.8 1.3 collective-permute-start.18
  137.1 18.5 %collective-permute-start.19 = (f32[16,128]{1,0:T(8,128)S(1)}, f32[16,128]{1,0:T(8,128)S(1)}, u32[]{:S(2)}, u32[]{:S(2)}) collective-permute-start(f32[16,128]{1,0:T(8,128)S(1)} %add.34), channel_id=1, source_target_pairs={{0,64},{1,65},{2,66},{3,67},{4,68},{5,69},{6,70},{7,71},{8,72},{9,... | collective-permute-start | bytes 24584 | tf_op jit(solution)/shard_map/ppermute | solution.py:386
  139.1 16.6 %collective-permute-start.20 = (f32[16,128]{1,0:T(8,128)S(1)}, f32[16,128]{1,0:T(8,128)S(1)}, u32[]{:S(2)}, u32[]{:S(2)}) collective-permute-start(f32[16,128]{1,0:T(8,128)S(1)} %add.34), channel_id=1, source_target_pairs={{0,1},{1,0},{2,3},{3,2},{4,5},{5,4},{6,7},{7,6},{8,9},{9,8},{10,11... | collective-permute-start | bytes 24584 | tf_op jit(solution)/shard_map/ppermute | solution.py:386
  144.3 11.4 %collective-permute-start.21 = (f32[16,128]{1,0:T(8,128)S(1)}, f32[16,128]{1,0:T(8,128)S(1)}, u32[]{:S(2)}, u32[]{:S(2)}) collective-permute-start(f32[16,128]{1,0:T(8,128)S(1)} %add.34), channel_id=1, source_target_pairs={{0,65},{1,64},{2,67},{3,66},{4,69},{5,68},{6,71},{7,70},{8,73},{9,... | collective-permute-start | bytes 24584 | tf_op jit(solution)/shard_map/ppermute | solution.py:386
  155.7 3.8 %collective-permute-start.22 = (f32[16,128]{1,0:T(8,128)S(1)}, f32[16,128]{1,0:T(8,128)S(1)}, u32[]{:S(2)}, u32[]{:S(2)}) collective-permute-start(f32[16,128]{1,0:T(8,128)S(1)} %add_add_fusion.2), channel_id=1, source_target_pairs={{0,4},{2,6},{4,8},{6,10},{8,12},{10,14},{12,0},{14,2},{16,20},{18,... | collective-permute-start | bytes 24584 | tf_op jit(solution)/shard_map/ppermute | solution.py:375
  155.8 4.1 %collective-permute-start.23 = (f32[16,128]{1,0:T(8,128)S(1)}, f32[16,128]{1,0:T(8,128)S(1)}, u32[]{:S(2)}, u32[]{:S(2)}) collective-permute-start(f32[16,128]{1,0:T(8,128)S(1)} %add_add_fusion.2), channel_id=1, source_target_pairs={{0,8},{2,10},{4,12},{6,14},{8,0},{10,2},{12,4},{14,6},{16,24},{18,... | collective-permute-start | bytes 24584 | tf_op jit(solution)/shard_map/ppermute | solution.py:375
  158.5 2.6 %collective-permute-start.24 = (f32[16,128]{1,0:T(8,128)S(1)}, f32[16,128]{1,0:T(8,128)S(1)}, u32[]{:S(2)}, u32[]{:S(2)}) collective-permute-start(f32[16,128]{1,0:T(8,128)S(1)} %add_add_fusion.2), channel_id=1, source_target_pairs={{0,12},{2,14},{4,0},{6,2},{8,4},{10,6},{12,8},{14,10},{16,28},{18,... | collective-permute-start | bytes 24584 | tf_op jit(solution)/shard_map/ppermute | solution.py:375
  161.0 9.1 %collective-permute-start.25 = (f32[16,128]{1,0:T(8,128)S(1)}, f32[16,128]{1,0:T(8,128)S(1)}, u32[]{:S(2)}, u32[]{:S(2)}) collective-permute-start(f32[16,128]{1,0:T(8,128)S(1)} %add_add_fusion.1), channel_id=1, source_target_pairs={{0,16},{2,18},{4,20},{6,22},{8,24},{10,26},{12,28},{14,30},{16,32}... | collective-permute-start | bytes 24584 | tf_op jit(solution)/shard_map/ppermute | solution.py:375
  162.2 9.1 %collective-permute-start.26 = (f32[16,128]{1,0:T(8,128)S(1)}, f32[16,128]{1,0:T(8,128)S(1)}, u32[]{:S(2)}, u32[]{:S(2)}) collective-permute-start(f32[16,128]{1,0:T(8,128)S(1)} %add_add_fusion.1), channel_id=1, source_target_pairs={{0,32},{2,34},{4,36},{6,38},{8,40},{10,42},{12,44},{14,46},{16,48}... | collective-permute-start | bytes 24584 | tf_op jit(solution)/shard_map/ppermute | solution.py:375
  170.2 2.5 %collective-permute-start.27 = (f32[16,128]{1,0:T(8,128)S(1)}, f32[16,128]{1,0:T(8,128)S(1)}, u32[]{:S(2)}, u32[]{:S(2)}) collective-permute-start(f32[16,128]{1,0:T(8,128)S(1)} %add_add_fusion.1), channel_id=1, source_target_pairs={{0,48},{2,50},{4,52},{6,54},{8,56},{10,58},{12,60},{14,62},{16,0},... | collective-permute-start | bytes 24584 | tf_op jit(solution)/shard_map/ppermute | solution.py:375
where the time goes:
time: 189 us; the launch traced here: 186 us
  starting transfers between devices  84.3 us (45%)
  Pallas kernels  43.5 us (23%)
  waiting for transfers between devices  42.4 us (22%)
  local copies, waits for them, and re-layouts  9.73 us (5%)
  other arithmetic  4.72 us (2%)
    ppermute x5, starting transfers between devices, down(): return lax.ppermute(value, 'brick', downward)  15.3 us
    ppermute x6, starting transfers between devices, up(): return lax.ppermute(value, 'brick', upward)  15 us
    ppermute x5, waiting for transfers between devices, down(): return lax.ppermute(value, 'brick', downward)  14.6 us
    ppermute x2, starting transfers between devices, steps_of(): part = lax.ppermute(part, both, first_pairs)  13.7 us
    ppermute x7, starting transfers between devices, permute(): lax.ppermute(v, 'brick', [(place[0], moved(place, dim, by)) for place in...  12.4 us
    ppermute x3, waiting for transfers between devices, sum_everywhere(): lax.ppermute(value, ('brick', 'vec'), pairs[by])  11.4 us
    pallas_call x2, Pallas kernels, first_filter(): pl.pallas_call(functools.partial(first_filter_kernel, number * chunk, ter...  11.4 us
    ppermute x2, starting transfers between devices, steps_of(): x_relayed.append(lax.ppermute(part, both, second_pairs))  10.8 us
  transfers between devices with their start and end apart: 29, of which 12 were waited for; matrix products, arithmetic and copies ran while one was open for 3% of the time, Pallas kernels for 21%

commit v1 on v0

--- a/solution.py
+++ b/solution.py
@@ -19,6 +19,7 @@
 ANY = pl.BlockSpec(memory_space=pl.ANY)
 SMEM = pl.BlockSpec(memory_space=pltpu.SMEM)
 VMEM = pl.BlockSpec(memory_space=pltpu.VMEM)
+HBM = pl.BlockSpec(memory_space=pltpu.HBM)
 
 
 def params(mib):
@@ -73,9 +74,9 @@
     out_ref[...] = to_weight(raw_ref[...])
 
 
-def degree_kernel(flag_ref, levels_ref, halo_ref, root_ref):
+def degree_kernel(levels_ref, halo_ref, start_ref, root_ref, *edge_refs):
     planes = levels_ref.shape[1]
-    inside_above = flag_ref[0].astype(f32)
+    inside_above = (lax.axis_index("brick") < lax.axis_size("brick") - 1).astype(f32)
 
     def plane(x, _):
         total = jnp.ones(levels_ref.shape[2:], f32)
@@ -94,38 +95,34 @@
         return 0
 
     lax.fori_loop(0, planes, plane, 0, unroll=4)
-
-
-def weights_kernel(levels_ref, halo_ref, root_ref, above_ref, below_ref, out_ref):
+    for number in range(len(edge_refs) // 2):
+        low_ref, high_ref = edge_refs[2 * number : 2 * number + 2]
+
+        def edge(x, _, number=number, low_ref=low_ref, high_ref=high_ref):
+            for ref, far in ((low_ref, x), (high_ref, x + planes - deepest)):
+                ref[:, x] = start_ref[pl.ds(number * chunk, chunk), far] * root_ref[far][None]
+            return 0
+
+        lax.fori_loop(0, deepest, edge, 0, unroll=3)
+
+
+def weights_kernel(levels_ref, halo_ref, out_ref):
     planes = levels_ref.shape[1]
 
     def plane(x, _):
-        root = root_ref[x]
-        half = 0.5 * root
         slot = 0
         for position, offset in enumerate(offsets_cube):
-            ahead = jnp.where(
-                x + offset < planes,
-                root_ref[jnp.minimum(x + offset, planes - 1)],
-                above_ref[jnp.maximum(x + offset - planes, 0)],
-            )
-            out_ref[slot, x] = to_weight(levels_ref[position, x]) * half * ahead
-            back = jnp.maximum(x - offset, 0)
-            base = halo_start(position)
-            weight = jnp.where(
-                x >= offset, to_weight(levels_ref[position, back]), halo_ref[base + jnp.minimum(x, offset - 1)]
-            )
-            behind = jnp.where(
-                x >= offset, root_ref[back], below_ref[jnp.clip(deepest + x - offset, 0, deepest - 1)]
-            )
-            out_ref[slot + 1, x] = weight * half * behind
+            out_ref[slot, x] = to_weight(levels_ref[position, x])
+            own = to_weight(levels_ref[position, jnp.maximum(x - offset, 0)])
+            far = halo_ref[halo_start(position) + jnp.minimum(x, offset - 1)]
+            out_ref[slot + 1, x] = jnp.where(x >= offset, own, far)
             slot += 2
         for axis, shift in ((1, shift_rows), (2, shift_lanes)):
             for position, offset in enumerate(offsets_cube):
-                if offset >= root.shape[axis - 1]:
+                if offset >= levels_ref.shape[axis + 1]:
                     continue
                 weight = to_weight(levels_ref[4 * axis + position, x])
-                forward = weight * half * shift(root, offset)
+                forward = weight * shift(jnp.ones_like(weight), offset)
                 out_ref[slot, x] = forward
                 out_ref[slot + 1, x] = shift(forward, -offset)
                 slot += 2
@@ -141,66 +138,77 @@
     return found
 
 
-def filter_plane(ext_ref, weight_ref, x_local, x_plane, terms, rows, lanes, put):
-    for first in range(0, rows, 8):
-        base = pl.multiple_of((x_plane + deepest) * rows + first, 8)
+def filter_plane(ext_ref, weight_ref, root_ref, own_ref, first, x, terms, rows, lanes, put):
+    for row in range(0, rows, 8):
+        base = pl.multiple_of((x + deepest) * rows + row, 8)
         here = ext_ref[:, pl.ds(base, 8), :]
-        total = 0.5 * here
+        total = None
         for slot, (kind, by) in enumerate(terms):
-            weight = weight_ref[slot, x_local, pl.ds(first, 8)]
+            weight = weight_ref[slot, x, pl.ds(row, 8)]
             if kind == "x":
                 moved = ext_ref[:, pl.ds(base + by * rows, 8), :]
             elif kind == "y":
                 moved = ext_ref[:, pl.ds(base + by, 8), :]
             else:
                 moved = pltpu.roll(here, (-by) % lanes, 2)
-            total = total + weight[None] * moved
-        put(first, total)
-
-
-def load_extended(own_ref, below_ref, above_ref, ext_ref, first, rows):
+            term = weight[None] * moved
+            total = term if total is None else total + term
+        own = own_ref[pl.ds(first, ext_ref.shape[0]), x, pl.ds(row, 8)]
+        put(row, 0.5 * (own + root_ref[x, pl.ds(row, 8)][None] * total))
+
+
+def load_extended(own_ref, below_ref, above_ref, root_ref, ext_ref, first, rows):
     count = ext_ref.shape[0]
+    planes = root_ref.shape[0]
     edge = deepest * rows
-    own_rows = own_ref.shape[1]
     ext_ref[:, pl.ds(0, edge)] = below_ref[...]
-    ext_ref[:, pl.ds(edge, own_rows)] = own_ref[pl.ds(first, count)]
-    ext_ref[:, pl.ds(edge + own_rows, edge)] = above_ref[...]
-
-
-def first_filter_kernel(first, terms, rows, lanes, weight_ref, own_ref, below_ref, above_ref,
-                        out_ref, low_ref, high_ref, ext_ref):
+    ext_ref[:, pl.ds(edge + planes * rows, edge)] = above_ref[...]
+
+    def plane(x, _):
+        place = pl.ds(pl.multiple_of(edge + x * rows, rows), rows)
+        ext_ref[:, place] = own_ref[pl.ds(first, count), x] * root_ref[x][None]
+        return 0
+
+    lax.fori_loop(0, planes, plane, 0, unroll=4)
+
+
+def first_filter_kernel(first, terms, rows, lanes, weight_ref, root_ref, own_ref, below_ref, above_ref,
+                        out_ref, low_ref, high_ref, *rest):
+    ext_ref = rest[-1]
     planes = weight_ref.shape[1]
-    load_extended(own_ref, below_ref, above_ref, ext_ref, first, rows)
+    load_extended(own_ref, below_ref, above_ref, root_ref, ext_ref, first, rows)
 
     def plane(x, _):
         def put(row, total):
             out_ref[:, x, pl.ds(row, 8)] = total
 
-        filter_plane(ext_ref, weight_ref, x, x, terms, rows, lanes, put)
+        filter_plane(ext_ref, weight_ref, root_ref, own_ref, first, x, terms, rows, lanes, put)
         return 0
 
     lax.fori_loop(0, planes, plane, 0, unroll=4)
-    low_ref[...] = out_ref[:, :deepest]
-    high_ref[...] = out_ref[:, planes - deepest :]
-
-
-def second_filter_kernel(terms, rows, lanes, vec_ref, weight_ref, own_ref, below_ref, above_ref,
-                         theirs_ref, mine_ref, ext_ref):
-    halves = theirs_ref.shape[1]
-    load_extended(own_ref, below_ref, above_ref, ext_ref, 0, rows)
-    for target_ref, start in ((theirs_ref, (1 - vec_ref[0]) * halves), (mine_ref, vec_ref[0] * halves)):
-
-        def plane(i, _, target_ref=target_ref, start=start):
-            def put(row, total):
-                target_ref[:, i, pl.ds(row, 8)] = total
-
-            filter_plane(ext_ref, weight_ref, start + i, start + i, terms, rows, lanes, put)
-            return 0
-
-        lax.fori_loop(0, halves, plane, 0, unroll=4)
-
-
-def gram_kernel(early, vec_ref, own_x_ref, other_x_ref, *refs):
+    low_ref[...] = out_ref[:, :deepest] * root_ref[:deepest][None]
+    high_ref[...] = out_ref[:, planes - deepest :] * root_ref[planes - deepest :][None]
+
+
+def second_filter_kernel(theirs, terms, rows, lanes, weight_ref, root_ref, own_ref, below_ref, above_ref,
+                         out_ref, *rest):
+    ext_ref = rest[-1]
+    halves = out_ref.shape[1]
+    load_extended(own_ref, below_ref, above_ref, root_ref, ext_ref, 0, rows)
+    vec = lax.axis_index("vec")
+    start = (1 - vec if theirs else vec) * halves
+
+    def plane(i, _):
+        def put(row, total):
+            out_ref[:, i, pl.ds(row, 8)] = total
+
+        filter_plane(ext_ref, weight_ref, root_ref, own_ref, 0, start + i, terms, rows, lanes, put)
+        return 0
+
+    lax.fori_loop(0, halves, plane, 0, unroll=4)
+
+
+def gram_kernel(early, own_x_ref, other_x_ref, *refs):
     if early:
         ys, (out_ref, late_ref, acc_ref) = refs[:2], refs[2:]
         for place, ref in enumerate(ys):
@@ -210,7 +218,7 @@
     cols = own_x_ref.shape[0]
     tiles = own_x_ref.shape[1] // 2
     group = chunk
-    vec = vec_ref[0]
+    vec = lax.axis_index("vec")
     acc_ref[...] = jnp.zeros_like(acc_ref)
 
     def load(kind, number, t):
@@ -297,7 +305,7 @@
     return lax.dot_general(a, b, (((1,), (1,)), ((), ())), precision=highest, preferred_element_type=f32)
 
 
-def algebra_kernel(scale, vec_ref, gram_ref, alpha_ref, beta_ref, table_ref):
+def algebra_kernel(scale, gram_ref, alpha_ref, beta_ref, table_ref, vec_ref):
     grams = [gram_ref[:, 16 * k : 16 * k + 16] for k in range(3)]
     _, inverse = eliminate(grams[0])
     coeffs = times_t(times(inverse, grams[1]), inverse)
@@ -307,7 +315,9 @@
     beta_ref[...] = factor
     of_image = scale * times(second, inverse)
     of_start = -scale * times(times(second, coeffs), inverse)
-    first = vec_ref[0] == 0
+    vec = lax.axis_index("vec").astype(jnp.int32)
+    vec_ref[0] = vec
+    first = vec == 0
     for place, mix in ((0, of_start), (16, of_image)):
         mine = jnp.where(first, mix[:8], mix[8:])
         table_ref[:, place : place + 8] = jnp.where(first, mine[:, :8], mine[:, 8:])
@@ -394,8 +404,6 @@
 def steps_of(levels, start_block):
     own_cols, planes, rows, lanes = start_block.shape
     bricks = lax.axis_size("brick")
-    brick = lax.axis_index("brick")
-    vec = lax.axis_index("vec").astype(jnp.int32)
     voxel_total = bricks * planes * rows * lanes
     halves = planes // 2
     upward = [(i, i + 1) for i in range(bricks - 1)]
@@ -408,99 +416,99 @@
     def down(value):
         return lax.ppermute(value, "brick", downward)
 
-    vec_scalar = vec.reshape(1)
     tail = pl.pallas_call(
         tail_kernel,
         out_shape=jax.ShapeDtypeStruct((sum(offsets_cube), rows, lanes), f32),
-        in_specs=[ANY],
+        in_specs=[HBM],
         out_specs=VMEM,
         scratch_shapes=[
             pltpu.VMEM((sum(offsets_cube), rows, lanes), jnp.int32),
             pltpu.SemaphoreType.DMA((len(offsets_cube),)),
         ],
-        compiler_params=params(4),
+        compiler_params=params(60),
         name="tail",
     )(levels)
     halo = up(tail)
     x_own = start_block.astype(f32)
-    x_above, x_below = [], []
-    numbers = range(own_cols // chunk)
-    for number in numbers:
-        part = start_block[number * chunk : (number + 1) * chunk]
-        x_above.append(down(part[:, :deepest].astype(f32)))
-        x_below.append(up(part[:, planes - deepest :].astype(f32)))
     both = ("brick", "vec")
     x_relayed = []
     for half in range(2):
         direct, first_pairs, second_pairs = swap_tables(half)
-        part = start_block[half * chunk : (half + 1) * chunk].astype(f32)
+        part = x_own[half * chunk : (half + 1) * chunk]
         part = lax.ppermute(part, both, first_pairs)
         x_relayed.append(lax.ppermute(part, both, second_pairs))
     x_other = lax.ppermute(x_own, both, direct)
     x_other = x_other + jnp.concatenate(x_relayed, axis=0)
 
-    inside_above = (brick < bricks - 1).astype(jnp.int32).reshape(1)
-    root = pl.pallas_call(
+    numbers = range(own_cols // chunk)
+    edge = jax.ShapeDtypeStruct((chunk, deepest, rows, lanes), f32)
+    root, *edges = pl.pallas_call(
         degree_kernel,
-        out_shape=jax.ShapeDtypeStruct((planes, rows, lanes), f32),
-        in_specs=[SMEM, VMEM, VMEM],
-        out_specs=VMEM,
+        out_shape=[jax.ShapeDtypeStruct((planes, rows, lanes), f32)] + [edge] * (2 * len(numbers)),
+        in_specs=[VMEM] * 3,
+        out_specs=[VMEM] * (1 + 2 * len(numbers)),
         compiler_params=params(4),
         name="degree",
-    )(inside_above, levels, halo)
-    root_above = down(root[:deepest])
-    root_below = up(root[planes - deepest :])
+    )(levels, halo, x_own)
+    x_above, x_below = [], []
+    for number in numbers:
+        x_above.append(down(edges[2 * number]))
+        x_below.append(up(edges[2 * number + 1]))
 
     terms = terms_of(rows, lanes)
     slots = len(terms)
     weights = pl.pallas_call(
         weights_kernel,
         out_shape=jax.ShapeDtypeStruct((slots, planes, rows, lanes), f32),
-        in_specs=[VMEM] * 5,
+        in_specs=[VMEM] * 2,
         out_specs=VMEM,
         compiler_params=params(4),
         name="weights",
-    )(levels, halo, root, root_above, root_below)
+    )(levels, halo)
     ext = pltpu.VMEM((chunk, (planes + 2 * deepest) * rows, lanes), f32)
 
     def flat(value):
         return value.reshape(value.shape[0], -1, lanes)
 
-    x_flat = flat(x_own)
-
-    def first_filter(number):
-        edge = jax.ShapeDtypeStruct((chunk, deepest, rows, lanes), f32)
+    keep = jax.ShapeDtypeStruct(weights.shape, f32)
+
+    def first_filter(number, weights):
+        field = jax.ShapeDtypeStruct((chunk, planes, rows, lanes), f32)
         return pl.pallas_call(
             functools.partial(first_filter_kernel, number * chunk, terms, rows, lanes),
-            out_shape=[jax.ShapeDtypeStruct((chunk, planes, rows, lanes), f32), edge, edge],
-            in_specs=[VMEM] * 4,
-            out_specs=[VMEM] * 3,
+            out_shape=[field, edge, edge, keep],
+            in_specs=[VMEM] * 5,
+            out_specs=[VMEM] * 4,
             scratch_shapes=[ext],
-            compiler_params=params(10),
-        )(weights, x_flat, flat(x_below[number]), flat(x_above[number]))
-
-    def second_filter(field, below, above):
+            input_output_aliases={0: 3},
+            compiler_params=params(8),
+        )(weights, root, x_own, flat(x_below[number]), flat(x_above[number]))
+
+    def second_filter(theirs, number, weights):
         return pl.pallas_call(
-            functools.partial(second_filter_kernel, terms, rows, lanes),
-            out_shape=[jax.ShapeDtypeStruct((chunk, halves, rows, lanes), f32)] * 2,
-            in_specs=[SMEM] + [VMEM] * 4,
+            functools.partial(second_filter_kernel, theirs, terms, rows, lanes),
+            out_shape=[jax.ShapeDtypeStruct((chunk, halves, rows, lanes), f32), keep],
+            in_specs=[VMEM] * 5,
             out_specs=[VMEM] * 2,
             scratch_shapes=[ext],
-            compiler_params=params(10),
-        )(vec_scalar, weights, flat(field), flat(below), flat(above))
+            input_output_aliases={0: 1},
+            compiler_params=params(8),
+        )(weights, root, fields[number], flat(belows[number]), flat(aboves[number]))
 
     fields, belows, aboves = [], [], []
     for number in numbers:
-        field, low, high = first_filter(number)
+        field, low, high, weights = first_filter(number, weights)
         fields.append(field)
         aboves.append(down(low))
         belows.append(up(high))
     y_theirs, y_mine, y_other_mine = [], [], []
     for number in numbers:
-        theirs, mine = second_filter(fields[number], belows[number], aboves[number])
+        theirs, weights = second_filter(True, number, weights)
         y_theirs.append(theirs)
+        y_other_mine.append(lax.ppermute(theirs, "vec", swap))
+    for number in numbers:
+        mine, weights = second_filter(False, number, weights)
         y_mine.append(mine)
-        y_other_mine.append(lax.ppermute(theirs, "vec", swap))
 
     def tiled(value):
         return value.reshape(value.shape[0], -1, 8, lanes) if value.shape[2] != 8 else value
@@ -511,12 +519,12 @@
         return pl.pallas_call(
             functools.partial(gram_kernel, early),
             out_shape=(out, late) if early else out,
-            in_specs=[SMEM] + [VMEM] * len(operands),
+            in_specs=[VMEM] * len(operands),
             out_specs=(VMEM, VMEM) if early else VMEM,
             scratch_shapes=[pltpu.VMEM((3, 256, 128), f32)],
             compiler_params=params(4),
             name="gram_early" if early else "gram_late",
-        )(vec_scalar, *operands)
+        )(*operands)
 
     mine_tiled = [tiled(value) for value in (x_own, x_other, *y_mine)]
     partial_gram, outgoing = gram_call(True, *mine_tiled)
@@ -525,14 +533,14 @@
     gram = sum_everywhere(gram)
 
     small = jax.ShapeDtypeStruct((16, 16), f32)
-    alpha, beta, table = pl.pallas_call(
+    alpha, beta, table, vec_scalar = pl.pallas_call(
         functools.partial(algebra_kernel, math.sqrt(voxel_total)),
-        out_shape=[small, small, jax.ShapeDtypeStruct((own_cols, 4 * own_cols), f32)],
-        in_specs=[SMEM, VMEM],
-        out_specs=[VMEM] * 3,
+        out_shape=[small, small, jax.ShapeDtypeStruct((own_cols, 4 * own_cols), f32), jax.ShapeDtypeStruct((1,), jnp.int32)],
+        in_specs=[VMEM],
+        out_specs=[VMEM] * 3 + [SMEM],
         compiler_params=params(4),
         name="algebra",
-    )(vec_scalar, gram)
+    )(gram)
 
     def combine(mine, *fields, before=None):
         parts = 4
@@ -556,7 +564,7 @@
             ),
             out_shape=jax.ShapeDtypeStruct((own_cols, planes * rows // 8, 8, lanes), f32),
             input_output_aliases={2 + len(fields): 0} if extra else {},
-            compiler_params=params(10),
+            compiler_params=params(8),
             name="combine",
         )(vec_scalar, table, *map(tiled, fields), *extra)
 

time: 189 us -> 165 us (0.87)
  local copies, waits for them, and re-layouts: 9.73 us -> 0.15 us
  starting transfers between devices: 84.3 us -> 75.8 us
  other arithmetic: 4.72 us -> 0.49 us
  Pallas kernels: 43.5 us -> 39.6 us
  waiting for transfers between devices: 42.4 us -> 45.9 us
    ppermute x6 -> x5, waiting for transfers between devices: 2.71 us -> 15.7 us  [up(): return lax.ppermute(value, 'brick', upward)]
    ppermute x2, waiting for transfers between devices: 7.76 us -> 18.7 us  [steps_of(): y_other_mine.append(lax.ppermute(theirs, 'vec', swap))]
    unnamed x26 -> x4, local copies, waits for them, and re-layouts: 9.7 us -> 0.01 us
    ppermute x5 -> x4, waiting for transfers between devices: 14.6 us -> 5.33 us  [down(): return lax.ppermute(value, 'brick', downward)]
    ppermute x3, waiting for transfers between devices: 11.4 us -> 2.58 us  [sum_everywhere(): lax.ppermute(value, ('brick', 'vec'), pairs[by])]
    ppermute x2, starting transfers between devices: 10.8 us -> 2.02 us  [steps_of(): x_relayed.append(lax.ppermute(part, both, second_pairs))]
    ppermute x3, starting transfers between devices: 7.13 us -> 14.9 us  [sum_everywhere(): lax.ppermute(value, ('brick', 'vec'), pairs[by])]
    ppermute x5 -> x4, starting transfers between devices: 15.3 us -> 8.21 us  [down(): return lax.ppermute(value, 'brick', downward)]
  transfers between devices with their start and end apart: 29 -> 27, of which waited for: 12 -> 14; matrix products, arithmetic and copies ran while one was open for 3% -> 0% of each run, Pallas kernels for 21% -> 20%
where the time goes in v1:
time: 165 us; the launch traced here: 163 us
  starting transfers between devices  75.8 us (46%)
  waiting for transfers between devices  45.9 us (28%)
  Pallas kernels  39.6 us (24%)
    ppermute x5, starting transfers between devices, up(): return lax.ppermute(value, 'brick', upward)  18.9 us
    ppermute x2, waiting for transfers between devices, steps_of(): y_other_mine.append(lax.ppermute(theirs, 'vec', swap))  18.7 us
    ppermute x5, waiting for transfers between devices, up(): return lax.ppermute(value, 'brick', upward)  15.7 us
    ppermute x3, starting transfers between devices, sum_everywhere(): lax.ppermute(value, ('brick', 'vec'), pairs[by])  14.9 us
    ppermute x7, starting transfers between devices, permute(): lax.ppermute(v, 'brick', [(place[0], moved(place, dim, by)) for place in...  13.7 us
    ppermute x2, starting transfers between devices, steps_of(): part = lax.ppermute(part, both, first_pairs)  10.2 us
    pallas_call x2, Pallas kernels, combine(): pl.pallas_call(combine_kernel, grid_spec=pltpu.PrefetchScalarGridSpec(num...  9.35 us
    ppermute x4, starting transfers between devices, down(): return lax.ppermute(value, 'brick', downward)  8.21 us
  transfers between devices with their start and end apart: 27, of which 14 were waited for; matrix products, arithmetic and copies ran while one was open for 0% of the time, Pallas kernels for 20%

profile of v1, /device:TPU:1, one launch (start us, length us, event | category | flops | bytes accessed | tf_op | source)
XLA Modules:
  0.0 162.9 jit_solution(3501732951137363619)
XLA Ops:
  0.6 1.9 %tail.1 = f32[40,16,128]{2,1,0:T(8,128)} custom-call(s32[12,32,16,128]{3,2,1,0:T(8,128)} %levels_ref.5), custom_call_target="tpu_custom_call" | custom-call | tf_op jit(solution)/shard_map/tail/pallas_call | solution.py:419
  2.6 4.6 %collective-permute-start.5 = (f32[40,16,128]{2,1,0:T(8,128)}, f32[40,16,128]{2,1,0:T(8,128)S(1)}, u32[]{:S(2)}, u32[]{:S(2)}) collective-permute-start(f32[40,16,128]{2,1,0:T(8,128)} %tail.1), channel_id=1, source_target_pairs={{0,2},{2,4},{4,6},{6,8},{8,10},{10,12},{12,14},{14,16},{16,18},{18... | collective-permute-start | bytes 983048 | tf_op jit(solution)/shard_map/ppermute | solution.py:414
  7.2 0.2 convert_element_type.3.start_ref.own_ref
  7.4 0.0 copy-start
  7.4 0.1 fusion
  7.6 8.3 %collective-permute-start.1 = (f32[4,32,16,128]{3,2,1,0:T(8,128)S(1)}, f32[4,32,16,128]{3,2,1,0:T(8,128)S(1)}, u32[]{:S(2)}, u32[]{:S(2)}) collective-permute-start(f32[4,32,16,128]{3,2,1,0:T(8,128)S(1)} %get-tuple-element.55), channel_id=1, source_target_pairs={{0,17},{1,16},{2,35},{3,34},{124,77},{125,76},{126,95},{127,94}} | collective-permute-start | bytes 3145736 | tf_op jit(solution)/shard_map/ppermute | solution.py:438
  15.9 1.9 %collective-permute-start.3 = (f32[4,32,16,128]{3,2,1,0:T(8,128)S(1)}, f32[4,32,16,128]{3,2,1,0:T(8,128)S(1)}, u32[]{:S(2)}, u32[]{:S(2)}) collective-permute-start(f32[4,32,16,128]{3,2,1,0:T(8,128)S(1)} %get-tuple-element.56), channel_id=1, source_target_pairs={{0,49},{1,48},{2,3},{3,2},{124,109},{125,108},{126,127},{127,126}} | collective-permute-start | bytes 3145736 | tf_op jit(solution)/shard_map/ppermute | solution.py:438
  17.8 1.4 degree.1
  19.3 1.9 %collective-permute-start.6 = (f32[4,27,16,128]{3,2,1,0:T(8,128)S(1)}, f32[4,27,16,128]{3,2,1,0:T(8,128)S(1)}, u32[]{:S(2)}, u32[]{:S(2)}) collective-permute-start(f32[4,27,16,128]{3,2,1,0:T(8,128)S(1)} %get-tuple-element.30), channel_id=1, source_target_pairs={{0,2},{2,4},{4,6},{6,8},{8,10},{10,12},{12,14},{14,16},{16,18},{18... | collective-permute-start | bytes 2654216 | tf_op jit(solution)/shard_map/ppermute | solution.py:414
  21.2 2.5 %collective-permute-start.7 = (f32[4,27,16,128]{3,2,1,0:T(8,128)S(1)}, f32[4,27,16,128]{3,2,1,0:T(8,128)S(1)}, u32[]{:S(2)}, u32[]{:S(2)}) collective-permute-start(f32[4,27,16,128]{3,2,1,0:T(8,128)S(1)} %get-tuple-element.31), channel_id=1, source_target_pairs={{2,0},{4,2},{6,4},{8,6},{10,8},{12,10},{14,12},{16,14},{18,16},{20... | collective-permute-start | bytes 2654216 | tf_op jit(solution)/shard_map/ppermute | solution.py:417
  23.7 0.8 collective-permute-start
  24.5 6.7 %collective-permute-done.6 = f32[4,27,16,128]{3,2,1,0:T(8,128)S(1)} collective-permute-done((f32[4,27,16,128]{3,2,1,0:T(8,128)S(1)}, f32[4,27,16,128]{3,2,1,0:T(8,128)S(1)}, u32[]{:S(2)}, u32[]{:S(2)}) %collective-permute-start.6) | collective-permute-done | bytes 884768 | tf_op jit(solution)/shard_map/ppermute | solution.py:414
  31.2 4.4 %collective-permute-start.8 = (f32[4,27,16,128]{3,2,1,0:T(8,128)S(1)}, f32[4,27,16,128]{3,2,1,0:T(8,128)S(1)}, u32[]{:S(2)}, u32[]{:S(2)}) collective-permute-start(f32[4,27,16,128]{3,2,1,0:T(8,128)S(1)} %get-tuple-element.33), channel_id=1, source_target_pairs={{0,2},{2,4},{4,6},{6,8},{8,10},{10,12},{12,14},{14,16},{16,18},{18... | collective-permute-start | bytes 2654216 | tf_op jit(solution)/shard_map/ppermute | solution.py:414
  35.5 0.0 collective-permute-done.7
  35.5 1.9 %collective-permute-start.9 = (f32[4,27,16,128]{3,2,1,0:T(8,128)S(1)}, f32[4,27,16,128]{3,2,1,0:T(8,128)S(1)}, u32[]{:S(2)}, u32[]{:S(2)}) collective-permute-start(f32[4,27,16,128]{3,2,1,0:T(8,128)S(1)} %get-tuple-element.34), channel_id=1, source_target_pairs={{2,0},{4,2},{6,4},{8,6},{10,8},{12,10},{14,12},{16,14},{18,16},{20... | collective-permute-start | bytes 2654216 | tf_op jit(solution)/shard_map/ppermute | solution.py:417
  37.5 2.9 %weights.1.weight_ref = f32[22,32,16,128]{3,2,1,0:T(8,128)S(1)} custom-call(s32[12,32,16,128]{3,2,1,0:T(8,128)S(1)} %copy-done, f32[40,16,128]{2,1,0:T(8,128)S(1)} %collective-permute-done.5.halo_ref), custom_call_target="tpu_custom_call" | custom-call | tf_op jit(solution)/shard_map/weights/pallas_call | solution.py:460
  40.3 3.1 %shard_map.49 = (f32[4,32,16,128]{3,2,1,0:T(8,128)S(1)}, f32[4,27,16,128]{3,2,1,0:T(8,128)S(1)}, f32[4,27,16,128]{3,2,1,0:T(8,128)S(1)}, f32[22,32,16,128]{3,2,1,0:T(8,128)S(1)}) custom-call(f32[22,32,16,128]{3,2,1,0:T(8,128)S(1)} %weights.1.weight_ref, f32[32,16,128]{2,1,0:T(8,128)S(1)} %get-tuple-element.29.root_ref, ...), custom_call_target="tpu_custom_call", output_to_operand_aliasing={{3}: (0, {})} | custom-call | tf_op jit(solution)/shard_map/pallas_call | solution.py:477
  43.5 3.6 %collective-permute-start.10 = (f32[4,27,16,128]{3,2,1,0:T(8,128)S(1)}, f32[4,27,16,128]{3,2,1,0:T(8,128)S(1)}, u32[]{:S(2)}, u32[]{:S(2)}) collective-permute-start(f32[4,27,16,128]{3,2,1,0:T(8,128)S(1)} %get-tuple-element.37), channel_id=1, source_target_pairs={{0,2},{2,4},{4,6},{6,8},{8,10},{10,12},{12,14},{14,16},{16,18},{18... | collective-permute-start | bytes 2654216 | tf_op jit(solution)/shard_map/ppermute | solution.py:414
  47.1 0.0 collective-permute-done.3
  47.1 1.9 %collective-permute-start.11 = (f32[4,27,16,128]{3,2,1,0:T(8,128)S(1)}, f32[4,27,16,128]{3,2,1,0:T(8,128)S(1)}, u32[]{:S(2)}, u32[]{:S(2)}) collective-permute-start(f32[4,27,16,128]{3,2,1,0:T(8,128)S(1)} %get-tuple-element.38), channel_id=1, source_target_pairs={{2,0},{4,2},{6,4},{8,6},{10,8},{12,10},{14,12},{16,14},{18,16},{20... | collective-permute-start | bytes 2654216 | tf_op jit(solution)/shard_map/ppermute | solution.py:417
  49.1 1.3 collective-permute-start.2
  50.4 0.7 collective-permute-start.4
  51.1 3.1 %shard_map.50 = (f32[4,32,16,128]{3,2,1,0:T(8,128)S(1)}, f32[4,27,16,128]{3,2,1,0:T(8,128)S(1)}, f32[4,27,16,128]{3,2,1,0:T(8,128)S(1)}, f32[22,32,16,128]{3,2,1,0:T(8,128)S(1)}) custom-call(f32[22,32,16,128]{3,2,1,0:T(8,128)S(1)} %get-tuple-element.32.weight_ref, f32[32,16,128]{2,1,0:T(8,128)S(1)} %get-tuple-element.29.root_ref, ...), custom_call_target="tpu_custom_call", output_to_operand_aliasing={{3}: (0, {})} | custom-call | tf_op jit(solution)/shard_map/pallas_call | solution.py:477
  54.2 2.8 %collective-permute-done.10 = f32[4,27,16,128]{3,2,1,0:T(8,128)S(1)} collective-permute-done((f32[4,27,16,128]{3,2,1,0:T(8,128)S(1)}, f32[4,27,16,128]{3,2,1,0:T(8,128)S(1)}, u32[]{:S(2)}, u32[]{:S(2)}) %collective-permute-start.10) | collective-permute-done | bytes 884768 | tf_op jit(solution)/shard_map/ppermute | solution.py:414
  57.1 4.4 %collective-permute-start.12 = (f32[4,27,16,128]{3,2,1,0:T(8,128)S(1)}, f32[4,27,16,128]{3,2,1,0:T(8,128)S(1)}, u32[]{:S(2)}, u32[]{:S(2)}) collective-permute-start(f32[4,27,16,128]{3,2,1,0:T(8,128)S(1)} %get-tuple-element.41), channel_id=1, source_target_pairs={{0,2},{2,4},{4,6},{6,8},{8,10},{10,12},{12,14},{14,16},{16,18},{18... | collective-permute-start | bytes 2654216 | tf_op jit(solution)/shard_map/ppermute | solution.py:414
  61.5 0.3 collective-permute-done.11
  61.8 1.9 %collective-permute-start.13 = (f32[4,27,16,128]{3,2,1,0:T(8,128)S(1)}, f32[4,27,16,128]{3,2,1,0:T(8,128)S(1)}, u32[]{:S(2)}, u32[]{:S(2)}) collective-permute-start(f32[4,27,16,128]{3,2,1,0:T(8,128)S(1)} %get-tuple-element.42), channel_id=1, source_target_pairs={{2,0},{4,2},{6,4},{8,6},{10,8},{12,10},{14,12},{16,14},{18,16},{20... | collective-permute-start | bytes 2654216 | tf_op jit(solution)/shard_map/ppermute | solution.py:417
  63.7 1.6 shard_map.51
  65.3 6.1 %collective-permute-done.12 = f32[4,27,16,128]{3,2,1,0:T(8,128)S(1)} collective-permute-done((f32[4,27,16,128]{3,2,1,0:T(8,128)S(1)}, f32[4,27,16,128]{3,2,1,0:T(8,128)S(1)}, u32[]{:S(2)}, u32[]{:S(2)}) %collective-permute-start.12) | collective-permute-done | bytes 884768 | tf_op jit(solution)/shard_map/ppermute | solution.py:414
  71.4 5.0 %collective-permute-done.13 = f32[4,27,16,128]{3,2,1,0:T(8,128)S(1)} collective-permute-done((f32[4,27,16,128]{3,2,1,0:T(8,128)S(1)}, f32[4,27,16,128]{3,2,1,0:T(8,128)S(1)}, u32[]{:S(2)}, u32[]{:S(2)}) %collective-permute-start.13) | collective-permute-done | bytes 884768 | tf_op jit(solution)/shard_map/ppermute | solution.py:417
  76.4 1.6 shard_map.52
  78.0 1.6 shard_map.53
  79.6 1.6 shard_map.54
  81.2 3.0 %collective-permute-start.15 = (f32[4,16,16,128]{3,2,1,0:T(8,128)S(1)}, f32[4,16,16,128]{3,2,1,0:T(8,128)S(1)}, u32[]{:S(2)}, u32[]{:S(2)}) collective-permute-start(f32[4,16,16,128]{3,2,1,0:T(8,128)S(1)} %get-tuple-element.48), channel_id=1, source_target_pairs={{0,1},{1,0},{2,3},{3,2},{4,5},{5,4},{6,7},{7,6},{8,9},{9,8},{10,11... | collective-permute-start | bytes 1572872 | tf_op jit(solution)/shard_map/ppermute | solution.py:508
  84.3 0.1 collective-permute-start.14
  84.4 0.3 maximum_add_fusion
  84.7 4.3 %gram_early.1 = (f32[16,128]{1,0:T(8,128)S(1)}, f32[8,32,8,128]{3,2,1,0:T(8,128)S(1)}) custom-call(f32[8,64,8,128]{3,2,1,0:T(8,128)S(1)} %bitcast.19, f32[8,64,8,128]{3,2,1,0:T(8,128)S(1)} %bitcast.23, f32[4,32,8,128]{3,2,1,0:T(8,128)S(1)} %bitcast.27, f32[4,32,8,128]{3,2,1,0:T(8,128)S(1)} %bitcast.30), custom_call_target="tpu_custom_call" | custom-call | tf_op jit(solution)/shard_map/gram_early/pallas_call | solution.py:519
  89.0 3.9 %collective-permute-start.26 = (f32[8,32,8,128]{3,2,1,0:T(8,128)S(1)}, f32[8,32,8,128]{3,2,1,0:T(8,128)S(1)}, u32[]{:S(2)}, u32[]{:S(2)}) collective-permute-start(f32[8,32,8,128]{3,2,1,0:T(8,128)S(1)} %get-tuple-element.54), channel_id=1, source_target_pairs={{0,1},{2,3},{4,5},{6,7},{8,9},{10,11},{12,13},{14,15},{16,17},{18,... | collective-permute-start | bytes 3145736 | tf_op jit(solution)/shard_map/ppermute | solution.py:531
  92.9 8.8 %collective-permute-done.15 = f32[4,16,16,128]{3,2,1,0:T(8,128)S(1)} collective-permute-done((f32[4,16,16,128]{3,2,1,0:T(8,128)S(1)}, f32[4,16,16,128]{3,2,1,0:T(8,128)S(1)}, u32[]{:S(2)}, u32[]{:S(2)}) %collective-permute-start.15) | collective-permute-done | bytes 524320 | tf_op jit(solution)/shard_map/ppermute | solution.py:508
  101.7 9.9 %collective-permute-done.14 = f32[4,16,16,128]{3,2,1,0:T(8,128)S(1)} collective-permute-done((f32[4,16,16,128]{3,2,1,0:T(8,128)S(1)}, f32[4,16,16,128]{3,2,1,0:T(8,128)S(1)}, u32[]{:S(2)}, u32[]{:S(2)}) %collective-permute-start.14) | collective-permute-done | bytes 524320 | tf_op jit(solution)/shard_map/ppermute | solution.py:508
  111.6 2.2 %gram_late.1 = f32[16,128]{1,0:T(8,128)S(1)} custom-call(f32[8,64,8,128]{3,2,1,0:T(8,128)S(1)} %bitcast.20, f32[8,64,8,128]{3,2,1,0:T(8,128)S(1)} %bitcast.24, f32[4,32,8,128]{3,2,1,0:T(8,128)S(1)} %bitcast.28, f32[4,32,8,128]{3,2,1,0:T(8,128)S(1)} %bitcast.31, f32[4,32,8,128]{3,2,1,0:T(8,128)S(1)} %bitcast.43, f32[4,32,8,128]{3,2,1,0:T(8,128)S(1)} %bitcast.41, ...), custom_call_target="tpu_custom_call" | custom-call | tf_op jit(solution)/shard_map/gram_late/pallas_call | solution.py:519
  113.8 0.1 collective-permute-start.16
  113.9 1.2 collective-permute-done.16
  115.1 9.7 %collective-permute-start.17 = (f32[16,128]{1,0:T(8,128)S(1)}, f32[16,128]{1,0:T(8,128)S(1)}, u32[]{:S(2)}, u32[]{:S(2)}) collective-permute-start(f32[16,128]{1,0:T(8,128)S(1)} %add.34), channel_id=1, source_target_pairs={{0,64},{1,65},{2,66},{3,67},{4,68},{5,69},{6,70},{7,71},{8,72},{9,... | collective-permute-start | bytes 24584 | tf_op jit(solution)/shard_map/ppermute | solution.py:396
  124.8 5.2 %collective-permute-start.18 = (f32[16,128]{1,0:T(8,128)S(1)}, f32[16,128]{1,0:T(8,128)S(1)}, u32[]{:S(2)}, u32[]{:S(2)}) collective-permute-start(f32[16,128]{1,0:T(8,128)S(1)} %add.34), channel_id=1, source_target_pairs={{0,1},{1,0},{2,3},{3,2},{4,5},{5,4},{6,7},{7,6},{8,9},{9,8},{10,11... | collective-permute-start | bytes 24584 | tf_op jit(solution)/shard_map/ppermute | solution.py:396
  130.0 0.0 collective-permute-start.19
  130.0 0.0 collective-permute-done.17
  130.0 1.1 collective-permute-done.18
  131.1 1.5 collective-permute-done.19
  132.6 0.0 collective-permute-start.20
  132.6 1.5 collective-permute-start.21
  134.1 1.2 collective-permute-start.22
  135.2 1.0 collective-permute-done.20
  136.3 0.4 collective-permute-done.21
  136.7 0.3 collective-permute-done.22
  137.0 0.9 collective-permute-start.23
  137.8 8.1 %collective-permute-start.24 = (f32[16,128]{1,0:T(8,128)S(1)}, f32[16,128]{1,0:T(8,128)S(1)}, u32[]{:S(2)}, u32[]{:S(2)}) collective-permute-start(f32[16,128]{1,0:T(8,128)S(1)} %add_add_fusion.1), channel_id=1, source_target_pairs={{0,32},{2,34},{4,36},{6,38},{8,40},{10,42},{12,44},{14,46},{16,48}... | collective-permute-start | bytes 24584 | tf_op jit(solution)/shard_map/ppermute | solution.py:385
  145.9 2.0 %collective-permute-start.25 = (f32[16,128]{1,0:T(8,128)S(1)}, f32[16,128]{1,0:T(8,128)S(1)}, u32[]{:S(2)}, u32[]{:S(2)}) collective-permute-start(f32[16,128]{1,0:T(8,128)S(1)} %add_add_fusion.1), channel_id=1, source_target_pairs={{0,48},{2,50},{4,52},{6,54},{8,56},{10,58},{12,60},{14,62},{16,0},... | collective-permute-start | bytes 24584 | tf_op jit(solution)/shard_map/ppermute | solution.py:385
  147.9 0.0 collective-permute-done.23
  147.9 0.0 collective-permute-done.24
  147.9 0.8 collective-permute-done.25
  148.7 4.9 %algebra.1 = (f32[16,16]{1,0:T(8,128)}, f32[16,16]{1,0:T(8,128)}, f32[8,32]{1,0:T(8,128)S(1)}, s32[1]{0:T(128)}) custom-call(f32[16,128]{1,0:T(8,128)S(1)} %add_add_fusion.gram_ref), custom_call_target="tpu_custom_call" | custom-call | tf_op jit(solution)/shard_map/algebra/pallas_call | solution.py:536
  153.6 4.7 %combine.2.refs_3_ = f32[8,64,8,128]{3,2,1,0:T(8,128)} custom-call(s32[1]{0:T(128)} %get-tuple-element.52.vec_ref, f32[8,32]{1,0:T(8,128)S(1)} %get-tuple-element.53.table_ref, f32[8,64,8,128]{3,2,1,0:T(8,128)S(1)} %bitcast.21, f32[8,64,8,128]{3,2,1,0:T(8,128)S(1)} %bitcast.25, f32[4,32,8,128]{3,2,1,0:T(8,128)S(1)} %bitcast.29, ...), custom_call_target="tpu_custom_call" | custom-call | tf_op jit(solution)/shard_map/combine/pallas_call | solution.py:557
  158.2 4.7 %combine.3 = f32[8,64,8,128]{3,2,1,0:T(8,128)} custom-call(s32[1]{0:T(128)} %get-tuple-element.52.vec_ref, f32[8,32]{1,0:T(8,128)S(1)} %get-tuple-element.53.table_ref, f32[8,64,8,128]{3,2,1,0:T(8,128)S(1)} %bitcast.22, f32[8,64,8,128]{3,2,1,0:T(8,128)S(1)} %bitcast.26, f32[4,32,8,128]{3,2,1,0:T(8,128)S(1)} %bitcast.49, ...), custom_call_target="tpu_custom_call", output_to_operand_aliasing={{}: (7, {})} | custom-call | tf_op jit(solution)/shard_map/combine/pallas_call | solution.py:557
  (15 shorter events, 0.0 us)
Async XLA Ops:
  0.6 6.6 %copy-start.1 = (s32[8,32,16,128]{3,2,1,0:T(8,128)S(1)}, s32[8,32,16,128]{3,2,1,0:T(8,128)}, u32[]{:S(2)}) copy-start(s32[8,32,16,128]{3,2,1,0:T(8,128)} %param.3) | copy-start | bytes 6291460
  2.6 15.2 %collective-permute-start.5 = (f32[40,16,128]{2,1,0:T(8,128)}, f32[40,16,128]{2,1,0:T(8,128)S(1)}, u32[]{:S(2)}, u32[]{:S(2)}) collective-permute-start(f32[40,16,128]{2,1,0:T(8,128)} %tail.1), channel_id=1, source_target_pairs={{0,2},{2,4},{4,6},{6,8},{8,10},{10,12},{12,14},{14,16},{16,18},{18... | collective-permute-start | bytes 983048 | tf_op jit(solution)/shard_map/ppermute | solution.py:414
  7.4 10.4 %copy-start = (s32[12,32,16,128]{3,2,1,0:T(8,128)S(1)}, s32[12,32,16,128]{3,2,1,0:T(8,128)}, u32[]{:S(2)}) copy-start(s32[12,32,16,128]{3,2,1,0:T(8,128)} %levels_ref.5) | copy-start | bytes 9437188
  7.6 35.9 %collective-permute-start.1 = (f32[4,32,16,128]{3,2,1,0:T(8,128)S(1)}, f32[4,32,16,128]{3,2,1,0:T(8,128)S(1)}, u32[]{:S(2)}, u32[]{:S(2)}) collective-permute-start(f32[4,32,16,128]{3,2,1,0:T(8,128)S(1)} %get-tuple-element.55), channel_id=1, source_target_pairs={{0,17},{1,16},{2,35},{3,34},{124,77},{125,76},{126,95},{127,94}} | collective-permute-start | bytes 3145736 | tf_op jit(solution)/shard_map/ppermute | solution.py:438
  15.9 31.3 %collective-permute-start.3 = (f32[4,32,16,128]{3,2,1,0:T(8,128)S(1)}, f32[4,32,16,128]{3,2,1,0:T(8,128)S(1)}, u32[]{:S(2)}, u32[]{:S(2)}) collective-permute-start(f32[4,32,16,128]{3,2,1,0:T(8,128)S(1)} %get-tuple-element.56), channel_id=1, source_target_pairs={{0,49},{1,48},{2,3},{3,2},{124,109},{125,108},{126,127},{127,126}} | collective-permute-start | bytes 3145736 | tf_op jit(solution)/shard_map/ppermute | solution.py:438
  19.3 11.9 %collective-permute-start.6 = (f32[4,27,16,128]{3,2,1,0:T(8,128)S(1)}, f32[4,27,16,128]{3,2,1,0:T(8,128)S(1)}, u32[]{:S(2)}, u32[]{:S(2)}) collective-permute-start(f32[4,27,16,128]{3,2,1,0:T(8,128)S(1)} %get-tuple-element.30), channel_id=1, source_target_pairs={{0,2},{2,4},{4,6},{6,8},{8,10},{10,12},{12,14},{14,16},{16,18},{18... | collective-permute-start | bytes 2654216 | tf_op jit(solution)/shard_map/ppermute | solution.py:414
  21.2 14.4 %collective-permute-start.7 = (f32[4,27,16,128]{3,2,1,0:T(8,128)S(1)}, f32[4,27,16,128]{3,2,1,0:T(8,128)S(1)}, u32[]{:S(2)}, u32[]{:S(2)}) collective-permute-start(f32[4,27,16,128]{3,2,1,0:T(8,128)S(1)} %get-tuple-element.31), channel_id=1, source_target_pairs={{2,0},{4,2},{6,4},{8,6},{10,8},{12,10},{14,12},{16,14},{18,16},{20... | collective-permute-start | bytes 2654216 | tf_op jit(solution)/shard_map/ppermute | solution.py:417
  23.7 60.7 %collective-permute-start = (f32[8,32,16,128]{3,2,1,0:T(8,128)S(1)}, f32[8,32,16,128]{3,2,1,0:T(8,128)S(1)}, u32[]{:S(2)}, u32[]{:S(2)}) collective-permute-start(f32[8,32,16,128]{3,2,1,0:T(8,128)S(1)} %convert_element_type.3.start_ref.own_ref), channel_id=1, source_target_pairs={{4,5},{5,4},{6,7},{7,6},{8,9},{9,8},{10,11},{11,10},{12,13},{13,12... | collective-permute-start | bytes 6291464 | tf_op jit(solution)/shard_map/ppermute | solution.py:440
  31.2 17.9 %collective-permute-start.8 = (f32[4,27,16,128]{3,2,1,0:T(8,128)S(1)}, f32[4,27,16,128]{3,2,1,0:T(8,128)S(1)}, u32[]{:S(2)}, u32[]{:S(2)}) collective-permute-start(f32[4,27,16,128]{3,2,1,0:T(8,128)S(1)} %get-tuple-element.33), channel_id=1, source_target_pairs={{0,2},{2,4},{4,6},{6,8},{8,10},{10,12},{12,14},{14,16},{16,18},{18... | collective-permute-start | bytes 2654216 | tf_op jit(solution)/shard_map/ppermute | solution.py:414
  35.5 14.8 %collective-permute-start.9 = (f32[4,27,16,128]{3,2,1,0:T(8,128)S(1)}, f32[4,27,16,128]{3,2,1,0:T(8,128)S(1)}, u32[]{:S(2)}, u32[]{:S(2)}) collective-permute-start(f32[4,27,16,128]{3,2,1,0:T(8,128)S(1)} %get-tuple-element.34), channel_id=1, source_target_pairs={{2,0},{4,2},{6,4},{8,6},{10,8},{12,10},{14,12},{16,14},{18,16},{20... | collective-permute-start | bytes 2654216 | tf_op jit(solution)/shard_map/ppermute | solution.py:417
  43.5 13.6 %collective-permute-start.10 = (f32[4,27,16,128]{3,2,1,0:T(8,128)S(1)}, f32[4,27,16,128]{3,2,1,0:T(8,128)S(1)}, u32[]{:S(2)}, u32[]{:S(2)}) collective-permute-start(f32[4,27,16,128]{3,2,1,0:T(8,128)S(1)} %get-tuple-element.37), channel_id=1, source_target_pairs={{0,2},{2,4},{4,6},{6,8},{8,10},{10,12},{12,14},{14,16},{16,18},{18... | collective-permute-start | bytes 2654216 | tf_op jit(solution)/shard_map/ppermute | solution.py:414
  47.1 14.7 %collective-permute-start.11 = (f32[4,27,16,128]{3,2,1,0:T(8,128)S(1)}, f32[4,27,16,128]{3,2,1,0:T(8,128)S(1)}, u32[]{:S(2)}, u32[]{:S(2)}) collective-permute-start(f32[4,27,16,128]{3,2,1,0:T(8,128)S(1)} %get-tuple-element.38), channel_id=1, source_target_pairs={{2,0},{4,2},{6,4},{8,6},{10,8},{12,10},{14,12},{16,14},{18,16},{20... | collective-permute-start | bytes 2654216 | tf_op jit(solution)/shard_map/ppermute | solution.py:417
  49.1 35.3 %collective-permute-start.2 = (f32[4,32,16,128]{3,2,1,0:T(8,128)S(1)}, f32[4,32,16,128]{3,2,1,0:T(8,128)S(1)}, u32[]{:S(2)}, u32[]{:S(2)}) collective-permute-start(f32[4,32,16,128]{3,2,1,0:T(8,128)S(1)} %collective-permute-done.1), channel_id=1, source_target_pairs={{17,1},{16,0},{35,3},{34,2},{77,125},{76,124},{95,127},{94,126}} | collective-permute-start | bytes 3145736 | tf_op jit(solution)/shard_map/ppermute | solution.py:439
  50.4 34.0 %collective-permute-start.4 = (f32[4,32,16,128]{3,2,1,0:T(8,128)S(1)}, f32[4,32,16,128]{3,2,1,0:T(8,128)S(1)}, u32[]{:S(2)}, u32[]{:S(2)}) collective-permute-start(f32[4,32,16,128]{3,2,1,0:T(8,128)S(1)} %collective-permute-done.3), channel_id=1, source_target_pairs={{49,1},{48,0},{3,3},{2,2},{109,125},{108,124},{127,127},{126,126}} | collective-permute-start | bytes 3145736 | tf_op jit(solution)/shard_map/ppermute | solution.py:439
  57.1 14.4 %collective-permute-start.12 = (f32[4,27,16,128]{3,2,1,0:T(8,128)S(1)}, f32[4,27,16,128]{3,2,1,0:T(8,128)S(1)}, u32[]{:S(2)}, u32[]{:S(2)}) collective-permute-start(f32[4,27,16,128]{3,2,1,0:T(8,128)S(1)} %get-tuple-element.41), channel_id=1, source_target_pairs={{0,2},{2,4},{4,6},{6,8},{8,10},{10,12},{12,14},{14,16},{16,18},{18... | collective-permute-start | bytes 2654216 | tf_op jit(solution)/shard_map/ppermute | solution.py:414
  61.8 14.6 %collective-permute-start.13 = (f32[4,27,16,128]{3,2,1,0:T(8,128)S(1)}, f32[4,27,16,128]{3,2,1,0:T(8,128)S(1)}, u32[]{:S(2)}, u32[]{:S(2)}) collective-permute-start(f32[4,27,16,128]{3,2,1,0:T(8,128)S(1)} %get-tuple-element.42), channel_id=1, source_target_pairs={{2,0},{4,2},{6,4},{8,6},{10,8},{12,10},{14,12},{16,14},{18,16},{20... | collective-permute-start | bytes 2654216 | tf_op jit(solution)/shard_map/ppermute | solution.py:417
  81.2 20.5 %collective-permute-start.15 = (f32[4,16,16,128]{3,2,1,0:T(8,128)S(1)}, f32[4,16,16,128]{3,2,1,0:T(8,128)S(1)}, u32[]{:S(2)}, u32[]{:S(2)}) collective-permute-start(f32[4,16,16,128]{3,2,1,0:T(8,128)S(1)} %get-tuple-element.48), channel_id=1, source_target_pairs={{0,1},{1,0},{2,3},{3,2},{4,5},{5,4},{6,7},{7,6},{8,9},{9,8},{10,11... | collective-permute-start | bytes 1572872 | tf_op jit(solution)/shard_map/ppermute | solution.py:508
  84.3 27.3 %collective-permute-start.14 = (f32[4,16,16,128]{3,2,1,0:T(8,128)S(1)}, f32[4,16,16,128]{3,2,1,0:T(8,128)S(1)}, u32[]{:S(2)}, u32[]{:S(2)}) collective-permute-start(f32[4,16,16,128]{3,2,1,0:T(8,128)S(1)} %get-tuple-element.47), channel_id=1, source_target_pairs={{0,1},{1,0},{2,3},{3,2},{4,5},{5,4},{6,7},{7,6},{8,9},{9,8},{10,11... | collective-permute-start | bytes 1572872 | tf_op jit(solution)/shard_map/ppermute | solution.py:508
  89.0 69.3 %collective-permute-start.26 = (f32[8,32,8,128]{3,2,1,0:T(8,128)S(1)}, f32[8,32,8,128]{3,2,1,0:T(8,128)S(1)}, u32[]{:S(2)}, u32[]{:S(2)}) collective-permute-start(f32[8,32,8,128]{3,2,1,0:T(8,128)S(1)} %get-tuple-element.54), channel_id=1, source_target_pairs={{0,1},{2,3},{4,5},{6,7},{8,9},{10,11},{12,13},{14,15},{16,17},{18,... | collective-permute-start | bytes 3145736 | tf_op jit(solution)/shard_map/ppermute | solution.py:531
  113.8 1.3 collective-permute-start.16
  115.1 14.9 %collective-permute-start.17 = (f32[16,128]{1,0:T(8,128)S(1)}, f32[16,128]{1,0:T(8,128)S(1)}, u32[]{:S(2)}, u32[]{:S(2)}) collective-permute-start(f32[16,128]{1,0:T(8,128)S(1)} %add.34), channel_id=1, source_target_pairs={{0,64},{1,65},{2,66},{3,67},{4,68},{5,69},{6,70},{7,71},{8,72},{9,... | collective-permute-start | bytes 24584 | tf_op jit(solution)/shard_map/ppermute | solution.py:396
  124.8 6.3 %collective-permute-start.18 = (f32[16,128]{1,0:T(8,128)S(1)}, f32[16,128]{1,0:T(8,128)S(1)}, u32[]{:S(2)}, u32[]{:S(2)}) collective-permute-start(f32[16,128]{1,0:T(8,128)S(1)} %add.34), channel_id=1, source_target_pairs={{0,1},{1,0},{2,3},{3,2},{4,5},{5,4},{6,7},{7,6},{8,9},{9,8},{10,11... | collective-permute-start | bytes 24584 | tf_op jit(solution)/shard_map/ppermute | solution.py:396
  130.0 2.6 %collective-permute-start.19 = (f32[16,128]{1,0:T(8,128)S(1)}, f32[16,128]{1,0:T(8,128)S(1)}, u32[]{:S(2)}, u32[]{:S(2)}) collective-permute-start(f32[16,128]{1,0:T(8,128)S(1)} %add.34), channel_id=1, source_target_pairs={{0,65},{1,64},{2,67},{3,66},{4,69},{5,68},{6,71},{7,70},{8,73},{9,... | collective-permute-start | bytes 24584 | tf_op jit(solution)/shard_map/ppermute | solution.py:396
  132.6 3.7 %collective-permute-start.20 = (f32[16,128]{1,0:T(8,128)S(1)}, f32[16,128]{1,0:T(8,128)S(1)}, u32[]{:S(2)}, u32[]{:S(2)}) collective-permute-start(f32[16,128]{1,0:T(8,128)S(1)} %add_add_fusion.2), channel_id=1, source_target_pairs={{0,4},{2,6},{4,8},{6,10},{8,12},{10,14},{12,0},{14,2},{16,20},{18,... | collective-permute-start | bytes 24584 | tf_op jit(solution)/shard_map/ppermute | solution.py:385
  132.6 4.1 %collective-permute-start.21 = (f32[16,128]{1,0:T(8,128)S(1)}, f32[16,128]{1,0:T(8,128)S(1)}, u32[]{:S(2)}, u32[]{:S(2)}) collective-permute-start(f32[16,128]{1,0:T(8,128)S(1)} %add_add_fusion.2), channel_id=1, source_target_pairs={{0,8},{2,10},{4,12},{6,14},{8,0},{10,2},{12,4},{14,6},{16,24},{18,... | collective-permute-start | bytes 24584 | tf_op jit(solution)/shard_map/ppermute | solution.py:385
  134.1 2.9 %collective-permute-start.22 = (f32[16,128]{1,0:T(8,128)S(1)}, f32[16,128]{1,0:T(8,128)S(1)}, u32[]{:S(2)}, u32[]{:S(2)}) collective-permute-start(f32[16,128]{1,0:T(8,128)S(1)} %add_add_fusion.2), channel_id=1, source_target_pairs={{0,12},{2,14},{4,0},{6,2},{8,4},{10,6},{12,8},{14,10},{16,28},{18,... | collective-permute-start | bytes 24584 | tf_op jit(solution)/shard_map/ppermute | solution.py:385
  137.0 10.9 %collective-permute-start.23 = (f32[16,128]{1,0:T(8,128)S(1)}, f32[16,128]{1,0:T(8,128)S(1)}, u32[]{:S(2)}, u32[]{:S(2)}) collective-permute-start(f32[16,128]{1,0:T(8,128)S(1)} %add_add_fusion.1), channel_id=1, source_target_pairs={{0,16},{2,18},{4,20},{6,22},{8,24},{10,26},{12,28},{14,30},{16,32}... | collective-permute-start | bytes 24584 | tf_op jit(solution)/shard_map/ppermute | solution.py:385
  137.8 10.1 %collective-permute-start.24 = (f32[16,128]{1,0:T(8,128)S(1)}, f32[16,128]{1,0:T(8,128)S(1)}, u32[]{:S(2)}, u32[]{:S(2)}) collective-permute-start(f32[16,128]{1,0:T(8,128)S(1)} %add_add_fusion.1), channel_id=1, source_target_pairs={{0,32},{2,34},{4,36},{6,38},{8,40},{10,42},{12,44},{14,46},{16,48}... | collective-permute-start | bytes 24584 | tf_op jit(solution)/shard_map/ppermute | solution.py:385
  145.9 2.8 %collective-permute-start.25 = (f32[16,128]{1,0:T(8,128)S(1)}, f32[16,128]{1,0:T(8,128)S(1)}, u32[]{:S(2)}, u32[]{:S(2)}) collective-permute-start(f32[16,128]{1,0:T(8,128)S(1)} %add_add_fusion.1), channel_id=1, source_target_pairs={{0,48},{2,50},{4,52},{6,54},{8,56},{10,58},{12,60},{14,62},{16,0},... | collective-permute-start | bytes 24584 | tf_op jit(solution)/shard_map/ppermute | solution.py:385

commit v2 on v1

--- a/solution.py
+++ b/solution.py
@@ -128,7 +128,7 @@
                 slot += 2
         return 0
 
-    lax.fori_loop(0, planes, plane, 0, unroll=2)
+    lax.fori_loop(0, planes, plane, 0, unroll=4)
 
 
 def terms_of(rows, lanes):
@@ -305,38 +305,58 @@
     return lax.dot_general(a, b, (((1,), (1,)), ((), ())), precision=highest, preferred_element_type=f32)
 
 
-def algebra_kernel(scale, gram_ref, alpha_ref, beta_ref, table_ref, vec_ref):
-    grams = [gram_ref[:, 16 * k : 16 * k + 16] for k in range(3)]
-    _, inverse = eliminate(grams[0])
-    coeffs = times_t(times(inverse, grams[1]), inverse)
-    image = times_t(times(inverse, grams[2]), inverse)
+def algebra_kernel(scale, gram_ref, alpha_ref, beta_ref, table_ref):
+    size = gram_ref.shape[0]
+    _, inverse = eliminate(gram_ref[:, :size])
+    half_way = times(inverse, gram_ref[...])
+    both = jnp.concatenate([half_way[:, size : 2 * size], half_way[:, 2 * size : 3 * size]], axis=0)
+    both = times_t(both, inverse)
+    coeffs, image = both[:size], both[size:]
     factor, second = eliminate(image - times_t(coeffs, coeffs))
     alpha_ref[...] = coeffs
     beta_ref[...] = factor
-    of_image = scale * times(second, inverse)
-    of_start = -scale * times(times(second, coeffs), inverse)
-    vec = lax.axis_index("vec").astype(jnp.int32)
-    vec_ref[0] = vec
-    first = vec == 0
+    both = times(jnp.concatenate([times(second, coeffs), second], axis=0), inverse)
+    of_start, of_image = -scale * both[:size], scale * both[size:]
+    first = lax.axis_index("vec") == 0
     for place, mix in ((0, of_start), (16, of_image)):
         mine = jnp.where(first, mix[:8], mix[8:])
         table_ref[:, place : place + 8] = jnp.where(first, mine[:, :8], mine[:, 8:])
         table_ref[:, place + 8 : place + 16] = jnp.where(first, mine[:, 8:], mine[:, :8])
 
 
-def combine_kernel(vec_ref, table_ref, own_x_ref, other_x_ref, *refs):
+def combine_kernel(mine, table_ref, own_x_ref, other_x_ref, *refs):
     fields = [own_x_ref, other_x_ref]
     for ref in refs:
         if sum(field.shape[0] for field in fields) < table_ref.shape[1]:
             fields.append(ref)
-    out_ref = refs[-1]
+    out_ref, block_ref, sem = refs[-3:]
     sources = [(ref, k) for ref in fields for k in range(ref.shape[0])]
-    for i in range(out_ref.shape[0]):
-        acc = None
-        for j, (ref, k) in enumerate(sources):
-            term = table_ref[i, j] * ref[k]
-            acc = term if acc is None else acc + term
-        out_ref[i] = acc
+    cols, tiles = block_ref.shape[:2]
+    group = 8
+    vec = lax.axis_index("vec")
+    base = (vec if mine else 1 - vec) * tiles
+
+    def copy(g):
+        place = pl.multiple_of(g * group, group)
+        return pltpu.make_async_copy(
+            block_ref.at[:, pl.ds(place, group)], out_ref.at[:, pl.ds(base + place, group)], sem.at[g]
+        )
+
+    def step(g, _):
+        first = pl.multiple_of(g * group, group)
+        for i in range(cols):
+            acc = None
+            for j, (ref, k) in enumerate(sources):
+                at = base + first if j < 2 * cols else first
+                term = table_ref[i, j] * ref[k, pl.ds(at, group)]
+                acc = term if acc is None else acc + term
+            block_ref[i, pl.ds(first, group)] = acc
+        copy(g).start()
+        return 0
+
+    lax.fori_loop(0, tiles // group, step, 0)
+    for g in range(tiles // group):
+        copy(g).wait()
 
 
 def brick_of(zl, x, y, c):
@@ -357,14 +377,15 @@
 
 def swap_tables(half):
     direct, first, second = [], [], []
-    detour = {0: (1, 3), 1: (2, 0)}
+    detour = {0: ((1, 0), (3, 0)), 1: ((0, 1), (0, 3))}
     for brick, zl, x, y, c in places():
         for vec in range(2):
             here, there = brick * 2 + vec, brick * 2 + 1 - vec
             if not crowded(zl, x, y):
                 direct.append((here, there))
                 continue
-            relay = brick_of(zl, (x + detour[c][half]) % 4, y, c) * 2 + 1 - vec
+            dx, dy = detour[c][half]
+            relay = brick_of(zl, (x + dx) % 4, (y + dy) % 4, c) * 2 + 1 - vec
             first.append((here, relay))
             second.append((relay, there))
     return direct, first, second
@@ -533,40 +554,31 @@
     gram = sum_everywhere(gram)
 
     small = jax.ShapeDtypeStruct((16, 16), f32)
-    alpha, beta, table, vec_scalar = pl.pallas_call(
+    alpha, beta, table = pl.pallas_call(
         functools.partial(algebra_kernel, math.sqrt(voxel_total)),
-        out_shape=[small, small, jax.ShapeDtypeStruct((own_cols, 4 * own_cols), f32), jax.ShapeDtypeStruct((1,), jnp.int32)],
+        out_shape=[small, small, jax.ShapeDtypeStruct((own_cols, 4 * own_cols), f32)],
         in_specs=[VMEM],
-        out_specs=[VMEM] * 3 + [SMEM],
+        out_specs=[VMEM] * 3,
         compiler_params=params(4),
         name="algebra",
     )(gram)
 
     def combine(mine, *fields, before=None):
-        parts = 4
-        block_tiles = halves * rows // 8 // parts
-
-        def whole(g, vec_ref):
-            half = vec_ref[0] if mine else 1 - vec_ref[0]
-            return (0, half * parts + g, 0, 0)
-
+        half_tiles = halves * rows // 8
         extra = [] if before is None else [before]
-        specs = [pl.BlockSpec((own_cols, block_tiles, 8, lanes), whole)] * 2
-        for value in fields[2:]:
-            specs.append(pl.BlockSpec((value.shape[0], block_tiles, 8, lanes), lambda g, vec_ref: (0, g, 0, 0)))
         return pl.pallas_call(
-            combine_kernel,
-            grid_spec=pltpu.PrefetchScalarGridSpec(
-                num_scalar_prefetch=1,
-                grid=(parts,),
-                in_specs=[SMEM] + specs + [ANY] * len(extra),
-                out_specs=pl.BlockSpec((own_cols, block_tiles, 8, lanes), whole),
-            ),
-            out_shape=jax.ShapeDtypeStruct((own_cols, planes * rows // 8, 8, lanes), f32),
-            input_output_aliases={2 + len(fields): 0} if extra else {},
-            compiler_params=params(8),
-            name="combine",
-        )(vec_scalar, table, *map(tiled, fields), *extra)
+            functools.partial(combine_kernel, mine),
+            in_specs=[SMEM] + [VMEM] * len(fields) + [HBM] * len(extra),
+            out_specs=HBM,
+            out_shape=jax.ShapeDtypeStruct((own_cols, 2 * half_tiles, 8, lanes), f32),
+            scratch_shapes=[
+                pltpu.VMEM((own_cols, half_tiles, 8, lanes), f32),
+                pltpu.SemaphoreType.DMA((half_tiles // 8,)),
+            ],
+            input_output_aliases={1 + len(fields): 0} if extra else {},
+            compiler_params=params(4),
+            name="combine_mine" if mine else "combine_theirs",
+        )(table, *map(tiled, fields), *extra)
 
     basis = combine(True, x_own, x_other, *y_mine, *y_other_mine)
     basis = combine(False, x_own, x_other, *y_theirs, late, before=basis)

time: 165 us -> 163 us (0.988)
  starting transfers between devices: 75.8 us -> 63.3 us
  waiting for transfers between devices: 45.9 us -> 57.6 us
  Pallas kernels: 39.6 us -> 37.8 us
    ppermute x4, waiting for transfers between devices: 5.33 us -> 20.6 us  [down(): return lax.ppermute(value, 'brick', downward)]
    ppermute x3, starting transfers between devices: 14.9 us -> 9.44 us  [sum_everywhere(): lax.ppermute(value, ('brick', 'vec'), pairs[by])]
    ppermute x2, waiting for transfers between devices: 18.7 us -> 14.2 us  [steps_of(): y_other_mine.append(lax.ppermute(theirs, 'vec', swap))]
    ppermute x7, starting transfers between devices: 13.7 us -> 10.5 us  [permute(): lax.ppermute(v, 'brick', [(place[0], moved(place, dim, by)) for place in...]
    ppermute x1, starting transfers between devices: 3.93 us -> 1.36 us  [steps_of(): late = lax.ppermute(outgoing, 'vec', [(0, 1)])]
    ppermute x3, waiting for transfers between devices: 2.58 us -> 4.59 us  [sum_everywhere(): lax.ppermute(value, ('brick', 'vec'), pairs[by])]
    ppermute x2, starting transfers between devices: 10.2 us -> 8.45 us  [steps_of(): part = lax.ppermute(part, both, first_pairs)]
where the time goes in v2:
time: 163 us; the launch traced here: 160 us
  starting transfers between devices  63.3 us (39%)
  waiting for transfers between devices  57.6 us (35%)
  Pallas kernels  37.8 us (23%)
    ppermute x4, waiting for transfers between devices, down(): return lax.ppermute(value, 'brick', downward)  20.6 us
    ppermute x5, starting transfers between devices, up(): return lax.ppermute(value, 'brick', upward)  18.9 us
    ppermute x2, waiting for transfers between devices, steps_of(): y_other_mine.append(lax.ppermute(theirs, 'vec', swap))  14.2 us
    ppermute x5, waiting for transfers between devices, up(): return lax.ppermute(value, 'brick', upward)  14.1 us
    ppermute x7, starting transfers between devices, permute(): lax.ppermute(v, 'brick', [(place[0], moved(place, dim, by)) for place in...  10.5 us
    ppermute x3, starting transfers between devices, sum_everywhere(): lax.ppermute(value, ('brick', 'vec'), pairs[by])  9.44 us
    pallas_call x2, Pallas kernels, combine(): pl.pallas_call(functools.partial(combine_kernel, mine), in_specs=[SMEM] +...  8.77 us
    ppermute x2, starting transfers between devices, steps_of(): part = lax.ppermute(part, both, first_pairs)  8.45 us
  transfers between devices with their start and end apart: 27, of which 14 were waited for; matrix products, arithmetic and copies ran while one was open for 0% of the time, Pallas kernels for 20%

profile of v2, /device:TPU:1, one launch (start us, length us, event | category | flops | bytes accessed | tf_op | source)
XLA Modules:
  0.0 160.5 jit_solution(12431388992727369134)
XLA Ops:
  0.6 1.9 %tail.1 = f32[40,16,128]{2,1,0:T(8,128)} custom-call(s32[12,32,16,128]{3,2,1,0:T(8,128)} %levels_ref.5), custom_call_target="tpu_custom_call" | custom-call | tf_op jit(solution)/shard_map/tail/pallas_call | solution.py:440
  2.6 4.6 %collective-permute-start.5 = (f32[40,16,128]{2,1,0:T(8,128)}, f32[40,16,128]{2,1,0:T(8,128)S(1)}, u32[]{:S(2)}, u32[]{:S(2)}) collective-permute-start(f32[40,16,128]{2,1,0:T(8,128)} %tail.1), channel_id=1, source_target_pairs={{0,2},{2,4},{4,6},{6,8},{8,10},{10,12},{12,14},{14,16},{16,18},{18... | collective-permute-start | bytes 983048 | tf_op jit(solution)/shard_map/ppermute | solution.py:435
  7.2 0.2 convert_element_type.3.start_ref.own_ref
  7.4 0.0 copy-start
  7.4 0.1 fusion
  7.6 6.8 %collective-permute-start.1 = (f32[4,32,16,128]{3,2,1,0:T(8,128)S(1)}, f32[4,32,16,128]{3,2,1,0:T(8,128)S(1)}, u32[]{:S(2)}, u32[]{:S(2)}) collective-permute-start(f32[4,32,16,128]{3,2,1,0:T(8,128)S(1)} %get-tuple-element.53), channel_id=1, source_target_pairs={{0,17},{1,16},{2,7},{3,6},{124,77},{125,76},{126,115},{127,114}} | collective-permute-start | bytes 3145736 | tf_op jit(solution)/shard_map/ppermute | solution.py:459
  14.4 1.6 %collective-permute-start.3 = (f32[4,32,16,128]{3,2,1,0:T(8,128)S(1)}, f32[4,32,16,128]{3,2,1,0:T(8,128)S(1)}, u32[]{:S(2)}, u32[]{:S(2)}) collective-permute-start(f32[4,32,16,128]{3,2,1,0:T(8,128)S(1)} %get-tuple-element.54), channel_id=1, source_target_pairs={{0,49},{1,48},{2,15},{3,14},{124,109},{125,108},{126,123},{127,122}} | collective-permute-start | bytes 3145736 | tf_op jit(solution)/shard_map/ppermute | solution.py:459
  16.0 1.4 degree.1
  17.5 1.9 %collective-permute-start.6 = (f32[4,27,16,128]{3,2,1,0:T(8,128)S(1)}, f32[4,27,16,128]{3,2,1,0:T(8,128)S(1)}, u32[]{:S(2)}, u32[]{:S(2)}) collective-permute-start(f32[4,27,16,128]{3,2,1,0:T(8,128)S(1)} %get-tuple-element.29), channel_id=1, source_target_pairs={{0,2},{2,4},{4,6},{6,8},{8,10},{10,12},{12,14},{14,16},{16,18},{18... | collective-permute-start | bytes 2654216 | tf_op jit(solution)/shard_map/ppermute | solution.py:435
  19.4 2.5 %collective-permute-start.7 = (f32[4,27,16,128]{3,2,1,0:T(8,128)S(1)}, f32[4,27,16,128]{3,2,1,0:T(8,128)S(1)}, u32[]{:S(2)}, u32[]{:S(2)}) collective-permute-start(f32[4,27,16,128]{3,2,1,0:T(8,128)S(1)} %get-tuple-element.30), channel_id=1, source_target_pairs={{2,0},{4,2},{6,4},{8,6},{10,8},{12,10},{14,12},{16,14},{18,16},{20... | collective-permute-start | bytes 2654216 | tf_op jit(solution)/shard_map/ppermute | solution.py:438
  21.9 0.8 collective-permute-start
  22.7 12.8 %collective-permute-done.6 = f32[4,27,16,128]{3,2,1,0:T(8,128)S(1)} collective-permute-done((f32[4,27,16,128]{3,2,1,0:T(8,128)S(1)}, f32[4,27,16,128]{3,2,1,0:T(8,128)S(1)}, u32[]{:S(2)}, u32[]{:S(2)}) %collective-permute-start.6) | collective-permute-done | bytes 884768 | tf_op jit(solution)/shard_map/ppermute | solution.py:435
  35.5 4.4 %collective-permute-start.8 = (f32[4,27,16,128]{3,2,1,0:T(8,128)S(1)}, f32[4,27,16,128]{3,2,1,0:T(8,128)S(1)}, u32[]{:S(2)}, u32[]{:S(2)}) collective-permute-start(f32[4,27,16,128]{3,2,1,0:T(8,128)S(1)} %get-tuple-element.32), channel_id=1, source_target_pairs={{0,2},{2,4},{4,6},{6,8},{8,10},{10,12},{12,14},{14,16},{16,18},{18... | collective-permute-start | bytes 2654216 | tf_op jit(solution)/shard_map/ppermute | solution.py:435
  39.9 0.0 collective-permute-done.7
  39.9 1.9 %collective-permute-start.9 = (f32[4,27,16,128]{3,2,1,0:T(8,128)S(1)}, f32[4,27,16,128]{3,2,1,0:T(8,128)S(1)}, u32[]{:S(2)}, u32[]{:S(2)}) collective-permute-start(f32[4,27,16,128]{3,2,1,0:T(8,128)S(1)} %get-tuple-element.33), channel_id=1, source_target_pairs={{2,0},{4,2},{6,4},{8,6},{10,8},{12,10},{14,12},{16,14},{18,16},{20... | collective-permute-start | bytes 2654216 | tf_op jit(solution)/shard_map/ppermute | solution.py:438
  41.9 1.4 weights.1.weight_ref
  43.2 3.1 %shard_map.49 = (f32[4,32,16,128]{3,2,1,0:T(8,128)S(1)}, f32[4,27,16,128]{3,2,1,0:T(8,128)S(1)}, f32[4,27,16,128]{3,2,1,0:T(8,128)S(1)}, f32[22,32,16,128]{3,2,1,0:T(8,128)S(1)}) custom-call(f32[22,32,16,128]{3,2,1,0:T(8,128)S(1)} %weights.1.weight_ref, f32[32,16,128]{2,1,0:T(8,128)S(1)} %get-tuple-element.28.root_ref, ...), custom_call_target="tpu_custom_call", output_to_operand_aliasing={{3}: (0, {})} | custom-call | tf_op jit(solution)/shard_map/pallas_call | solution.py:498
  46.4 0.0 collective-permute-done.1
  46.4 3.6 %collective-permute-start.10 = (f32[4,27,16,128]{3,2,1,0:T(8,128)S(1)}, f32[4,27,16,128]{3,2,1,0:T(8,128)S(1)}, u32[]{:S(2)}, u32[]{:S(2)}) collective-permute-start(f32[4,27,16,128]{3,2,1,0:T(8,128)S(1)} %get-tuple-element.36), channel_id=1, source_target_pairs={{0,2},{2,4},{4,6},{6,8},{8,10},{10,12},{12,14},{14,16},{16,18},{18... | collective-permute-start | bytes 2654216 | tf_op jit(solution)/shard_map/ppermute | solution.py:435
  50.0 0.0 collective-permute-done.3
  50.0 1.9 %collective-permute-start.11 = (f32[4,27,16,128]{3,2,1,0:T(8,128)S(1)}, f32[4,27,16,128]{3,2,1,0:T(8,128)S(1)}, u32[]{:S(2)}, u32[]{:S(2)}) collective-permute-start(f32[4,27,16,128]{3,2,1,0:T(8,128)S(1)} %get-tuple-element.37), channel_id=1, source_target_pairs={{2,0},{4,2},{6,4},{8,6},{10,8},{12,10},{14,12},{16,14},{18,16},{20... | collective-permute-start | bytes 2654216 | tf_op jit(solution)/shard_map/ppermute | solution.py:438
  52.0 1.3 collective-permute-start.2
  53.3 1.0 collective-permute-done.9
  54.3 1.3 collective-permute-start.4
  55.6 3.1 %shard_map.50 = (f32[4,32,16,128]{3,2,1,0:T(8,128)S(1)}, f32[4,27,16,128]{3,2,1,0:T(8,128)S(1)}, f32[4,27,16,128]{3,2,1,0:T(8,128)S(1)}, f32[22,32,16,128]{3,2,1,0:T(8,128)S(1)}) custom-call(f32[22,32,16,128]{3,2,1,0:T(8,128)S(1)} %get-tuple-element.31.weight_ref, f32[32,16,128]{2,1,0:T(8,128)S(1)} %get-tuple-element.28.root_ref, ...), custom_call_target="tpu_custom_call", output_to_operand_aliasing={{3}: (0, {})} | custom-call | tf_op jit(solution)/shard_map/pallas_call | solution.py:498
  58.7 1.3 collective-permute-done.10
  60.0 4.4 %collective-permute-start.12 = (f32[4,27,16,128]{3,2,1,0:T(8,128)S(1)}, f32[4,27,16,128]{3,2,1,0:T(8,128)S(1)}, u32[]{:S(2)}, u32[]{:S(2)}) collective-permute-start(f32[4,27,16,128]{3,2,1,0:T(8,128)S(1)} %get-tuple-element.40), channel_id=1, source_target_pairs={{0,2},{2,4},{4,6},{6,8},{8,10},{10,12},{12,14},{14,16},{16,18},{18... | collective-permute-start | bytes 2654216 | tf_op jit(solution)/shard_map/ppermute | solution.py:435
  64.4 8.4 %collective-permute-done.11 = f32[4,27,16,128]{3,2,1,0:T(8,128)S(1)} collective-permute-done((f32[4,27,16,128]{3,2,1,0:T(8,128)S(1)}, f32[4,27,16,128]{3,2,1,0:T(8,128)S(1)}, u32[]{:S(2)}, u32[]{:S(2)}) %collective-permute-start.11) | collective-permute-done | bytes 884768 | tf_op jit(solution)/shard_map/ppermute | solution.py:438
  72.8 1.9 %collective-permute-start.13 = (f32[4,27,16,128]{3,2,1,0:T(8,128)S(1)}, f32[4,27,16,128]{3,2,1,0:T(8,128)S(1)}, u32[]{:S(2)}, u32[]{:S(2)}) collective-permute-start(f32[4,27,16,128]{3,2,1,0:T(8,128)S(1)} %get-tuple-element.41), channel_id=1, source_target_pairs={{2,0},{4,2},{6,4},{8,6},{10,8},{12,10},{14,12},{16,14},{18,16},{20... | collective-permute-start | bytes 2654216 | tf_op jit(solution)/shard_map/ppermute | solution.py:438
  74.7 1.6 shard_map.51
  76.3 11.1 %collective-permute-done.13 = f32[4,27,16,128]{3,2,1,0:T(8,128)S(1)} collective-permute-done((f32[4,27,16,128]{3,2,1,0:T(8,128)S(1)}, f32[4,27,16,128]{3,2,1,0:T(8,128)S(1)}, u32[]{:S(2)}, u32[]{:S(2)}) %collective-permute-start.13) | collective-permute-done | bytes 884768 | tf_op jit(solution)/shard_map/ppermute | solution.py:438
  87.4 1.6 shard_map.52
  89.0 1.6 shard_map.53
  90.6 1.6 shard_map.54
  92.3 0.2 collective-permute-start.15
  92.5 2.8 %collective-permute-start.14 = (f32[4,16,16,128]{3,2,1,0:T(8,128)S(1)}, f32[4,16,16,128]{3,2,1,0:T(8,128)S(1)}, u32[]{:S(2)}, u32[]{:S(2)}) collective-permute-start(f32[4,16,16,128]{3,2,1,0:T(8,128)S(1)} %get-tuple-element.46), channel_id=1, source_target_pairs={{0,1},{1,0},{2,3},{3,2},{4,5},{5,4},{6,7},{7,6},{8,9},{9,8},{10,11... | collective-permute-start | bytes 1572872 | tf_op jit(solution)/shard_map/ppermute | solution.py:529
  95.3 0.0 collective-permute-done.2
  95.3 0.0 collective-permute-done.4
  95.3 0.0 collective-permute-done
  95.3 0.3 maximum_add_fusion
  95.6 4.3 %gram_early.1 = (f32[16,128]{1,0:T(8,128)S(1)}, f32[8,32,8,128]{3,2,1,0:T(8,128)S(1)}) custom-call(f32[8,64,8,128]{3,2,1,0:T(8,128)S(1)} %bitcast.19, f32[8,64,8,128]{3,2,1,0:T(8,128)S(1)} %bitcast.23, f32[4,32,8,128]{3,2,1,0:T(8,128)S(1)} %bitcast.27, f32[4,32,8,128]{3,2,1,0:T(8,128)S(1)} %bitcast.30), custom_call_target="tpu_custom_call" | custom-call | tf_op jit(solution)/shard_map/gram_early/pallas_call | solution.py:540
  99.9 1.4 collective-permute-start.26
  101.3 6.5 %collective-permute-done.15 = f32[4,16,16,128]{3,2,1,0:T(8,128)S(1)} collective-permute-done((f32[4,16,16,128]{3,2,1,0:T(8,128)S(1)}, f32[4,16,16,128]{3,2,1,0:T(8,128)S(1)}, u32[]{:S(2)}, u32[]{:S(2)}) %collective-permute-start.15) | collective-permute-done | bytes 524320 | tf_op jit(solution)/shard_map/ppermute | solution.py:529
  107.8 7.7 %collective-permute-done.14 = f32[4,16,16,128]{3,2,1,0:T(8,128)S(1)} collective-permute-done((f32[4,16,16,128]{3,2,1,0:T(8,128)S(1)}, f32[4,16,16,128]{3,2,1,0:T(8,128)S(1)}, u32[]{:S(2)}, u32[]{:S(2)}) %collective-permute-start.14) | collective-permute-done | bytes 524320 | tf_op jit(solution)/shard_map/ppermute | solution.py:529
  115.5 2.2 %gram_late.1 = f32[16,128]{1,0:T(8,128)S(1)} custom-call(f32[8,64,8,128]{3,2,1,0:T(8,128)S(1)} %bitcast.20, f32[8,64,8,128]{3,2,1,0:T(8,128)S(1)} %bitcast.24, f32[4,32,8,128]{3,2,1,0:T(8,128)S(1)} %bitcast.28, f32[4,32,8,128]{3,2,1,0:T(8,128)S(1)} %bitcast.31, f32[4,32,8,128]{3,2,1,0:T(8,128)S(1)} %bitcast.43, f32[4,32,8,128]{3,2,1,0:T(8,128)S(1)} %bitcast.41, ...), custom_call_target="tpu_custom_call" | custom-call | tf_op jit(solution)/shard_map/gram_late/pallas_call | solution.py:540
  117.7 0.1 collective-permute-start.16
  117.8 1.2 collective-permute-done.16
  118.9 4.2 %collective-permute-start.17 = (f32[16,128]{1,0:T(8,128)S(1)}, f32[16,128]{1,0:T(8,128)S(1)}, u32[]{:S(2)}, u32[]{:S(2)}) collective-permute-start(f32[16,128]{1,0:T(8,128)S(1)} %add.34), channel_id=1, source_target_pairs={{0,64},{1,65},{2,66},{3,67},{4,68},{5,69},{6,70},{7,71},{8,72},{9,... | collective-permute-start | bytes 24584 | tf_op jit(solution)/shard_map/ppermute | solution.py:417
  123.2 5.2 %collective-permute-start.18 = (f32[16,128]{1,0:T(8,128)S(1)}, f32[16,128]{1,0:T(8,128)S(1)}, u32[]{:S(2)}, u32[]{:S(2)}) collective-permute-start(f32[16,128]{1,0:T(8,128)S(1)} %add.34), channel_id=1, source_target_pairs={{0,1},{1,0},{2,3},{3,2},{4,5},{5,4},{6,7},{7,6},{8,9},{9,8},{10,11... | collective-permute-start | bytes 24584 | tf_op jit(solution)/shard_map/ppermute | solution.py:417
  128.4 4.5 %collective-permute-done.17 = f32[16,128]{1,0:T(8,128)S(1)} collective-permute-done((f32[16,128]{1,0:T(8,128)S(1)}, f32[16,128]{1,0:T(8,128)S(1)}, u32[]{:S(2)}, u32[]{:S(2)}) %collective-permute-start.17) | collective-permute-done | bytes 8224 | tf_op jit(solution)/shard_map/ppermute | solution.py:417
  132.9 0.1 collective-permute-done.18
  133.0 0.0 collective-permute-start.20
  133.0 0.1 collective-permute-start.21
  133.1 2.6 %collective-permute-start.22 = (f32[16,128]{1,0:T(8,128)S(1)}, f32[16,128]{1,0:T(8,128)S(1)}, u32[]{:S(2)}, u32[]{:S(2)}) collective-permute-start(f32[16,128]{1,0:T(8,128)S(1)} %add_add_fusion.2), channel_id=1, source_target_pairs={{0,12},{2,14},{4,0},{6,2},{8,4},{10,6},{12,8},{14,10},{16,28},{18,... | collective-permute-start | bytes 24584 | tf_op jit(solution)/shard_map/ppermute | solution.py:406
  135.7 1.0 collective-permute-done.20
  136.7 0.5 collective-permute-done.21
  137.2 0.5 collective-permute-done.22
  137.7 6.1 %collective-permute-start.24 = (f32[16,128]{1,0:T(8,128)S(1)}, f32[16,128]{1,0:T(8,128)S(1)}, u32[]{:S(2)}, u32[]{:S(2)}) collective-permute-start(f32[16,128]{1,0:T(8,128)S(1)} %add_add_fusion.1), channel_id=1, source_target_pairs={{0,32},{2,34},{4,36},{6,38},{8,40},{10,42},{12,44},{14,46},{16,48}... | collective-permute-start | bytes 24584 | tf_op jit(solution)/shard_map/ppermute | solution.py:406
  143.8 1.6 %collective-permute-start.25 = (f32[16,128]{1,0:T(8,128)S(1)}, f32[16,128]{1,0:T(8,128)S(1)}, u32[]{:S(2)}, u32[]{:S(2)}) collective-permute-start(f32[16,128]{1,0:T(8,128)S(1)} %add_add_fusion.1), channel_id=1, source_target_pairs={{0,48},{2,50},{4,52},{6,54},{8,56},{10,58},{12,60},{14,62},{16,0},... | collective-permute-start | bytes 24584 | tf_op jit(solution)/shard_map/ppermute | solution.py:406
  145.4 0.9 collective-permute-done.25
  146.4 5.2 %algebra.1 = (f32[16,16]{1,0:T(8,128)}, f32[16,16]{1,0:T(8,128)}, f32[8,32]{1,0:T(8,128)S(1)}) custom-call(f32[16,128]{1,0:T(8,128)S(1)} %add_add_fusion.gram_ref), custom_call_target="tpu_custom_call" | custom-call | tf_op jit(solution)/shard_map/algebra/pallas_call | solution.py:557
  151.5 4.4 %combine_mine.1.refs_3_ = f32[8,64,8,128]{3,2,1,0:T(8,128)} custom-call(f32[8,32]{1,0:T(8,128)S(1)} %get-tuple-element.51.table_ref, f32[8,64,8,128]{3,2,1,0:T(8,128)S(1)} %bitcast.21, f32[8,64,8,128]{3,2,1,0:T(8,128)S(1)} %bitcast.25, f32[4,32,8,128]{3,2,1,0:T(8,128)S(1)} %bitcast.29, f32[4,32,8,128]{3,2,1,0:T(8,128)S(1)} %bitcast.32, ...), custom_call_target="tpu_custom_call" | custom-call | tf_op jit(solution)/shard_map/combine_mine/pallas_call | solution.py:569
  155.9 0.0 collective-permute-done.26.refs_2_
  155.9 4.4 %combine_theirs.1 = f32[8,64,8,128]{3,2,1,0:T(8,128)} custom-call(f32[8,32]{1,0:T(8,128)S(1)} %get-tuple-element.51.table_ref, f32[8,64,8,128]{3,2,1,0:T(8,128)S(1)} %bitcast.22, f32[8,64,8,128]{3,2,1,0:T(8,128)S(1)} %bitcast.26, f32[4,32,8,128]{3,2,1,0:T(8,128)S(1)} %bitcast.49, f32[4,32,8,128]{3,2,1,0:T(8,128)S(1)} %bitcast.50, ...), custom_call_target="tpu_custom_call", output_to_operand_aliasing={{}: (6, {})} | custom-call | tf_op jit(solution)/shard_map/combine_theirs/pallas_call | solution.py:569
  (15 shorter events, 0.0 us)
Async XLA Ops:
  0.6 6.6 %copy-start.1 = (s32[8,32,16,128]{3,2,1,0:T(8,128)S(1)}, s32[8,32,16,128]{3,2,1,0:T(8,128)}, u32[]{:S(2)}) copy-start(s32[8,32,16,128]{3,2,1,0:T(8,128)} %param.3) | copy-start | bytes 6291460
  2.6 13.4 %collective-permute-start.5 = (f32[40,16,128]{2,1,0:T(8,128)}, f32[40,16,128]{2,1,0:T(8,128)S(1)}, u32[]{:S(2)}, u32[]{:S(2)}) collective-permute-start(f32[40,16,128]{2,1,0:T(8,128)} %tail.1), channel_id=1, source_target_pairs={{0,2},{2,4},{4,6},{6,8},{8,10},{10,12},{12,14},{14,16},{16,18},{18... | collective-permute-start | bytes 983048 | tf_op jit(solution)/shard_map/ppermute | solution.py:435
  7.4 8.6 %copy-start = (s32[12,32,16,128]{3,2,1,0:T(8,128)S(1)}, s32[12,32,16,128]{3,2,1,0:T(8,128)}, u32[]{:S(2)}) copy-start(s32[12,32,16,128]{3,2,1,0:T(8,128)} %levels_ref.5) | copy-start | bytes 9437188
  7.6 38.8 %collective-permute-start.1 = (f32[4,32,16,128]{3,2,1,0:T(8,128)S(1)}, f32[4,32,16,128]{3,2,1,0:T(8,128)S(1)}, u32[]{:S(2)}, u32[]{:S(2)}) collective-permute-start(f32[4,32,16,128]{3,2,1,0:T(8,128)S(1)} %get-tuple-element.53), channel_id=1, source_target_pairs={{0,17},{1,16},{2,7},{3,6},{124,77},{125,76},{126,115},{127,114}} | collective-permute-start | bytes 3145736 | tf_op jit(solution)/shard_map/ppermute | solution.py:459
  14.4 35.6 %collective-permute-start.3 = (f32[4,32,16,128]{3,2,1,0:T(8,128)S(1)}, f32[4,32,16,128]{3,2,1,0:T(8,128)S(1)}, u32[]{:S(2)}, u32[]{:S(2)}) collective-permute-start(f32[4,32,16,128]{3,2,1,0:T(8,128)S(1)} %get-tuple-element.54), channel_id=1, source_target_pairs={{0,49},{1,48},{2,15},{3,14},{124,109},{125,108},{126,123},{127,122}} | collective-permute-start | bytes 3145736 | tf_op jit(solution)/shard_map/ppermute | solution.py:459
  17.5 18.0 %collective-permute-start.6 = (f32[4,27,16,128]{3,2,1,0:T(8,128)S(1)}, f32[4,27,16,128]{3,2,1,0:T(8,128)S(1)}, u32[]{:S(2)}, u32[]{:S(2)}) collective-permute-start(f32[4,27,16,128]{3,2,1,0:T(8,128)S(1)} %get-tuple-element.29), channel_id=1, source_target_pairs={{0,2},{2,4},{4,6},{6,8},{8,10},{10,12},{12,14},{14,16},{16,18},{18... | collective-permute-start | bytes 2654216 | tf_op jit(solution)/shard_map/ppermute | solution.py:435
  19.4 20.5 %collective-permute-start.7 = (f32[4,27,16,128]{3,2,1,0:T(8,128)S(1)}, f32[4,27,16,128]{3,2,1,0:T(8,128)S(1)}, u32[]{:S(2)}, u32[]{:S(2)}) collective-permute-start(f32[4,27,16,128]{3,2,1,0:T(8,128)S(1)} %get-tuple-element.30), channel_id=1, source_target_pairs={{2,0},{4,2},{6,4},{8,6},{10,8},{12,10},{14,12},{16,14},{18,16},{20... | collective-permute-start | bytes 2654216 | tf_op jit(solution)/shard_map/ppermute | solution.py:438
  21.9 73.4 %collective-permute-start = (f32[8,32,16,128]{3,2,1,0:T(8,128)S(1)}, f32[8,32,16,128]{3,2,1,0:T(8,128)S(1)}, u32[]{:S(2)}, u32[]{:S(2)}) collective-permute-start(f32[8,32,16,128]{3,2,1,0:T(8,128)S(1)} %convert_element_type.3.start_ref.own_ref), channel_id=1, source_target_pairs={{4,5},{5,4},{6,7},{7,6},{8,9},{9,8},{10,11},{11,10},{12,13},{13,12... | collective-permute-start | bytes 6291464 | tf_op jit(solution)/shard_map/ppermute | solution.py:461
  35.5 16.4 %collective-permute-start.8 = (f32[4,27,16,128]{3,2,1,0:T(8,128)S(1)}, f32[4,27,16,128]{3,2,1,0:T(8,128)S(1)}, u32[]{:S(2)}, u32[]{:S(2)}) collective-permute-start(f32[4,27,16,128]{3,2,1,0:T(8,128)S(1)} %get-tuple-element.32), channel_id=1, source_target_pairs={{0,2},{2,4},{4,6},{6,8},{8,10},{10,12},{12,14},{14,16},{16,18},{18... | collective-permute-start | bytes 2654216 | tf_op jit(solution)/shard_map/ppermute | solution.py:435
  39.9 14.4 %collective-permute-start.9 = (f32[4,27,16,128]{3,2,1,0:T(8,128)S(1)}, f32[4,27,16,128]{3,2,1,0:T(8,128)S(1)}, u32[]{:S(2)}, u32[]{:S(2)}) collective-permute-start(f32[4,27,16,128]{3,2,1,0:T(8,128)S(1)} %get-tuple-element.33), channel_id=1, source_target_pairs={{2,0},{4,2},{6,4},{8,6},{10,8},{12,10},{14,12},{16,14},{18,16},{20... | collective-permute-start | bytes 2654216 | tf_op jit(solution)/shard_map/ppermute | solution.py:438
  46.4 13.6 %collective-permute-start.10 = (f32[4,27,16,128]{3,2,1,0:T(8,128)S(1)}, f32[4,27,16,128]{3,2,1,0:T(8,128)S(1)}, u32[]{:S(2)}, u32[]{:S(2)}) collective-permute-start(f32[4,27,16,128]{3,2,1,0:T(8,128)S(1)} %get-tuple-element.36), channel_id=1, source_target_pairs={{0,2},{2,4},{4,6},{6,8},{8,10},{10,12},{12,14},{14,16},{16,18},{18... | collective-permute-start | bytes 2654216 | tf_op jit(solution)/shard_map/ppermute | solution.py:435
  50.0 22.8 %collective-permute-start.11 = (f32[4,27,16,128]{3,2,1,0:T(8,128)S(1)}, f32[4,27,16,128]{3,2,1,0:T(8,128)S(1)}, u32[]{:S(2)}, u32[]{:S(2)}) collective-permute-start(f32[4,27,16,128]{3,2,1,0:T(8,128)S(1)} %get-tuple-element.37), channel_id=1, source_target_pairs={{2,0},{4,2},{6,4},{8,6},{10,8},{12,10},{14,12},{16,14},{18,16},{20... | collective-permute-start | bytes 2654216 | tf_op jit(solution)/shard_map/ppermute | solution.py:438
  52.0 43.3 %collective-permute-start.2 = (f32[4,32,16,128]{3,2,1,0:T(8,128)S(1)}, f32[4,32,16,128]{3,2,1,0:T(8,128)S(1)}, u32[]{:S(2)}, u32[]{:S(2)}) collective-permute-start(f32[4,32,16,128]{3,2,1,0:T(8,128)S(1)} %collective-permute-done.1), channel_id=1, source_target_pairs={{17,1},{16,0},{7,3},{6,2},{77,125},{76,124},{115,127},{114,126}} | collective-permute-start | bytes 3145736 | tf_op jit(solution)/shard_map/ppermute | solution.py:460
  54.3 41.0 %collective-permute-start.4 = (f32[4,32,16,128]{3,2,1,0:T(8,128)S(1)}, f32[4,32,16,128]{3,2,1,0:T(8,128)S(1)}, u32[]{:S(2)}, u32[]{:S(2)}) collective-permute-start(f32[4,32,16,128]{3,2,1,0:T(8,128)S(1)} %collective-permute-done.3), channel_id=1, source_target_pairs={{49,1},{48,0},{15,3},{14,2},{109,125},{108,124},{123,127},{122,126}} | collective-permute-start | bytes 3145736 | tf_op jit(solution)/shard_map/ppermute | solution.py:460
  60.0 16.3 %collective-permute-start.12 = (f32[4,27,16,128]{3,2,1,0:T(8,128)S(1)}, f32[4,27,16,128]{3,2,1,0:T(8,128)S(1)}, u32[]{:S(2)}, u32[]{:S(2)}) collective-permute-start(f32[4,27,16,128]{3,2,1,0:T(8,128)S(1)} %get-tuple-element.40), channel_id=1, source_target_pairs={{0,2},{2,4},{4,6},{6,8},{8,10},{10,12},{12,14},{14,16},{16,18},{18... | collective-permute-start | bytes 2654216 | tf_op jit(solution)/shard_map/ppermute | solution.py:435
  72.8 14.6 %collective-permute-start.13 = (f32[4,27,16,128]{3,2,1,0:T(8,128)S(1)}, f32[4,27,16,128]{3,2,1,0:T(8,128)S(1)}, u32[]{:S(2)}, u32[]{:S(2)}) collective-permute-start(f32[4,27,16,128]{3,2,1,0:T(8,128)S(1)} %get-tuple-element.41), channel_id=1, source_target_pairs={{2,0},{4,2},{6,4},{8,6},{10,8},{12,10},{14,12},{16,14},{18,16},{20... | collective-permute-start | bytes 2654216 | tf_op jit(solution)/shard_map/ppermute | solution.py:438
  92.3 15.5 %collective-permute-start.15 = (f32[4,16,16,128]{3,2,1,0:T(8,128)S(1)}, f32[4,16,16,128]{3,2,1,0:T(8,128)S(1)}, u32[]{:S(2)}, u32[]{:S(2)}) collective-permute-start(f32[4,16,16,128]{3,2,1,0:T(8,128)S(1)} %get-tuple-element.47), channel_id=1, source_target_pairs={{0,1},{1,0},{2,3},{3,2},{4,5},{5,4},{6,7},{7,6},{8,9},{9,8},{10,11... | collective-permute-start | bytes 1572872 | tf_op jit(solution)/shard_map/ppermute | solution.py:529
  92.5 23.0 %collective-permute-start.14 = (f32[4,16,16,128]{3,2,1,0:T(8,128)S(1)}, f32[4,16,16,128]{3,2,1,0:T(8,128)S(1)}, u32[]{:S(2)}, u32[]{:S(2)}) collective-permute-start(f32[4,16,16,128]{3,2,1,0:T(8,128)S(1)} %get-tuple-element.46), channel_id=1, source_target_pairs={{0,1},{1,0},{2,3},{3,2},{4,5},{5,4},{6,7},{7,6},{8,9},{9,8},{10,11... | collective-permute-start | bytes 1572872 | tf_op jit(solution)/shard_map/ppermute | solution.py:529
  99.9 56.0 %collective-permute-start.26 = (f32[8,32,8,128]{3,2,1,0:T(8,128)S(1)}, f32[8,32,8,128]{3,2,1,0:T(8,128)S(1)}, u32[]{:S(2)}, u32[]{:S(2)}) collective-permute-start(f32[8,32,8,128]{3,2,1,0:T(8,128)S(1)} %get-tuple-element.52), channel_id=1, source_target_pairs={{0,1},{2,3},{4,5},{6,7},{8,9},{10,11},{12,13},{14,15},{16,17},{18,... | collective-permute-start | bytes 3145736 | tf_op jit(solution)/shard_map/ppermute | solution.py:552
  117.7 1.3 collective-permute-start.16
  118.9 13.9 %collective-permute-start.17 = (f32[16,128]{1,0:T(8,128)S(1)}, f32[16,128]{1,0:T(8,128)S(1)}, u32[]{:S(2)}, u32[]{:S(2)}) collective-permute-start(f32[16,128]{1,0:T(8,128)S(1)} %add.34), channel_id=1, source_target_pairs={{0,64},{1,65},{2,66},{3,67},{4,68},{5,69},{6,70},{7,71},{8,72},{9,... | collective-permute-start | bytes 24584 | tf_op jit(solution)/shard_map/ppermute | solution.py:417
  123.2 9.8 %collective-permute-start.18 = (f32[16,128]{1,0:T(8,128)S(1)}, f32[16,128]{1,0:T(8,128)S(1)}, u32[]{:S(2)}, u32[]{:S(2)}) collective-permute-start(f32[16,128]{1,0:T(8,128)S(1)} %add.34), channel_id=1, source_target_pairs={{0,1},{1,0},{2,3},{3,2},{4,5},{5,4},{6,7},{7,6},{8,9},{9,8},{10,11... | collective-permute-start | bytes 24584 | tf_op jit(solution)/shard_map/ppermute | solution.py:417
  128.4 4.6 %collective-permute-start.19 = (f32[16,128]{1,0:T(8,128)S(1)}, f32[16,128]{1,0:T(8,128)S(1)}, u32[]{:S(2)}, u32[]{:S(2)}) collective-permute-start(f32[16,128]{1,0:T(8,128)S(1)} %add.34), channel_id=1, source_target_pairs={{0,65},{1,64},{2,67},{3,66},{4,69},{5,68},{6,71},{7,70},{8,73},{9,... | collective-permute-start | bytes 24584 | tf_op jit(solution)/shard_map/ppermute | solution.py:417
  133.0 3.8 %collective-permute-start.20 = (f32[16,128]{1,0:T(8,128)S(1)}, f32[16,128]{1,0:T(8,128)S(1)}, u32[]{:S(2)}, u32[]{:S(2)}) collective-permute-start(f32[16,128]{1,0:T(8,128)S(1)} %add_add_fusion.2), channel_id=1, source_target_pairs={{0,4},{2,6},{4,8},{6,10},{8,12},{10,14},{12,0},{14,2},{16,20},{18,... | collective-permute-start | bytes 24584 | tf_op jit(solution)/shard_map/ppermute | solution.py:406
  133.0 4.2 %collective-permute-start.21 = (f32[16,128]{1,0:T(8,128)S(1)}, f32[16,128]{1,0:T(8,128)S(1)}, u32[]{:S(2)}, u32[]{:S(2)}) collective-permute-start(f32[16,128]{1,0:T(8,128)S(1)} %add_add_fusion.2), channel_id=1, source_target_pairs={{0,8},{2,10},{4,12},{6,14},{8,0},{10,2},{12,4},{14,6},{16,24},{18,... | collective-permute-start | bytes 24584 | tf_op jit(solution)/shard_map/ppermute | solution.py:406
  133.1 4.6 %collective-permute-start.22 = (f32[16,128]{1,0:T(8,128)S(1)}, f32[16,128]{1,0:T(8,128)S(1)}, u32[]{:S(2)}, u32[]{:S(2)}) collective-permute-start(f32[16,128]{1,0:T(8,128)S(1)} %add_add_fusion.2), channel_id=1, source_target_pairs={{0,12},{2,14},{4,0},{6,2},{8,4},{10,6},{12,8},{14,10},{16,28},{18,... | collective-permute-start | bytes 24584 | tf_op jit(solution)/shard_map/ppermute | solution.py:406
  137.7 7.7 %collective-permute-start.23 = (f32[16,128]{1,0:T(8,128)S(1)}, f32[16,128]{1,0:T(8,128)S(1)}, u32[]{:S(2)}, u32[]{:S(2)}) collective-permute-start(f32[16,128]{1,0:T(8,128)S(1)} %add_add_fusion.1), channel_id=1, source_target_pairs={{0,16},{2,18},{4,20},{6,22},{8,24},{10,26},{12,28},{14,30},{16,32}... | collective-permute-start | bytes 24584 | tf_op jit(solution)/shard_map/ppermute | solution.py:406
  137.7 7.7 %collective-permute-start.24 = (f32[16,128]{1,0:T(8,128)S(1)}, f32[16,128]{1,0:T(8,128)S(1)}, u32[]{:S(2)}, u32[]{:S(2)}) collective-permute-start(f32[16,128]{1,0:T(8,128)S(1)} %add_add_fusion.1), channel_id=1, source_target_pairs={{0,32},{2,34},{4,36},{6,38},{8,40},{10,42},{12,44},{14,46},{16,48}... | collective-permute-start | bytes 24584 | tf_op jit(solution)/shard_map/ppermute | solution.py:406
  143.8 2.6 %collective-permute-start.25 = (f32[16,128]{1,0:T(8,128)S(1)}, f32[16,128]{1,0:T(8,128)S(1)}, u32[]{:S(2)}, u32[]{:S(2)}) collective-permute-start(f32[16,128]{1,0:T(8,128)S(1)} %add_add_fusion.1), channel_id=1, source_target_pairs={{0,48},{2,50},{4,52},{6,54},{8,56},{10,58},{12,60},{14,62},{16,0},... | collective-permute-start | bytes 24584 | tf_op jit(solution)/shard_map/ppermute | solution.py:406

commit v3 on v2

--- a/solution.py
+++ b/solution.py
@@ -320,14 +320,15 @@
     first = lax.axis_index("vec") == 0
     for place, mix in ((0, of_start), (16, of_image)):
         mine = jnp.where(first, mix[:8], mix[8:])
-        table_ref[:, place : place + 8] = jnp.where(first, mine[:, :8], mine[:, 8:])
-        table_ref[:, place + 8 : place + 16] = jnp.where(first, mine[:, 8:], mine[:, :8])
+        for part, half in enumerate((jnp.where(first, mine[:, :8], mine[:, 8:]), jnp.where(first, mine[:, 8:], mine[:, :8]))):
+            for j in range(8):
+                table_ref[place + 8 * part + j] = jnp.broadcast_to(half[:, j : j + 1], table_ref.shape[1:])
 
 
 def combine_kernel(mine, table_ref, own_x_ref, other_x_ref, *refs):
     fields = [own_x_ref, other_x_ref]
     for ref in refs:
-        if sum(field.shape[0] for field in fields) < table_ref.shape[1]:
+        if sum(field.shape[0] for field in fields) < table_ref.shape[0]:
             fields.append(ref)
     out_ref, block_ref, sem = refs[-3:]
     sources = [(ref, k) for ref in fields for k in range(ref.shape[0])]
@@ -348,7 +349,8 @@
             acc = None
             for j, (ref, k) in enumerate(sources):
                 at = base + first if j < 2 * cols else first
-                term = table_ref[i, j] * ref[k, pl.ds(at, group)]
+                factor = jnp.broadcast_to(table_ref[j, pl.ds(i, 1)], table_ref.shape[1:])
+                term = factor[None] * ref[k, pl.ds(at, group)]
                 acc = term if acc is None else acc + term
             block_ref[i, pl.ds(first, group)] = acc
         copy(g).start()
@@ -556,7 +558,7 @@
     small = jax.ShapeDtypeStruct((16, 16), f32)
     alpha, beta, table = pl.pallas_call(
         functools.partial(algebra_kernel, math.sqrt(voxel_total)),
-        out_shape=[small, small, jax.ShapeDtypeStruct((own_cols, 4 * own_cols), f32)],
+        out_shape=[small, small, jax.ShapeDtypeStruct((4 * own_cols, own_cols, lanes), f32)],
         in_specs=[VMEM],
         out_specs=[VMEM] * 3,
         compiler_params=params(4),
@@ -568,7 +570,7 @@
         extra = [] if before is None else [before]
         return pl.pallas_call(
             functools.partial(combine_kernel, mine),
-            in_specs=[SMEM] + [VMEM] * len(fields) + [HBM] * len(extra),
+            in_specs=[VMEM] * (1 + len(fields)) + [HBM] * len(extra),
             out_specs=HBM,
             out_shape=jax.ShapeDtypeStruct((own_cols, 2 * half_tiles, 8, lanes), f32),
             scratch_shapes=[

time: 163 us -> 162 us (level)
  transfers between devices with their start and end apart: 27 -> 27, of which waited for: 14 -> 14; matrix products, arithmetic and copies ran while one was open for 0% -> 0% of each run, Pallas kernels for 20% -> 19%
where the time goes in v3:
time: 162 us; the launch traced here: 159 us
  starting transfers between devices  63.3 us (39%)
  waiting for transfers between devices  57.6 us (36%)
  Pallas kernels  36.5 us (23%)
    ppermute x4, waiting for transfers between devices, down(): return lax.ppermute(value, 'brick', downward)  20.6 us
    ppermute x5, starting transfers between devices, up(): return lax.ppermute(value, 'brick', upward)  18.9 us
    ppermute x2, waiting for transfers between devices, steps_of(): y_other_mine.append(lax.ppermute(theirs, 'vec', swap))  14.2 us
    ppermute x5, waiting for transfers between devices, up(): return lax.ppermute(value, 'brick', upward)  14.1 us
    ppermute x7, starting transfers between devices, permute(): lax.ppermute(v, 'brick', [(place[0], moved(place, dim, by)) for place in...  10.5 us
    ppermute x3, starting transfers between devices, sum_everywhere(): lax.ppermute(value, ('brick', 'vec'), pairs[by])  9.44 us
    ppermute x2, starting transfers between devices, steps_of(): part = lax.ppermute(part, both, first_pairs)  8.45 us
    ppermute x4, starting transfers between devices, down(): return lax.ppermute(value, 'brick', downward)  8.21 us
  transfers between devices with their start and end apart: 27, of which 14 were waited for; matrix products, arithmetic and copies ran while one was open for 0% of the time, Pallas kernels for 19%

profile of v3, /device:TPU:1, one launch (start us, length us, event | category | flops | bytes accessed | tf_op | source)
XLA Modules:
  0.0 159.2 jit_solution(5069695375264768507)
XLA Ops:
  0.6 1.9 %tail.1 = f32[40,16,128]{2,1,0:T(8,128)} custom-call(s32[12,32,16,128]{3,2,1,0:T(8,128)} %levels_ref.5), custom_call_target="tpu_custom_call" | custom-call | tf_op jit(solution)/shard_map/tail/pallas_call | solution.py:442
  2.6 4.6 %collective-permute-start.5 = (f32[40,16,128]{2,1,0:T(8,128)}, f32[40,16,128]{2,1,0:T(8,128)S(1)}, u32[]{:S(2)}, u32[]{:S(2)}) collective-permute-start(f32[40,16,128]{2,1,0:T(8,128)} %tail.1), channel_id=1, source_target_pairs={{0,2},{2,4},{4,6},{6,8},{8,10},{10,12},{12,14},{14,16},{16,18},{18... | collective-permute-start | bytes 983048 | tf_op jit(solution)/shard_map/ppermute | solution.py:437
  7.2 0.2 convert_element_type.3.start_ref.own_ref
  7.4 0.0 copy-start
  7.4 0.1 fusion
  7.6 6.8 %collective-permute-start.1 = (f32[4,32,16,128]{3,2,1,0:T(8,128)S(1)}, f32[4,32,16,128]{3,2,1,0:T(8,128)S(1)}, u32[]{:S(2)}, u32[]{:S(2)}) collective-permute-start(f32[4,32,16,128]{3,2,1,0:T(8,128)S(1)} %get-tuple-element.53), channel_id=1, source_target_pairs={{0,17},{1,16},{2,7},{3,6},{124,77},{125,76},{126,115},{127,114}} | collective-permute-start | bytes 3145736 | tf_op jit(solution)/shard_map/ppermute | solution.py:461
  14.4 1.6 %collective-permute-start.3 = (f32[4,32,16,128]{3,2,1,0:T(8,128)S(1)}, f32[4,32,16,128]{3,2,1,0:T(8,128)S(1)}, u32[]{:S(2)}, u32[]{:S(2)}) collective-permute-start(f32[4,32,16,128]{3,2,1,0:T(8,128)S(1)} %get-tuple-element.54), channel_id=1, source_target_pairs={{0,49},{1,48},{2,15},{3,14},{124,109},{125,108},{126,123},{127,122}} | collective-permute-start | bytes 3145736 | tf_op jit(solution)/shard_map/ppermute | solution.py:461
  16.0 1.4 degree.1
  17.5 1.9 %collective-permute-start.6 = (f32[4,27,16,128]{3,2,1,0:T(8,128)S(1)}, f32[4,27,16,128]{3,2,1,0:T(8,128)S(1)}, u32[]{:S(2)}, u32[]{:S(2)}) collective-permute-start(f32[4,27,16,128]{3,2,1,0:T(8,128)S(1)} %get-tuple-element.29), channel_id=1, source_target_pairs={{0,2},{2,4},{4,6},{6,8},{8,10},{10,12},{12,14},{14,16},{16,18},{18... | collective-permute-start | bytes 2654216 | tf_op jit(solution)/shard_map/ppermute | solution.py:437
  19.4 2.5 %collective-permute-start.7 = (f32[4,27,16,128]{3,2,1,0:T(8,128)S(1)}, f32[4,27,16,128]{3,2,1,0:T(8,128)S(1)}, u32[]{:S(2)}, u32[]{:S(2)}) collective-permute-start(f32[4,27,16,128]{3,2,1,0:T(8,128)S(1)} %get-tuple-element.30), channel_id=1, source_target_pairs={{2,0},{4,2},{6,4},{8,6},{10,8},{12,10},{14,12},{16,14},{18,16},{20... | collective-permute-start | bytes 2654216 | tf_op jit(solution)/shard_map/ppermute | solution.py:440
  21.9 0.8 collective-permute-start
  22.7 12.8 %collective-permute-done.6 = f32[4,27,16,128]{3,2,1,0:T(8,128)S(1)} collective-permute-done((f32[4,27,16,128]{3,2,1,0:T(8,128)S(1)}, f32[4,27,16,128]{3,2,1,0:T(8,128)S(1)}, u32[]{:S(2)}, u32[]{:S(2)}) %collective-permute-start.6) | collective-permute-done | bytes 884768 | tf_op jit(solution)/shard_map/ppermute | solution.py:437
  35.5 4.4 %collective-permute-start.8 = (f32[4,27,16,128]{3,2,1,0:T(8,128)S(1)}, f32[4,27,16,128]{3,2,1,0:T(8,128)S(1)}, u32[]{:S(2)}, u32[]{:S(2)}) collective-permute-start(f32[4,27,16,128]{3,2,1,0:T(8,128)S(1)} %get-tuple-element.32), channel_id=1, source_target_pairs={{0,2},{2,4},{4,6},{6,8},{8,10},{10,12},{12,14},{14,16},{16,18},{18... | collective-permute-start | bytes 2654216 | tf_op jit(solution)/shard_map/ppermute | solution.py:437
  39.9 0.0 collective-permute-done.7
  39.9 1.9 %collective-permute-start.9 = (f32[4,27,16,128]{3,2,1,0:T(8,128)S(1)}, f32[4,27,16,128]{3,2,1,0:T(8,128)S(1)}, u32[]{:S(2)}, u32[]{:S(2)}) collective-permute-start(f32[4,27,16,128]{3,2,1,0:T(8,128)S(1)} %get-tuple-element.33), channel_id=1, source_target_pairs={{2,0},{4,2},{6,4},{8,6},{10,8},{12,10},{14,12},{16,14},{18,16},{20... | collective-permute-start | bytes 2654216 | tf_op jit(solution)/shard_map/ppermute | solution.py:440
  41.9 1.4 weights.1.weight_ref
  43.2 3.1 %shard_map.49 = (f32[4,32,16,128]{3,2,1,0:T(8,128)S(1)}, f32[4,27,16,128]{3,2,1,0:T(8,128)S(1)}, f32[4,27,16,128]{3,2,1,0:T(8,128)S(1)}, f32[22,32,16,128]{3,2,1,0:T(8,128)S(1)}) custom-call(f32[22,32,16,128]{3,2,1,0:T(8,128)S(1)} %weights.1.weight_ref, f32[32,16,128]{2,1,0:T(8,128)S(1)} %get-tuple-element.28.root_ref, ...), custom_call_target="tpu_custom_call", output_to_operand_aliasing={{3}: (0, {})} | custom-call | tf_op jit(solution)/shard_map/pallas_call | solution.py:500
  46.4 0.0 collective-permute-done.1
  46.4 3.6 %collective-permute-start.10 = (f32[4,27,16,128]{3,2,1,0:T(8,128)S(1)}, f32[4,27,16,128]{3,2,1,0:T(8,128)S(1)}, u32[]{:S(2)}, u32[]{:S(2)}) collective-permute-start(f32[4,27,16,128]{3,2,1,0:T(8,128)S(1)} %get-tuple-element.36), channel_id=1, source_target_pairs={{0,2},{2,4},{4,6},{6,8},{8,10},{10,12},{12,14},{14,16},{16,18},{18... | collective-permute-start | bytes 2654216 | tf_op jit(solution)/shard_map/ppermute | solution.py:437
  50.0 0.0 collective-permute-done.3
  50.0 1.9 %collective-permute-start.11 = (f32[4,27,16,128]{3,2,1,0:T(8,128)S(1)}, f32[4,27,16,128]{3,2,1,0:T(8,128)S(1)}, u32[]{:S(2)}, u32[]{:S(2)}) collective-permute-start(f32[4,27,16,128]{3,2,1,0:T(8,128)S(1)} %get-tuple-element.37), channel_id=1, source_target_pairs={{2,0},{4,2},{6,4},{8,6},{10,8},{12,10},{14,12},{16,14},{18,16},{20... | collective-permute-start | bytes 2654216 | tf_op jit(solution)/shard_map/ppermute | solution.py:440
  52.0 1.3 collective-permute-start.2
  53.3 1.0 collective-permute-done.9
  54.3 1.3 collective-permute-start.4
  55.6 3.1 %shard_map.50 = (f32[4,32,16,128]{3,2,1,0:T(8,128)S(1)}, f32[4,27,16,128]{3,2,1,0:T(8,128)S(1)}, f32[4,27,16,128]{3,2,1,0:T(8,128)S(1)}, f32[22,32,16,128]{3,2,1,0:T(8,128)S(1)}) custom-call(f32[22,32,16,128]{3,2,1,0:T(8,128)S(1)} %get-tuple-element.31.weight_ref, f32[32,16,128]{2,1,0:T(8,128)S(1)} %get-tuple-element.28.root_ref, ...), custom_call_target="tpu_custom_call", output_to_operand_aliasing={{3}: (0, {})} | custom-call | tf_op jit(solution)/shard_map/pallas_call | solution.py:500
  58.7 1.3 collective-permute-done.10
  60.0 4.4 %collective-permute-start.12 = (f32[4,27,16,128]{3,2,1,0:T(8,128)S(1)}, f32[4,27,16,128]{3,2,1,0:T(8,128)S(1)}, u32[]{:S(2)}, u32[]{:S(2)}) collective-permute-start(f32[4,27,16,128]{3,2,1,0:T(8,128)S(1)} %get-tuple-element.40), channel_id=1, source_target_pairs={{0,2},{2,4},{4,6},{6,8},{8,10},{10,12},{12,14},{14,16},{16,18},{18... | collective-permute-start | bytes 2654216 | tf_op jit(solution)/shard_map/ppermute | solution.py:437
  64.4 8.4 %collective-permute-done.11 = f32[4,27,16,128]{3,2,1,0:T(8,128)S(1)} collective-permute-done((f32[4,27,16,128]{3,2,1,0:T(8,128)S(1)}, f32[4,27,16,128]{3,2,1,0:T(8,128)S(1)}, u32[]{:S(2)}, u32[]{:S(2)}) %collective-permute-start.11) | collective-permute-done | bytes 884768 | tf_op jit(solution)/shard_map/ppermute | solution.py:440
  72.8 1.9 %collective-permute-start.13 = (f32[4,27,16,128]{3,2,1,0:T(8,128)S(1)}, f32[4,27,16,128]{3,2,1,0:T(8,128)S(1)}, u32[]{:S(2)}, u32[]{:S(2)}) collective-permute-start(f32[4,27,16,128]{3,2,1,0:T(8,128)S(1)} %get-tuple-element.41), channel_id=1, source_target_pairs={{2,0},{4,2},{6,4},{8,6},{10,8},{12,10},{14,12},{16,14},{18,16},{20... | collective-permute-start | bytes 2654216 | tf_op jit(solution)/shard_map/ppermute | solution.py:440
  74.7 1.6 %shard_map.51 = (f32[4,16,16,128]{3,2,1,0:T(8,128)S(1)}, f32[22,32,16,128]{3,2,1,0:T(8,128)S(1)}) custom-call(f32[22,32,16,128]{3,2,1,0:T(8,128)S(1)} %get-tuple-element.34.weight_ref, f32[32,16,128]{2,1,0:T(8,128)S(1)} %get-tuple-element.28.root_ref, f32[4,32,16,128]{3,2,1,0:T(8,128)S(1)} %get-tuple-element.35.own_ref, ...), custom_call_target="tpu_custom_call", output_to_operand_aliasing={{1}: (0, {})} | custom-call | tf_op jit(solution)/shard_map/pallas_call | solution.py:511
  76.3 11.1 %collective-permute-done.13 = f32[4,27,16,128]{3,2,1,0:T(8,128)S(1)} collective-permute-done((f32[4,27,16,128]{3,2,1,0:T(8,128)S(1)}, f32[4,27,16,128]{3,2,1,0:T(8,128)S(1)}, u32[]{:S(2)}, u32[]{:S(2)}) %collective-permute-start.13) | collective-permute-done | bytes 884768 | tf_op jit(solution)/shard_map/ppermute | solution.py:440
  87.4 1.6 shard_map.52
  89.0 1.6 %shard_map.53 = (f32[4,16,16,128]{3,2,1,0:T(8,128)S(1)}, f32[22,32,16,128]{3,2,1,0:T(8,128)S(1)}) custom-call(f32[22,32,16,128]{3,2,1,0:T(8,128)S(1)} %get-tuple-element.42.weight_ref, f32[32,16,128]{2,1,0:T(8,128)S(1)} %get-tuple-element.28.root_ref, f32[4,32,16,128]{3,2,1,0:T(8,128)S(1)} %get-tuple-element.35.own_ref, ...), custom_call_target="tpu_custom_call", output_to_operand_aliasing={{1}: (0, {})} | custom-call | tf_op jit(solution)/shard_map/pallas_call | solution.py:511
  90.6 1.6 %shard_map.54 = (f32[4,16,16,128]{3,2,1,0:T(8,128)S(1)}, f32[22,32,16,128]{3,2,1,0:T(8,128)S(1)}) custom-call(f32[22,32,16,128]{3,2,1,0:T(8,128)S(1)} %get-tuple-element.44.weight_ref, f32[32,16,128]{2,1,0:T(8,128)S(1)} %get-tuple-element.28.root_ref, f32[4,32,16,128]{3,2,1,0:T(8,128)S(1)} %get-tuple-element.39.own_ref, ...), custom_call_target="tpu_custom_call", output_to_operand_aliasing={{1}: (0, {})} | custom-call | tf_op jit(solution)/shard_map/pallas_call | solution.py:511
  92.3 0.2 collective-permute-start.15
  92.5 2.8 %collective-permute-start.14 = (f32[4,16,16,128]{3,2,1,0:T(8,128)S(1)}, f32[4,16,16,128]{3,2,1,0:T(8,128)S(1)}, u32[]{:S(2)}, u32[]{:S(2)}) collective-permute-start(f32[4,16,16,128]{3,2,1,0:T(8,128)S(1)} %get-tuple-element.46), channel_id=1, source_target_pairs={{0,1},{1,0},{2,3},{3,2},{4,5},{5,4},{6,7},{7,6},{8,9},{9,8},{10,11... | collective-permute-start | bytes 1572872 | tf_op jit(solution)/shard_map/ppermute | solution.py:531
  95.3 0.0 collective-permute-done.2
  95.3 0.0 collective-permute-done.4
  95.3 0.0 collective-permute-done
  95.3 0.3 maximum_add_fusion
  95.6 4.3 %gram_early.1 = (f32[16,128]{1,0:T(8,128)S(1)}, f32[8,32,8,128]{3,2,1,0:T(8,128)S(1)}) custom-call(f32[8,64,8,128]{3,2,1,0:T(8,128)S(1)} %bitcast.19, f32[8,64,8,128]{3,2,1,0:T(8,128)S(1)} %bitcast.23, f32[4,32,8,128]{3,2,1,0:T(8,128)S(1)} %bitcast.27, f32[4,32,8,128]{3,2,1,0:T(8,128)S(1)} %bitcast.30), custom_call_target="tpu_custom_call" | custom-call | tf_op jit(solution)/shard_map/gram_early/pallas_call | solution.py:542
  99.9 1.4 collective-permute-start.26
  101.3 6.5 %collective-permute-done.15 = f32[4,16,16,128]{3,2,1,0:T(8,128)S(1)} collective-permute-done((f32[4,16,16,128]{3,2,1,0:T(8,128)S(1)}, f32[4,16,16,128]{3,2,1,0:T(8,128)S(1)}, u32[]{:S(2)}, u32[]{:S(2)}) %collective-permute-start.15) | collective-permute-done | bytes 524320 | tf_op jit(solution)/shard_map/ppermute | solution.py:531
  107.8 7.7 %collective-permute-done.14 = f32[4,16,16,128]{3,2,1,0:T(8,128)S(1)} collective-permute-done((f32[4,16,16,128]{3,2,1,0:T(8,128)S(1)}, f32[4,16,16,128]{3,2,1,0:T(8,128)S(1)}, u32[]{:S(2)}, u32[]{:S(2)}) %collective-permute-start.14) | collective-permute-done | bytes 524320 | tf_op jit(solution)/shard_map/ppermute | solution.py:531
  115.5 2.2 %gram_late.1 = f32[16,128]{1,0:T(8,128)S(1)} custom-call(f32[8,64,8,128]{3,2,1,0:T(8,128)S(1)} %bitcast.20, f32[8,64,8,128]{3,2,1,0:T(8,128)S(1)} %bitcast.24, f32[4,32,8,128]{3,2,1,0:T(8,128)S(1)} %bitcast.28, f32[4,32,8,128]{3,2,1,0:T(8,128)S(1)} %bitcast.31, f32[4,32,8,128]{3,2,1,0:T(8,128)S(1)} %bitcast.43, f32[4,32,8,128]{3,2,1,0:T(8,128)S(1)} %bitcast.41, ...), custom_call_target="tpu_custom_call" | custom-call | tf_op jit(solution)/shard_map/gram_late/pallas_call | solution.py:542
  117.7 0.1 collective-permute-start.16
  117.8 1.2 collective-permute-done.16
  118.9 4.2 %collective-permute-start.17 = (f32[16,128]{1,0:T(8,128)S(1)}, f32[16,128]{1,0:T(8,128)S(1)}, u32[]{:S(2)}, u32[]{:S(2)}) collective-permute-start(f32[16,128]{1,0:T(8,128)S(1)} %add.34), channel_id=1, source_target_pairs={{0,64},{1,65},{2,66},{3,67},{4,68},{5,69},{6,70},{7,71},{8,72},{9,... | collective-permute-start | bytes 24584 | tf_op jit(solution)/shard_map/ppermute | solution.py:419
  123.2 5.2 %collective-permute-start.18 = (f32[16,128]{1,0:T(8,128)S(1)}, f32[16,128]{1,0:T(8,128)S(1)}, u32[]{:S(2)}, u32[]{:S(2)}) collective-permute-start(f32[16,128]{1,0:T(8,128)S(1)} %add.34), channel_id=1, source_target_pairs={{0,1},{1,0},{2,3},{3,2},{4,5},{5,4},{6,7},{7,6},{8,9},{9,8},{10,11... | collective-permute-start | bytes 24584 | tf_op jit(solution)/shard_map/ppermute | solution.py:419
  128.4 4.5 %collective-permute-done.17 = f32[16,128]{1,0:T(8,128)S(1)} collective-permute-done((f32[16,128]{1,0:T(8,128)S(1)}, f32[16,128]{1,0:T(8,128)S(1)}, u32[]{:S(2)}, u32[]{:S(2)}) %collective-permute-start.17) | collective-permute-done | bytes 8224 | tf_op jit(solution)/shard_map/ppermute | solution.py:419
  132.9 0.1 collective-permute-done.18
  133.0 0.0 collective-permute-start.20
  133.0 0.1 collective-permute-start.21
  133.1 2.6 %collective-permute-start.22 = (f32[16,128]{1,0:T(8,128)S(1)}, f32[16,128]{1,0:T(8,128)S(1)}, u32[]{:S(2)}, u32[]{:S(2)}) collective-permute-start(f32[16,128]{1,0:T(8,128)S(1)} %add_add_fusion.2), channel_id=1, source_target_pairs={{0,12},{2,14},{4,0},{6,2},{8,4},{10,6},{12,8},{14,10},{16,28},{18,... | collective-permute-start | bytes 24584 | tf_op jit(solution)/shard_map/ppermute | solution.py:408
  135.7 1.0 collective-permute-done.20
  136.7 0.5 collective-permute-done.21
  137.2 0.5 collective-permute-done.22
  137.7 6.1 %collective-permute-start.24 = (f32[16,128]{1,0:T(8,128)S(1)}, f32[16,128]{1,0:T(8,128)S(1)}, u32[]{:S(2)}, u32[]{:S(2)}) collective-permute-start(f32[16,128]{1,0:T(8,128)S(1)} %add_add_fusion.1), channel_id=1, source_target_pairs={{0,32},{2,34},{4,36},{6,38},{8,40},{10,42},{12,44},{14,46},{16,48}... | collective-permute-start | bytes 24584 | tf_op jit(solution)/shard_map/ppermute | solution.py:408
  143.8 1.6 %collective-permute-start.25 = (f32[16,128]{1,0:T(8,128)S(1)}, f32[16,128]{1,0:T(8,128)S(1)}, u32[]{:S(2)}, u32[]{:S(2)}) collective-permute-start(f32[16,128]{1,0:T(8,128)S(1)} %add_add_fusion.1), channel_id=1, source_target_pairs={{0,48},{2,50},{4,52},{6,54},{8,56},{10,58},{12,60},{14,62},{16,0},... | collective-permute-start | bytes 24584 | tf_op jit(solution)/shard_map/ppermute | solution.py:408
  145.4 0.9 collective-permute-done.25
  146.4 5.1 %algebra.1 = (f32[16,16]{1,0:T(8,128)}, f32[16,16]{1,0:T(8,128)}, f32[32,8,128]{2,1,0:T(8,128)S(1)}) custom-call(f32[16,128]{1,0:T(8,128)S(1)} %add_add_fusion.gram_ref), custom_call_target="tpu_custom_call" | custom-call | tf_op jit(solution)/shard_map/algebra/pallas_call | solution.py:559
  151.4 3.8 %combine_mine.1.refs_3_ = f32[8,64,8,128]{3,2,1,0:T(8,128)} custom-call(f32[32,8,128]{2,1,0:T(8,128)S(1)} %get-tuple-element.51.table_ref, f32[8,64,8,128]{3,2,1,0:T(8,128)S(1)} %bitcast.21, f32[8,64,8,128]{3,2,1,0:T(8,128)S(1)} %bitcast.25, f32[4,32,8,128]{3,2,1,0:T(8,128)S(1)} %bitcast.29, f32[4,32,8,128]{3,2,1,0:T(8,128)S(1)} %bitcast.32, ...), custom_call_target="tpu_custom_call" | custom-call | tf_op jit(solution)/shard_map/combine_mine/pallas_call | solution.py:571
  155.2 0.0 collective-permute-done.26.refs_2_
  155.3 3.8 %combine_theirs.1 = f32[8,64,8,128]{3,2,1,0:T(8,128)} custom-call(f32[32,8,128]{2,1,0:T(8,128)S(1)} %get-tuple-element.51.table_ref, f32[8,64,8,128]{3,2,1,0:T(8,128)S(1)} %bitcast.22, f32[8,64,8,128]{3,2,1,0:T(8,128)S(1)} %bitcast.26, f32[4,32,8,128]{3,2,1,0:T(8,128)S(1)} %bitcast.49, ...), custom_call_target="tpu_custom_call", output_to_operand_aliasing={{}: (6, {})} | custom-call | tf_op jit(solution)/shard_map/combine_theirs/pallas_call | solution.py:571
  (15 shorter events, 0.0 us)
Async XLA Ops:
  0.6 6.6 %copy-start.1 = (s32[8,32,16,128]{3,2,1,0:T(8,128)S(1)}, s32[8,32,16,128]{3,2,1,0:T(8,128)}, u32[]{:S(2)}) copy-start(s32[8,32,16,128]{3,2,1,0:T(8,128)} %param.3) | copy-start | bytes 6291460
  2.6 13.4 %collective-permute-start.5 = (f32[40,16,128]{2,1,0:T(8,128)}, f32[40,16,128]{2,1,0:T(8,128)S(1)}, u32[]{:S(2)}, u32[]{:S(2)}) collective-permute-start(f32[40,16,128]{2,1,0:T(8,128)} %tail.1), channel_id=1, source_target_pairs={{0,2},{2,4},{4,6},{6,8},{8,10},{10,12},{12,14},{14,16},{16,18},{18... | collective-permute-start | bytes 983048 | tf_op jit(solution)/shard_map/ppermute | solution.py:437
  7.4 8.6 %copy-start = (s32[12,32,16,128]{3,2,1,0:T(8,128)S(1)}, s32[12,32,16,128]{3,2,1,0:T(8,128)}, u32[]{:S(2)}) copy-start(s32[12,32,16,128]{3,2,1,0:T(8,128)} %levels_ref.5) | copy-start | bytes 9437188
  7.6 38.8 %collective-permute-start.1 = (f32[4,32,16,128]{3,2,1,0:T(8,128)S(1)}, f32[4,32,16,128]{3,2,1,0:T(8,128)S(1)}, u32[]{:S(2)}, u32[]{:S(2)}) collective-permute-start(f32[4,32,16,128]{3,2,1,0:T(8,128)S(1)} %get-tuple-element.53), channel_id=1, source_target_pairs={{0,17},{1,16},{2,7},{3,6},{124,77},{125,76},{126,115},{127,114}} | collective-permute-start | bytes 3145736 | tf_op jit(solution)/shard_map/ppermute | solution.py:461
  14.4 35.6 %collective-permute-start.3 = (f32[4,32,16,128]{3,2,1,0:T(8,128)S(1)}, f32[4,32,16,128]{3,2,1,0:T(8,128)S(1)}, u32[]{:S(2)}, u32[]{:S(2)}) collective-permute-start(f32[4,32,16,128]{3,2,1,0:T(8,128)S(1)} %get-tuple-element.54), channel_id=1, source_target_pairs={{0,49},{1,48},{2,15},{3,14},{124,109},{125,108},{126,123},{127,122}} | collective-permute-start | bytes 3145736 | tf_op jit(solution)/shard_map/ppermute | solution.py:461
  17.5 18.0 %collective-permute-start.6 = (f32[4,27,16,128]{3,2,1,0:T(8,128)S(1)}, f32[4,27,16,128]{3,2,1,0:T(8,128)S(1)}, u32[]{:S(2)}, u32[]{:S(2)}) collective-permute-start(f32[4,27,16,128]{3,2,1,0:T(8,128)S(1)} %get-tuple-element.29), channel_id=1, source_target_pairs={{0,2},{2,4},{4,6},{6,8},{8,10},{10,12},{12,14},{14,16},{16,18},{18... | collective-permute-start | bytes 2654216 | tf_op jit(solution)/shard_map/ppermute | solution.py:437
  19.4 20.5 %collective-permute-start.7 = (f32[4,27,16,128]{3,2,1,0:T(8,128)S(1)}, f32[4,27,16,128]{3,2,1,0:T(8,128)S(1)}, u32[]{:S(2)}, u32[]{:S(2)}) collective-permute-start(f32[4,27,16,128]{3,2,1,0:T(8,128)S(1)} %get-tuple-element.30), channel_id=1, source_target_pairs={{2,0},{4,2},{6,4},{8,6},{10,8},{12,10},{14,12},{16,14},{18,16},{20... | collective-permute-start | bytes 2654216 | tf_op jit(solution)/shard_map/ppermute | solution.py:440
  21.9 73.4 %collective-permute-start = (f32[8,32,16,128]{3,2,1,0:T(8,128)S(1)}, f32[8,32,16,128]{3,2,1,0:T(8,128)S(1)}, u32[]{:S(2)}, u32[]{:S(2)}) collective-permute-start(f32[8,32,16,128]{3,2,1,0:T(8,128)S(1)} %convert_element_type.3.start_ref.own_ref), channel_id=1, source_target_pairs={{4,5},{5,4},{6,7},{7,6},{8,9},{9,8},{10,11},{11,10},{12,13},{13,12... | collective-permute-start | bytes 6291464 | tf_op jit(solution)/shard_map/ppermute | solution.py:463
  35.5 16.4 %collective-permute-start.8 = (f32[4,27,16,128]{3,2,1,0:T(8,128)S(1)}, f32[4,27,16,128]{3,2,1,0:T(8,128)S(1)}, u32[]{:S(2)}, u32[]{:S(2)}) collective-permute-start(f32[4,27,16,128]{3,2,1,0:T(8,128)S(1)} %get-tuple-element.32), channel_id=1, source_target_pairs={{0,2},{2,4},{4,6},{6,8},{8,10},{10,12},{12,14},{14,16},{16,18},{18... | collective-permute-start | bytes 2654216 | tf_op jit(solution)/shard_map/ppermute | solution.py:437
  39.9 14.4 %collective-permute-start.9 = (f32[4,27,16,128]{3,2,1,0:T(8,128)S(1)}, f32[4,27,16,128]{3,2,1,0:T(8,128)S(1)}, u32[]{:S(2)}, u32[]{:S(2)}) collective-permute-start(f32[4,27,16,128]{3,2,1,0:T(8,128)S(1)} %get-tuple-element.33), channel_id=1, source_target_pairs={{2,0},{4,2},{6,4},{8,6},{10,8},{12,10},{14,12},{16,14},{18,16},{20... | collective-permute-start | bytes 2654216 | tf_op jit(solution)/shard_map/ppermute | solution.py:440
  46.4 13.6 %collective-permute-start.10 = (f32[4,27,16,128]{3,2,1,0:T(8,128)S(1)}, f32[4,27,16,128]{3,2,1,0:T(8,128)S(1)}, u32[]{:S(2)}, u32[]{:S(2)}) collective-permute-start(f32[4,27,16,128]{3,2,1,0:T(8,128)S(1)} %get-tuple-element.36), channel_id=1, source_target_pairs={{0,2},{2,4},{4,6},{6,8},{8,10},{10,12},{12,14},{14,16},{16,18},{18... | collective-permute-start | bytes 2654216 | tf_op jit(solution)/shard_map/ppermute | solution.py:437
  50.0 22.8 %collective-permute-start.11 = (f32[4,27,16,128]{3,2,1,0:T(8,128)S(1)}, f32[4,27,16,128]{3,2,1,0:T(8,128)S(1)}, u32[]{:S(2)}, u32[]{:S(2)}) collective-permute-start(f32[4,27,16,128]{3,2,1,0:T(8,128)S(1)} %get-tuple-element.37), channel_id=1, source_target_pairs={{2,0},{4,2},{6,4},{8,6},{10,8},{12,10},{14,12},{16,14},{18,16},{20... | collective-permute-start | bytes 2654216 | tf_op jit(solution)/shard_map/ppermute | solution.py:440
  52.0 43.3 %collective-permute-start.2 = (f32[4,32,16,128]{3,2,1,0:T(8,128)S(1)}, f32[4,32,16,128]{3,2,1,0:T(8,128)S(1)}, u32[]{:S(2)}, u32[]{:S(2)}) collective-permute-start(f32[4,32,16,128]{3,2,1,0:T(8,128)S(1)} %collective-permute-done.1), channel_id=1, source_target_pairs={{17,1},{16,0},{7,3},{6,2},{77,125},{76,124},{115,127},{114,126}} | collective-permute-start | bytes 3145736 | tf_op jit(solution)/shard_map/ppermute | solution.py:462
  54.3 41.0 %collective-permute-start.4 = (f32[4,32,16,128]{3,2,1,0:T(8,128)S(1)}, f32[4,32,16,128]{3,2,1,0:T(8,128)S(1)}, u32[]{:S(2)}, u32[]{:S(2)}) collective-permute-start(f32[4,32,16,128]{3,2,1,0:T(8,128)S(1)} %collective-permute-done.3), channel_id=1, source_target_pairs={{49,1},{48,0},{15,3},{14,2},{109,125},{108,124},{123,127},{122,126}} | collective-permute-start | bytes 3145736 | tf_op jit(solution)/shard_map/ppermute | solution.py:462
  60.0 16.3 %collective-permute-start.12 = (f32[4,27,16,128]{3,2,1,0:T(8,128)S(1)}, f32[4,27,16,128]{3,2,1,0:T(8,128)S(1)}, u32[]{:S(2)}, u32[]{:S(2)}) collective-permute-start(f32[4,27,16,128]{3,2,1,0:T(8,128)S(1)} %get-tuple-element.40), channel_id=1, source_target_pairs={{0,2},{2,4},{4,6},{6,8},{8,10},{10,12},{12,14},{14,16},{16,18},{18... | collective-permute-start | bytes 2654216 | tf_op jit(solution)/shard_map/ppermute | solution.py:437
  72.8 14.6 %collective-permute-start.13 = (f32[4,27,16,128]{3,2,1,0:T(8,128)S(1)}, f32[4,27,16,128]{3,2,1,0:T(8,128)S(1)}, u32[]{:S(2)}, u32[]{:S(2)}) collective-permute-start(f32[4,27,16,128]{3,2,1,0:T(8,128)S(1)} %get-tuple-element.41), channel_id=1, source_target_pairs={{2,0},{4,2},{6,4},{8,6},{10,8},{12,10},{14,12},{16,14},{18,16},{20... | collective-permute-start | bytes 2654216 | tf_op jit(solution)/shard_map/ppermute | solution.py:440
  92.3 15.5 %collective-permute-start.15 = (f32[4,16,16,128]{3,2,1,0:T(8,128)S(1)}, f32[4,16,16,128]{3,2,1,0:T(8,128)S(1)}, u32[]{:S(2)}, u32[]{:S(2)}) collective-permute-start(f32[4,16,16,128]{3,2,1,0:T(8,128)S(1)} %get-tuple-element.47), channel_id=1, source_target_pairs={{0,1},{1,0},{2,3},{3,2},{4,5},{5,4},{6,7},{7,6},{8,9},{9,8},{10,11... | collective-permute-start | bytes 1572872 | tf_op jit(solution)/shard_map/ppermute | solution.py:531
  92.5 23.0 %collective-permute-start.14 = (f32[4,16,16,128]{3,2,1,0:T(8,128)S(1)}, f32[4,16,16,128]{3,2,1,0:T(8,128)S(1)}, u32[]{:S(2)}, u32[]{:S(2)}) collective-permute-start(f32[4,16,16,128]{3,2,1,0:T(8,128)S(1)} %get-tuple-element.46), channel_id=1, source_target_pairs={{0,1},{1,0},{2,3},{3,2},{4,5},{5,4},{6,7},{7,6},{8,9},{9,8},{10,11... | collective-permute-start | bytes 1572872 | tf_op jit(solution)/shard_map/ppermute | solution.py:531
  99.9 55.3 %collective-permute-start.26 = (f32[8,32,8,128]{3,2,1,0:T(8,128)S(1)}, f32[8,32,8,128]{3,2,1,0:T(8,128)S(1)}, u32[]{:S(2)}, u32[]{:S(2)}) collective-permute-start(f32[8,32,8,128]{3,2,1,0:T(8,128)S(1)} %get-tuple-element.52), channel_id=1, source_target_pairs={{0,1},{2,3},{4,5},{6,7},{8,9},{10,11},{12,13},{14,15},{16,17},{18,... | collective-permute-start | bytes 3145736 | tf_op jit(solution)/shard_map/ppermute | solution.py:554
  117.7 1.3 collective-permute-start.16
  118.9 13.9 %collective-permute-start.17 = (f32[16,128]{1,0:T(8,128)S(1)}, f32[16,128]{1,0:T(8,128)S(1)}, u32[]{:S(2)}, u32[]{:S(2)}) collective-permute-start(f32[16,128]{1,0:T(8,128)S(1)} %add.34), channel_id=1, source_target_pairs={{0,64},{1,65},{2,66},{3,67},{4,68},{5,69},{6,70},{7,71},{8,72},{9,... | collective-permute-start | bytes 24584 | tf_op jit(solution)/shard_map/ppermute | solution.py:419
  123.2 9.8 %collective-permute-start.18 = (f32[16,128]{1,0:T(8,128)S(1)}, f32[16,128]{1,0:T(8,128)S(1)}, u32[]{:S(2)}, u32[]{:S(2)}) collective-permute-start(f32[16,128]{1,0:T(8,128)S(1)} %add.34), channel_id=1, source_target_pairs={{0,1},{1,0},{2,3},{3,2},{4,5},{5,4},{6,7},{7,6},{8,9},{9,8},{10,11... | collective-permute-start | bytes 24584 | tf_op jit(solution)/shard_map/ppermute | solution.py:419
  128.4 4.6 %collective-permute-start.19 = (f32[16,128]{1,0:T(8,128)S(1)}, f32[16,128]{1,0:T(8,128)S(1)}, u32[]{:S(2)}, u32[]{:S(2)}) collective-permute-start(f32[16,128]{1,0:T(8,128)S(1)} %add.34), channel_id=1, source_target_pairs={{0,65},{1,64},{2,67},{3,66},{4,69},{5,68},{6,71},{7,70},{8,73},{9,... | collective-permute-start | bytes 24584 | tf_op jit(solution)/shard_map/ppermute | solution.py:419
  133.0 3.8 %collective-permute-start.20 = (f32[16,128]{1,0:T(8,128)S(1)}, f32[16,128]{1,0:T(8,128)S(1)}, u32[]{:S(2)}, u32[]{:S(2)}) collective-permute-start(f32[16,128]{1,0:T(8,128)S(1)} %add_add_fusion.2), channel_id=1, source_target_pairs={{0,4},{2,6},{4,8},{6,10},{8,12},{10,14},{12,0},{14,2},{16,20},{18,... | collective-permute-start | bytes 24584 | tf_op jit(solution)/shard_map/ppermute | solution.py:408
  133.0 4.2 %collective-permute-start.21 = (f32[16,128]{1,0:T(8,128)S(1)}, f32[16,128]{1,0:T(8,128)S(1)}, u32[]{:S(2)}, u32[]{:S(2)}) collective-permute-start(f32[16,128]{1,0:T(8,128)S(1)} %add_add_fusion.2), channel_id=1, source_target_pairs={{0,8},{2,10},{4,12},{6,14},{8,0},{10,2},{12,4},{14,6},{16,24},{18,... | collective-permute-start | bytes 24584 | tf_op jit(solution)/shard_map/ppermute | solution.py:408
  133.1 4.6 %collective-permute-start.22 = (f32[16,128]{1,0:T(8,128)S(1)}, f32[16,128]{1,0:T(8,128)S(1)}, u32[]{:S(2)}, u32[]{:S(2)}) collective-permute-start(f32[16,128]{1,0:T(8,128)S(1)} %add_add_fusion.2), channel_id=1, source_target_pairs={{0,12},{2,14},{4,0},{6,2},{8,4},{10,6},{12,8},{14,10},{16,28},{18,... | collective-permute-start | bytes 24584 | tf_op jit(solution)/shard_map/ppermute | solution.py:408
  137.7 7.7 %collective-permute-start.23 = (f32[16,128]{1,0:T(8,128)S(1)}, f32[16,128]{1,0:T(8,128)S(1)}, u32[]{:S(2)}, u32[]{:S(2)}) collective-permute-start(f32[16,128]{1,0:T(8,128)S(1)} %add_add_fusion.1), channel_id=1, source_target_pairs={{0,16},{2,18},{4,20},{6,22},{8,24},{10,26},{12,28},{14,30},{16,32}... | collective-permute-start | bytes 24584 | tf_op jit(solution)/shard_map/ppermute | solution.py:408
  137.7 7.7 %collective-permute-start.24 = (f32[16,128]{1,0:T(8,128)S(1)}, f32[16,128]{1,0:T(8,128)S(1)}, u32[]{:S(2)}, u32[]{:S(2)}) collective-permute-start(f32[16,128]{1,0:T(8,128)S(1)} %add_add_fusion.1), channel_id=1, source_target_pairs={{0,32},{2,34},{4,36},{6,38},{8,40},{10,42},{12,44},{14,46},{16,48}... | collective-permute-start | bytes 24584 | tf_op jit(solution)/shard_map/ppermute | solution.py:408
  143.8 2.6 %collective-permute-start.25 = (f32[16,128]{1,0:T(8,128)S(1)}, f32[16,128]{1,0:T(8,128)S(1)}, u32[]{:S(2)}, u32[]{:S(2)}) collective-permute-start(f32[16,128]{1,0:T(8,128)S(1)} %add_add_fusion.1), channel_id=1, source_target_pairs={{0,48},{2,50},{4,52},{6,54},{8,56},{10,58},{12,60},{14,62},{16,0},... | collective-permute-start | bytes 24584 | tf_op jit(solution)/shard_map/ppermute | solution.py:408

commit v4 on v3

--- a/solution.py
+++ b/solution.py
@@ -250,7 +250,6 @@
             if early:
                 block_of_pairs(0, "x", left, "x", right)
             if (right < 2) == early:
-                block_of_pairs(2, "y", left, "y", right)
                 if left // 2 == right // 2:
                     block_of_pairs(1, "y", left, "x", right)
             if left // 2 != right // 2:
@@ -269,7 +268,7 @@
     lane = lax.broadcasted_iota(jnp.int32, (256, 128), 1)
     inner = lax.rem(lax.broadcasted_iota(jnp.int32, (256, 128), 0), 16)
     total = jnp.zeros((16, 128), f32) if early else before_ref[...]
-    for slot in range(0 if early else 1, 3):
+    for slot in range(0 if early else 1, 2):
         sums = jnp.sum(acc_ref[slot], axis=1, keepdims=True)
         placed = jnp.where(lane == inner + 16 * slot, sums, 0.0)
         total = total + jnp.sum(placed.reshape(16, 16, 128), axis=1)
@@ -305,18 +304,68 @@
     return lax.dot_general(a, b, (((1,), (1,)), ((), ())), precision=highest, preferred_element_type=f32)
 
 
-def algebra_kernel(scale, gram_ref, alpha_ref, beta_ref, table_ref):
+def project_kernel(gram_ref, alpha_ref, inverse_ref, mix_ref, table_ref):
     size = gram_ref.shape[0]
     _, inverse = eliminate(gram_ref[:, :size])
-    half_way = times(inverse, gram_ref[...])
-    both = jnp.concatenate([half_way[:, size : 2 * size], half_way[:, 2 * size : 3 * size]], axis=0)
-    both = times_t(both, inverse)
-    coeffs, image = both[:size], both[size:]
-    factor, second = eliminate(image - times_t(coeffs, coeffs))
-    alpha_ref[...] = coeffs
+    image = gram_ref[:, size : 2 * size]
+    right = times_t(image, inverse)
+    alpha_ref[...] = times(inverse, right)
+    inverse_ref[...] = inverse
+    mix = times(right, inverse)
+    mix_ref[...] = mix
+    first = lax.axis_index("vec") == 0
+    rows = jnp.where(first, mix, jnp.concatenate([mix[8:], mix[:8]], axis=0))
+    for j in range(size):
+        column = jnp.where(first, rows[:, j : j + 1], rows[:, (j + 8) % size : (j + 8) % size + 1])
+        table_ref[j] = jnp.broadcast_to(column, table_ref.shape[1:])
+
+
+def residual_kernel(table_ref, own_x_ref, other_x_ref, *refs):
+    ys, (out_ref, rest_ref, acc_ref) = refs[:4], refs[4:]
+    cols = own_x_ref.shape[0]
+    tiles = rest_ref.shape[1]
+    group = 8
+    vec = lax.axis_index("vec")
+    xs = [(ref, k) for ref in (own_x_ref, other_x_ref) for k in range(cols)]
+
+    def subtract(g, _):
+        first = pl.multiple_of(g * group, group)
+        for i in range(2 * cols):
+            acc = ys[i // chunk][i % chunk, pl.ds(first, group)]
+            for j, (ref, k) in enumerate(xs):
+                factor = jnp.broadcast_to(table_ref[j, pl.ds(i, 1)], (8, 128))
+                acc = acc - factor[None] * ref[k, pl.ds(vec * tiles + first, group)]
+            rest_ref[i, pl.ds(first, group)] = acc
+        return 0
+
+    lax.fori_loop(0, tiles // group, subtract, 0)
+    for left in range(0, 2 * cols, chunk):
+        for right in range(left, 2 * cols, chunk):
+            pairs = [(i, j) for i in range(left, left + chunk) for j in range(right, right + chunk) if i <= j]
+
+            def step(t, accs, pairs=pairs, left=left, right=right):
+                a = {i: rest_ref[i, t] for i in sorted({*range(left, left + chunk), *range(right, right + chunk)})}
+                return tuple(acc + a[i] * a[j] for (i, j), acc in zip(pairs, accs))
+
+            accs = lax.fori_loop(0, tiles, step, tuple(jnp.zeros((8, 128), f32) for _ in pairs), unroll=4)
+            for (i, j), acc in zip(pairs, accs):
+                row = jnp.sum(acc, axis=0, keepdims=True)
+                gi = lax.rem(i + cols * vec, 2 * cols)
+                gj = lax.rem(j + cols * vec, 2 * cols)
+                acc_ref[pl.ds(gi * 16 + gj, 1), :] = row
+                acc_ref[pl.ds(gj * 16 + gi, 1), :] = row
+    lane = lax.broadcasted_iota(jnp.int32, (256, 128), 1)
+    inner = lax.rem(lax.broadcasted_iota(jnp.int32, (256, 128), 0), 16)
+    sums = jnp.sum(acc_ref[...], axis=1, keepdims=True)
+    out_ref[...] = jnp.sum(jnp.where(lane == inner, sums, 0.0).reshape(16, 16, 128), axis=1)
+
+
+def algebra_kernel(scale, gram_ref, inverse_ref, mix_ref, beta_ref, table_ref):
+    inverse = inverse_ref[...]
+    factor, second = eliminate(times_t(times(inverse, gram_ref[:, :16]), inverse))
     beta_ref[...] = factor
-    both = times(jnp.concatenate([times(second, coeffs), second], axis=0), inverse)
-    of_start, of_image = -scale * both[:size], scale * both[size:]
+    of_image = scale * times(second, inverse)
+    of_start = -times(of_image, mix_ref[...])
     first = lax.axis_index("vec") == 0
     for place, mix in ((0, of_start), (16, of_image)):
         mine = jnp.where(first, mix[:8], mix[8:])
@@ -544,7 +593,7 @@
             out_shape=(out, late) if early else out,
             in_specs=[VMEM] * len(operands),
             out_specs=(VMEM, VMEM) if early else VMEM,
-            scratch_shapes=[pltpu.VMEM((3, 256, 128), f32)],
+            scratch_shapes=[pltpu.VMEM((2, 256, 128), f32)],
             compiler_params=params(4),
             name="gram_early" if early else "gram_late",
         )(*operands)
@@ -556,14 +605,35 @@
     gram = sum_everywhere(gram)
 
     small = jax.ShapeDtypeStruct((16, 16), f32)
-    alpha, beta, table = pl.pallas_call(
+    alpha, inverse, mix, project = pl.pallas_call(
+        project_kernel,
+        out_shape=[small, small, small, jax.ShapeDtypeStruct((2 * own_cols, 2 * own_cols, lanes), f32)],
+        in_specs=[VMEM],
+        out_specs=[VMEM] * 4,
+        compiler_params=params(4),
+        name="project",
+    )(gram)
+    rest_gram = pl.pallas_call(
+        residual_kernel,
+        out_shape=jax.ShapeDtypeStruct((2 * own_cols, 128), f32),
+        in_specs=[VMEM] * 7,
+        out_specs=VMEM,
+        scratch_shapes=[
+            pltpu.VMEM((2 * own_cols, halves * rows // 8, 8, lanes), f32),
+            pltpu.VMEM((256, 128), f32),
+        ],
+        compiler_params=params(6),
+        name="residual",
+    )(project, *mine_tiled, *map(tiled, y_other_mine))
+    rest_gram = sum_everywhere(rest_gram)
+    beta, table = pl.pallas_call(
         functools.partial(algebra_kernel, math.sqrt(voxel_total)),
-        out_shape=[small, small, jax.ShapeDtypeStruct((4 * own_cols, own_cols, lanes), f32)],
-        in_specs=[VMEM],
-        out_specs=[VMEM] * 3,
+        out_shape=[small, jax.ShapeDtypeStruct((4 * own_cols, own_cols, lanes), f32)],
+        in_specs=[VMEM] * 3,
+        out_specs=[VMEM] * 2,
         compiler_params=params(4),
         name="algebra",
-    )(gram)
+    )(rest_gram, inverse, mix)
 
     def combine(mine, *fields, before=None):
         half_tiles = halves * rows // 8

time: 162 us -> 182 us (1.12)
  the two profiles are of different devices: /device:TPU:1 before, /device:TPU:24 now
where the time goes in v4:
time: 182 us
  starting transfers between devices  76.8 us (42%)
  waiting for transfers between devices  65.2 us (36%)
  Pallas kernels  38 us (21%)
    ppermute x14, starting transfers between devices, permute(): lax.ppermute(v, 'brick', [(place[0], moved(place, dim, by)) for place in...  21.4 us
    ppermute x2, waiting for transfers between devices, steps_of(): y_other_mine.append(lax.ppermute(theirs, 'vec', swap))  18.5 us
    ppermute x5, starting transfers between devices, up(): return lax.ppermute(value, 'brick', upward)  17.4 us
    ppermute x14, waiting for transfers between devices, permute(): lax.ppermute(v, 'brick', [(place[0], moved(place, dim, by)) for place in...  13.7 us
    ppermute x5, waiting for transfers between devices, up(): return lax.ppermute(value, 'brick', upward)  13.4 us
    ppermute x6, starting transfers between devices, sum_everywhere(): lax.ppermute(value, ('brick', 'vec'), pairs[by])  11.2 us
    ppermute x4, starting transfers between devices, down(): return lax.ppermute(value, 'brick', downward)  10.7 us
    ppermute x4, waiting for transfers between devices, down(): return lax.ppermute(value, 'brick', downward)  8.13 us
  transfers between devices with their start and end apart: 37, of which 24 were waited for; matrix products, arithmetic and copies ran while one was open for 0% of the time, Pallas kernels for 17%

profile of v4, /device:TPU:24, one launch (start us, length us, event | category | flops | bytes accessed | tf_op | source)
XLA Modules:
  0.0 181.8 jit_solution(6065051946946972734)
XLA Ops:
  0.6 1.9 %tail.1 = f32[40,16,128]{2,1,0:T(8,128)} custom-call(s32[12,32,16,128]{3,2,1,0:T(8,128)} %levels_ref.5), custom_call_target="tpu_custom_call" | custom-call | tf_op jit(solution)/shard_map/tail/pallas_call | solution.py:491
  2.6 2.2 %collective-permute-start.5 = (f32[40,16,128]{2,1,0:T(8,128)}, f32[40,16,128]{2,1,0:T(8,128)S(1)}, u32[]{:S(2)}, u32[]{:S(2)}) collective-permute-start(f32[40,16,128]{2,1,0:T(8,128)} %tail.1), channel_id=1, source_target_pairs={{0,2},{2,4},{4,6},{6,8},{8,10},{10,12},{12,14},{14,16},{16,18},{18... | collective-permute-start | bytes 983048 | tf_op jit(solution)/shard_map/ppermute | solution.py:486
  5.0 6.5 %collective-permute-done.5.halo_ref = f32[40,16,128]{2,1,0:T(8,128)S(1)} collective-permute-done((f32[40,16,128]{2,1,0:T(8,128)}, f32[40,16,128]{2,1,0:T(8,128)S(1)}, u32[]{:S(2)}, u32[]{:S(2)}) %collective-permute-start.5) | collective-permute-done | bytes 327712 | tf_op jit(solution)/shard_map/ppermute | solution.py:486
  11.5 1.4 degree.1
  12.9 1.9 %collective-permute-start.6 = (f32[4,27,16,128]{3,2,1,0:T(8,128)S(1)}, f32[4,27,16,128]{3,2,1,0:T(8,128)S(1)}, u32[]{:S(2)}, u32[]{:S(2)}) collective-permute-start(f32[4,27,16,128]{3,2,1,0:T(8,128)S(1)} %get-tuple-element.32), channel_id=1, source_target_pairs={{0,2},{2,4},{4,6},{6,8},{8,10},{10,12},{12,14},{14,16},{16,18},{18... | collective-permute-start | bytes 2654216 | tf_op jit(solution)/shard_map/ppermute | solution.py:486
  14.8 3.6 %collective-permute-start.7 = (f32[4,27,16,128]{3,2,1,0:T(8,128)S(1)}, f32[4,27,16,128]{3,2,1,0:T(8,128)S(1)}, u32[]{:S(2)}, u32[]{:S(2)}) collective-permute-start(f32[4,27,16,128]{3,2,1,0:T(8,128)S(1)} %get-tuple-element.33), channel_id=1, source_target_pairs={{2,0},{4,2},{6,4},{8,6},{10,8},{12,10},{14,12},{16,14},{18,16},{20... | collective-permute-start | bytes 2654216 | tf_op jit(solution)/shard_map/ppermute | solution.py:489
  18.5 3.5 %collective-permute-start.8 = (f32[4,27,16,128]{3,2,1,0:T(8,128)S(1)}, f32[4,27,16,128]{3,2,1,0:T(8,128)S(1)}, u32[]{:S(2)}, u32[]{:S(2)}) collective-permute-start(f32[4,27,16,128]{3,2,1,0:T(8,128)S(1)} %get-tuple-element.35), channel_id=1, source_target_pairs={{0,2},{2,4},{4,6},{6,8},{8,10},{10,12},{12,14},{14,16},{16,18},{18... | collective-permute-start | bytes 2654216 | tf_op jit(solution)/shard_map/ppermute | solution.py:486
  22.1 2.0 %collective-permute-start.9 = (f32[4,27,16,128]{3,2,1,0:T(8,128)S(1)}, f32[4,27,16,128]{3,2,1,0:T(8,128)S(1)}, u32[]{:S(2)}, u32[]{:S(2)}) collective-permute-start(f32[4,27,16,128]{3,2,1,0:T(8,128)S(1)} %get-tuple-element.36), channel_id=1, source_target_pairs={{2,0},{4,2},{6,4},{8,6},{10,8},{12,10},{14,12},{16,14},{18,16},{20... | collective-permute-start | bytes 2654216 | tf_op jit(solution)/shard_map/ppermute | solution.py:489
  24.2 0.7 collective-permute-start.1
  25.0 2.3 %collective-permute-done.6 = f32[4,27,16,128]{3,2,1,0:T(8,128)S(1)} collective-permute-done((f32[4,27,16,128]{3,2,1,0:T(8,128)S(1)}, f32[4,27,16,128]{3,2,1,0:T(8,128)S(1)}, u32[]{:S(2)}, u32[]{:S(2)}) %collective-permute-start.6) | collective-permute-done | bytes 884768 | tf_op jit(solution)/shard_map/ppermute | solution.py:486
  28.0 1.0 collective-permute-done.7
  29.0 5.8 %collective-permute-start = (f32[8,32,16,128]{3,2,1,0:T(8,128)S(1)}, f32[8,32,16,128]{3,2,1,0:T(8,128)S(1)}, u32[]{:S(2)}, u32[]{:S(2)}) collective-permute-start(f32[8,32,16,128]{3,2,1,0:T(8,128)S(1)} %convert_element_type.3.start_ref.own_ref), channel_id=1, source_target_pairs={{4,5},{5,4},{6,7},{7,6},{8,9},{9,8},{10,11},{11,10},{12,13},{13,12... | collective-permute-start | bytes 6291464 | tf_op jit(solution)/shard_map/ppermute | solution.py:512
  34.8 1.4 weights.1.weight_ref
  36.2 3.1 %shard_map.49 = (f32[4,32,16,128]{3,2,1,0:T(8,128)S(1)}, f32[4,27,16,128]{3,2,1,0:T(8,128)S(1)}, f32[4,27,16,128]{3,2,1,0:T(8,128)S(1)}, f32[22,32,16,128]{3,2,1,0:T(8,128)S(1)}) custom-call(f32[22,32,16,128]{3,2,1,0:T(8,128)S(1)} %weights.1.weight_ref, f32[32,16,128]{2,1,0:T(8,128)S(1)} %get-tuple-element.31.root_ref, ...), custom_call_target="tpu_custom_call", output_to_operand_aliasing={{3}: (0, {})} | custom-call | tf_op jit(solution)/shard_map/pallas_call | solution.py:549
  39.3 7.4 %collective-permute-start.10 = (f32[4,27,16,128]{3,2,1,0:T(8,128)S(1)}, f32[4,27,16,128]{3,2,1,0:T(8,128)S(1)}, u32[]{:S(2)}, u32[]{:S(2)}) collective-permute-start(f32[4,27,16,128]{3,2,1,0:T(8,128)S(1)} %get-tuple-element.39), channel_id=1, source_target_pairs={{0,2},{2,4},{4,6},{6,8},{8,10},{10,12},{12,14},{14,16},{16,18},{18... | collective-permute-start | bytes 2654216 | tf_op jit(solution)/shard_map/ppermute | solution.py:486
  46.7 1.9 %collective-permute-start.11 = (f32[4,27,16,128]{3,2,1,0:T(8,128)S(1)}, f32[4,27,16,128]{3,2,1,0:T(8,128)S(1)}, u32[]{:S(2)}, u32[]{:S(2)}) collective-permute-start(f32[4,27,16,128]{3,2,1,0:T(8,128)S(1)} %get-tuple-element.40), channel_id=1, source_target_pairs={{2,0},{4,2},{6,4},{8,6},{10,8},{12,10},{14,12},{16,14},{18,16},{20... | collective-permute-start | bytes 2654216 | tf_op jit(solution)/shard_map/ppermute | solution.py:489
  48.6 3.1 %shard_map.50 = (f32[4,32,16,128]{3,2,1,0:T(8,128)S(1)}, f32[4,27,16,128]{3,2,1,0:T(8,128)S(1)}, f32[4,27,16,128]{3,2,1,0:T(8,128)S(1)}, f32[22,32,16,128]{3,2,1,0:T(8,128)S(1)}) custom-call(f32[22,32,16,128]{3,2,1,0:T(8,128)S(1)} %get-tuple-element.34.weight_ref, f32[32,16,128]{2,1,0:T(8,128)S(1)} %get-tuple-element.31.root_ref, ...), custom_call_target="tpu_custom_call", output_to_operand_aliasing={{3}: (0, {})} | custom-call | tf_op jit(solution)/shard_map/pallas_call | solution.py:549
  51.8 2.4 %collective-permute-start.12 = (f32[4,27,16,128]{3,2,1,0:T(8,128)S(1)}, f32[4,27,16,128]{3,2,1,0:T(8,128)S(1)}, u32[]{:S(2)}, u32[]{:S(2)}) collective-permute-start(f32[4,27,16,128]{3,2,1,0:T(8,128)S(1)} %get-tuple-element.43), channel_id=1, source_target_pairs={{0,2},{2,4},{4,6},{6,8},{8,10},{10,12},{12,14},{14,16},{16,18},{18... | collective-permute-start | bytes 2654216 | tf_op jit(solution)/shard_map/ppermute | solution.py:486
  54.2 3.1 %collective-permute-start.13 = (f32[4,27,16,128]{3,2,1,0:T(8,128)S(1)}, f32[4,27,16,128]{3,2,1,0:T(8,128)S(1)}, u32[]{:S(2)}, u32[]{:S(2)}) collective-permute-start(f32[4,27,16,128]{3,2,1,0:T(8,128)S(1)} %get-tuple-element.44), channel_id=1, source_target_pairs={{2,0},{4,2},{6,4},{8,6},{10,8},{12,10},{14,12},{16,14},{18,16},{20... | collective-permute-start | bytes 2654216 | tf_op jit(solution)/shard_map/ppermute | solution.py:489
  57.4 0.7 collective-permute-start.2
  58.1 1.1 collective-permute-done.11
  59.9 1.6 shard_map.51
  61.5 4.6 %collective-permute-done.12 = f32[4,27,16,128]{3,2,1,0:T(8,128)S(1)} collective-permute-done((f32[4,27,16,128]{3,2,1,0:T(8,128)S(1)}, f32[4,27,16,128]{3,2,1,0:T(8,128)S(1)}, u32[]{:S(2)}, u32[]{:S(2)}) %collective-permute-start.12) | collective-permute-done | bytes 884768 | tf_op jit(solution)/shard_map/ppermute | solution.py:486
  66.1 6.0 %collective-permute-done.13 = f32[4,27,16,128]{3,2,1,0:T(8,128)S(1)} collective-permute-done((f32[4,27,16,128]{3,2,1,0:T(8,128)S(1)}, f32[4,27,16,128]{3,2,1,0:T(8,128)S(1)}, u32[]{:S(2)}, u32[]{:S(2)}) %collective-permute-start.13) | collective-permute-done | bytes 884768 | tf_op jit(solution)/shard_map/ppermute | solution.py:489
  72.1 1.6 shard_map.52
  73.8 3.5 %collective-permute-start.14 = (f32[4,16,16,128]{3,2,1,0:T(8,128)S(1)}, f32[4,16,16,128]{3,2,1,0:T(8,128)S(1)}, u32[]{:S(2)}, u32[]{:S(2)}) collective-permute-start(f32[4,16,16,128]{3,2,1,0:T(8,128)S(1)} %get-tuple-element.49), channel_id=1, source_target_pairs={{0,1},{1,0},{2,3},{3,2},{4,5},{5,4},{6,7},{7,6},{8,9},{9,8},{10,11... | collective-permute-start | bytes 1572872 | tf_op jit(solution)/shard_map/ppermute | solution.py:580
  77.4 1.6 shard_map.53
  79.0 1.6 shard_map.54
  80.6 7.0 %collective-permute-done = f32[8,32,16,128]{3,2,1,0:T(8,128)S(1)} collective-permute-done((f32[8,32,16,128]{3,2,1,0:T(8,128)S(1)}, f32[8,32,16,128]{3,2,1,0:T(8,128)S(1)}, u32[]{:S(2)}, u32[]{:S(2)}) %collective-permute-start) | collective-permute-done | bytes 2097184 | tf_op jit(solution)/shard_map/ppermute | solution.py:512
  87.8 3.7 %gram_early.1 = (f32[16,128]{1,0:T(8,128)S(1)}, f32[8,32,8,128]{3,2,1,0:T(8,128)S(1)}) custom-call(f32[8,64,8,128]{3,2,1,0:T(8,128)S(1)} %bitcast.19, f32[8,64,8,128]{3,2,1,0:T(8,128)S(1)} %bitcast.24, f32[4,32,8,128]{3,2,1,0:T(8,128)S(1)} %bitcast.29, f32[4,32,8,128]{3,2,1,0:T(8,128)S(1)} %bitcast.33), custom_call_target="tpu_custom_call" | custom-call | tf_op jit(solution)/shard_map/gram_early/pallas_call | solution.py:591
  91.5 7.3 %collective-permute-done.15 = f32[4,16,16,128]{3,2,1,0:T(8,128)S(1)} collective-permute-done((f32[4,16,16,128]{3,2,1,0:T(8,128)S(1)}, f32[4,16,16,128]{3,2,1,0:T(8,128)S(1)}, u32[]{:S(2)}, u32[]{:S(2)}) %collective-permute-start.15) | collective-permute-done | bytes 524320 | tf_op jit(solution)/shard_map/ppermute | solution.py:580
  98.8 11.2 %collective-permute-done.14 = f32[4,16,16,128]{3,2,1,0:T(8,128)S(1)} collective-permute-done((f32[4,16,16,128]{3,2,1,0:T(8,128)S(1)}, f32[4,16,16,128]{3,2,1,0:T(8,128)S(1)}, u32[]{:S(2)}, u32[]{:S(2)}) %collective-permute-start.14) | collective-permute-done | bytes 524320 | tf_op jit(solution)/shard_map/ppermute | solution.py:580
  110.7 4.9 %collective-permute-start.16 = (f32[16,128]{1,0:T(8,128)S(1)}, f32[16,128]{1,0:T(8,128)S(1)}, u32[]{:S(2)}, u32[]{:S(2)}) collective-permute-start(f32[16,128]{1,0:T(8,128)S(1)} %gram_late.1), channel_id=1, source_target_pairs={{0,2},{2,0},{4,6},{6,4},{8,10},{10,8},{12,14},{14,12},{16,18},{18,... | collective-permute-start | bytes 24584 | tf_op jit(solution)/shard_map/ppermute | solution.py:457
  115.6 0.8 collective-permute-done.16
  116.4 4.4 %collective-permute-start.18 = (f32[16,128]{1,0:T(8,128)S(1)}, f32[16,128]{1,0:T(8,128)S(1)}, u32[]{:S(2)}, u32[]{:S(2)}) collective-permute-start(f32[16,128]{1,0:T(8,128)S(1)} %add.64), channel_id=1, source_target_pairs={{0,1},{1,0},{2,3},{3,2},{4,5},{5,4},{6,7},{7,6},{8,9},{9,8},{10,11... | collective-permute-start | bytes 24584 | tf_op jit(solution)/shard_map/ppermute | solution.py:468
  120.8 2.6 %collective-permute-start.19 = (f32[16,128]{1,0:T(8,128)S(1)}, f32[16,128]{1,0:T(8,128)S(1)}, u32[]{:S(2)}, u32[]{:S(2)}) collective-permute-start(f32[16,128]{1,0:T(8,128)S(1)} %add.64), channel_id=1, source_target_pairs={{0,65},{1,64},{2,67},{3,66},{4,69},{5,68},{6,71},{7,70},{8,73},{9,... | collective-permute-start | bytes 24584 | tf_op jit(solution)/shard_map/ppermute | solution.py:468
  123.5 1.4 collective-permute-done.19
  124.8 1.5 collective-permute-start.21
  126.4 1.4 collective-permute-start.22
  127.8 3.8 %collective-permute-start.36 = (f32[8,32,8,128]{3,2,1,0:T(8,128)S(1)}, f32[8,32,8,128]{3,2,1,0:T(8,128)S(1)}, u32[]{:S(2)}, u32[]{:S(2)}) collective-permute-start(f32[8,32,8,128]{3,2,1,0:T(8,128)S(1)} %get-tuple-element.58), channel_id=1, source_target_pairs={{0,1},{2,3},{4,5},{6,7},{8,9},{10,11},{12,13},{14,15},{16,17},{18,... | collective-permute-start | bytes 3145736 | tf_op jit(solution)/shard_map/ppermute | solution.py:603
  131.6 1.9 %collective-permute-start.23 = (f32[16,128]{1,0:T(8,128)S(1)}, f32[16,128]{1,0:T(8,128)S(1)}, u32[]{:S(2)}, u32[]{:S(2)}) collective-permute-start(f32[16,128]{1,0:T(8,128)S(1)} %add_add_fusion.4), channel_id=1, source_target_pairs={{0,16},{2,18},{4,20},{6,22},{8,24},{10,26},{12,28},{14,30},{16,32}... | collective-permute-start | bytes 24584 | tf_op jit(solution)/shard_map/ppermute | solution.py:457
  133.5 4.1 %collective-permute-start.24 = (f32[16,128]{1,0:T(8,128)S(1)}, f32[16,128]{1,0:T(8,128)S(1)}, u32[]{:S(2)}, u32[]{:S(2)}) collective-permute-start(f32[16,128]{1,0:T(8,128)S(1)} %add_add_fusion.4), channel_id=1, source_target_pairs={{0,32},{2,34},{4,36},{6,38},{8,40},{10,42},{12,44},{14,46},{16,48}... | collective-permute-start | bytes 24584 | tf_op jit(solution)/shard_map/ppermute | solution.py:457
  137.7 1.5 collective-permute-done.24
  139.3 1.9 %collective-permute-done.25 = f32[16,128]{1,0:T(8,128)S(1)} collective-permute-done((f32[16,128]{1,0:T(8,128)S(1)}, f32[16,128]{1,0:T(8,128)S(1)}, u32[]{:S(2)}, u32[]{:S(2)}) %collective-permute-start.25) | collective-permute-done | bytes 8224 | tf_op jit(solution)/shard_map/ppermute | solution.py:457
  141.2 2.7 %project.1 = (f32[16,16]{1,0:T(8,128)}, f32[16,16]{1,0:T(8,128)S(1)}, f32[16,16]{1,0:T(8,128)S(1)}, f32[16,16,128]{2,1,0:T(8,128)S(1)}) custom-call(f32[16,128]{1,0:T(8,128)S(1)} %add_add_fusion.3.gram_ref), custom_call_target="tpu_custom_call" | custom-call | tf_op jit(solution)/shard_map/project/pallas_call | solution.py:608
  143.9 4.3 %residual.1 = f32[16,128]{1,0:T(8,128)S(1)} custom-call(f32[16,16,128]{2,1,0:T(8,128)S(1)} %get-tuple-element.53.table_ref, f32[8,64,8,128]{3,2,1,0:T(8,128)S(1)} %bitcast.21, f32[8,64,8,128]{3,2,1,0:T(8,128)S(1)} %bitcast.26, f32[4,32,8,128]{3,2,1,0:T(8,128)S(1)} %bitcast.31, f32[4,32,8,128]{3,2,1,0:T(8,128)S(1)} %bitcast.35, ...), custom_call_target="tpu_custom_call" | custom-call | tf_op jit(solution)/shard_map/residual/pallas_call | solution.py:616
  148.3 1.2 collective-permute-done.26
  149.5 0.8 collective-permute-start.27
  150.3 2.8 %collective-permute-start.28 = (f32[16,128]{1,0:T(8,128)S(1)}, f32[16,128]{1,0:T(8,128)S(1)}, u32[]{:S(2)}, u32[]{:S(2)}) collective-permute-start(f32[16,128]{1,0:T(8,128)S(1)} %add.74), channel_id=1, source_target_pairs={{0,1},{1,0},{2,3},{3,2},{4,5},{5,4},{6,7},{7,6},{8,9},{9,8},{10,11... | collective-permute-start | bytes 24584 | tf_op jit(solution)/shard_map/ppermute | solution.py:468
  153.7 0.7 collective-permute-done.27
  154.4 1.0 collective-permute-done.28
  155.4 1.3 collective-permute-done.29
  156.7 1.1 collective-permute-start.30
  157.8 2.3 %collective-permute-start.31 = (f32[16,128]{1,0:T(8,128)S(1)}, f32[16,128]{1,0:T(8,128)S(1)}, u32[]{:S(2)}, u32[]{:S(2)}) collective-permute-start(f32[16,128]{1,0:T(8,128)S(1)} %add_add_fusion.2), channel_id=1, source_target_pairs={{0,8},{2,10},{4,12},{6,14},{8,0},{10,2},{12,4},{14,6},{16,24},{18,... | collective-permute-start | bytes 24584 | tf_op jit(solution)/shard_map/ppermute | solution.py:457
  160.4 2.6 %collective-permute-done.31 = f32[16,128]{1,0:T(8,128)S(1)} collective-permute-done((f32[16,128]{1,0:T(8,128)S(1)}, f32[16,128]{1,0:T(8,128)S(1)}, u32[]{:S(2)}, u32[]{:S(2)}) %collective-permute-start.31) | collective-permute-done | bytes 8224 | tf_op jit(solution)/shard_map/ppermute | solution.py:457
  163.0 2.0 %collective-permute-done.32 = f32[16,128]{1,0:T(8,128)S(1)} collective-permute-done((f32[16,128]{1,0:T(8,128)S(1)}, f32[16,128]{1,0:T(8,128)S(1)}, u32[]{:S(2)}, u32[]{:S(2)}) %collective-permute-start.32) | collective-permute-done | bytes 8224 | tf_op jit(solution)/shard_map/ppermute | solution.py:457
  165.0 1.0 collective-permute-start.33
  166.0 2.7 %collective-permute-start.34 = (f32[16,128]{1,0:T(8,128)S(1)}, f32[16,128]{1,0:T(8,128)S(1)}, u32[]{:S(2)}, u32[]{:S(2)}) collective-permute-start(f32[16,128]{1,0:T(8,128)S(1)} %add_add_fusion.1), channel_id=1, source_target_pairs={{0,32},{2,34},{4,36},{6,38},{8,40},{10,42},{12,44},{14,46},{16,48}... | collective-permute-start | bytes 24584 | tf_op jit(solution)/shard_map/ppermute | solution.py:457
  169.1 0.7 collective-permute-done.33
  169.8 1.3 collective-permute-done.34
  171.1 1.2 collective-permute-done.35
  172.3 2.7 %algebra.1 = (f32[16,16]{1,0:T(8,128)}, f32[32,8,128]{2,1,0:T(8,128)S(1)}) custom-call(f32[16,128]{1,0:T(8,128)S(1)} %add_add_fusion.gram_ref, f32[16,16]{1,0:T(8,128)S(1)} %get-tuple-element.54.inverse_ref, f32[16,16]{1,0:T(8,128)S(1)} %get-tuple-element.55.mix_ref), custom_call_target="tpu_custom_call" | custom-call | tf_op jit(solution)/shard_map/algebra/pallas_call | solution.py:629
  175.0 3.0 %combine_mine.1.refs_3_ = f32[8,64,8,128]{3,2,1,0:T(8,128)} custom-call(f32[32,8,128]{2,1,0:T(8,128)S(1)} %get-tuple-element.57.table_ref, f32[8,64,8,128]{3,2,1,0:T(8,128)S(1)} %bitcast.22, f32[8,64,8,128]{3,2,1,0:T(8,128)S(1)} %bitcast.27, f32[4,32,8,128]{3,2,1,0:T(8,128)S(1)} %bitcast.32, f32[4,32,8,128]{3,2,1,0:T(8,128)S(1)} %bitcast.36, ...), custom_call_target="tpu_custom_call" | custom-call | tf_op jit(solution)/shard_map/combine_mine/pallas_call | solution.py:641
  178.0 3.6 %combine_theirs.1 = f32[8,64,8,128]{3,2,1,0:T(8,128)} custom-call(f32[32,8,128]{2,1,0:T(8,128)S(1)} %get-tuple-element.57.table_ref, f32[8,64,8,128]{3,2,1,0:T(8,128)S(1)} %bitcast.23, f32[8,64,8,128]{3,2,1,0:T(8,128)S(1)} %bitcast.28, f32[4,32,8,128]{3,2,1,0:T(8,128)S(1)} %bitcast.55, ...), custom_call_target="tpu_custom_call", output_to_operand_aliasing={{}: (6, {})} | custom-call | tf_op jit(solution)/shard_map/combine_theirs/pallas_call | solution.py:641
  (41 shorter events, 4.5 us)
Async XLA Ops:
  0.6 4.2 %copy-start.1 = (s32[8,32,16,128]{3,2,1,0:T(8,128)S(1)}, s32[8,32,16,128]{3,2,1,0:T(8,128)}, u32[]{:S(2)}) copy-start(s32[8,32,16,128]{3,2,1,0:T(8,128)} %param.3) | copy-start | bytes 6291460
  2.6 8.9 %copy-start = (s32[12,32,16,128]{3,2,1,0:T(8,128)S(1)}, s32[12,32,16,128]{3,2,1,0:T(8,128)}, u32[]{:S(2)}) copy-start(s32[12,32,16,128]{3,2,1,0:T(8,128)} %levels_ref.5) | copy-start | bytes 9437188
  2.6 8.9 %collective-permute-start.5 = (f32[40,16,128]{2,1,0:T(8,128)}, f32[40,16,128]{2,1,0:T(8,128)S(1)}, u32[]{:S(2)}, u32[]{:S(2)}) collective-permute-start(f32[40,16,128]{2,1,0:T(8,128)} %tail.1), channel_id=1, source_target_pairs={{0,2},{2,4},{4,6},{6,8},{8,10},{10,12},{12,14},{14,16},{16,18},{18... | collective-permute-start | bytes 983048 | tf_op jit(solution)/shard_map/ppermute | solution.py:486
  12.9 14.4 %collective-permute-start.6 = (f32[4,27,16,128]{3,2,1,0:T(8,128)S(1)}, f32[4,27,16,128]{3,2,1,0:T(8,128)S(1)}, u32[]{:S(2)}, u32[]{:S(2)}) collective-permute-start(f32[4,27,16,128]{3,2,1,0:T(8,128)S(1)} %get-tuple-element.32), channel_id=1, source_target_pairs={{0,2},{2,4},{4,6},{6,8},{8,10},{10,12},{12,14},{14,16},{16,18},{18... | collective-permute-start | bytes 2654216 | tf_op jit(solution)/shard_map/ppermute | solution.py:486
  14.8 14.2 %collective-permute-start.7 = (f32[4,27,16,128]{3,2,1,0:T(8,128)S(1)}, f32[4,27,16,128]{3,2,1,0:T(8,128)S(1)}, u32[]{:S(2)}, u32[]{:S(2)}) collective-permute-start(f32[4,27,16,128]{3,2,1,0:T(8,128)S(1)} %get-tuple-element.33), channel_id=1, source_target_pairs={{2,0},{4,2},{6,4},{8,6},{10,8},{12,10},{14,12},{16,14},{18,16},{20... | collective-permute-start | bytes 2654216 | tf_op jit(solution)/shard_map/ppermute | solution.py:489
  18.5 20.8 %collective-permute-start.8 = (f32[4,27,16,128]{3,2,1,0:T(8,128)S(1)}, f32[4,27,16,128]{3,2,1,0:T(8,128)S(1)}, u32[]{:S(2)}, u32[]{:S(2)}) collective-permute-start(f32[4,27,16,128]{3,2,1,0:T(8,128)S(1)} %get-tuple-element.35), channel_id=1, source_target_pairs={{0,2},{2,4},{4,6},{6,8},{8,10},{10,12},{12,14},{14,16},{16,18},{18... | collective-permute-start | bytes 2654216 | tf_op jit(solution)/shard_map/ppermute | solution.py:486
  22.1 24.6 %collective-permute-start.9 = (f32[4,27,16,128]{3,2,1,0:T(8,128)S(1)}, f32[4,27,16,128]{3,2,1,0:T(8,128)S(1)}, u32[]{:S(2)}, u32[]{:S(2)}) collective-permute-start(f32[4,27,16,128]{3,2,1,0:T(8,128)S(1)} %get-tuple-element.36), channel_id=1, source_target_pairs={{2,0},{4,2},{6,4},{8,6},{10,8},{12,10},{14,12},{16,14},{18,16},{20... | collective-permute-start | bytes 2654216 | tf_op jit(solution)/shard_map/ppermute | solution.py:489
  24.2 27.5 %collective-permute-start.1 = (f32[4,32,16,128]{3,2,1,0:T(8,128)S(1)}, f32[4,32,16,128]{3,2,1,0:T(8,128)S(1)}, u32[]{:S(2)}, u32[]{:S(2)}) collective-permute-start(f32[4,32,16,128]{3,2,1,0:T(8,128)S(1)} %get-tuple-element.59), channel_id=1, source_target_pairs={{0,17},{1,16},{2,7},{3,6},{124,77},{125,76},{126,115},{127,114}} | collective-permute-start | bytes 3145736 | tf_op jit(solution)/shard_map/ppermute | solution.py:510
  27.3 26.9 %collective-permute-start.3 = (f32[4,32,16,128]{3,2,1,0:T(8,128)S(1)}, f32[4,32,16,128]{3,2,1,0:T(8,128)S(1)}, u32[]{:S(2)}, u32[]{:S(2)}) collective-permute-start(f32[4,32,16,128]{3,2,1,0:T(8,128)S(1)} %get-tuple-element.60), channel_id=1, source_target_pairs={{0,49},{1,48},{2,15},{3,14},{124,109},{125,108},{126,123},{127,122}} | collective-permute-start | bytes 3145736 | tf_op jit(solution)/shard_map/ppermute | solution.py:510
  29.0 58.5 %collective-permute-start = (f32[8,32,16,128]{3,2,1,0:T(8,128)S(1)}, f32[8,32,16,128]{3,2,1,0:T(8,128)S(1)}, u32[]{:S(2)}, u32[]{:S(2)}) collective-permute-start(f32[8,32,16,128]{3,2,1,0:T(8,128)S(1)} %convert_element_type.3.start_ref.own_ref), channel_id=1, source_target_pairs={{4,5},{5,4},{6,7},{7,6},{8,9},{9,8},{10,11},{11,10},{12,13},{13,12... | collective-permute-start | bytes 6291464 | tf_op jit(solution)/shard_map/ppermute | solution.py:512
  39.3 18.0 %collective-permute-start.10 = (f32[4,27,16,128]{3,2,1,0:T(8,128)S(1)}, f32[4,27,16,128]{3,2,1,0:T(8,128)S(1)}, u32[]{:S(2)}, u32[]{:S(2)}) collective-permute-start(f32[4,27,16,128]{3,2,1,0:T(8,128)S(1)} %get-tuple-element.39), channel_id=1, source_target_pairs={{0,2},{2,4},{4,6},{6,8},{8,10},{10,12},{12,14},{14,16},{16,18},{18... | collective-permute-start | bytes 2654216 | tf_op jit(solution)/shard_map/ppermute | solution.py:486
  46.7 12.5 %collective-permute-start.11 = (f32[4,27,16,128]{3,2,1,0:T(8,128)S(1)}, f32[4,27,16,128]{3,2,1,0:T(8,128)S(1)}, u32[]{:S(2)}, u32[]{:S(2)}) collective-permute-start(f32[4,27,16,128]{3,2,1,0:T(8,128)S(1)} %get-tuple-element.40), channel_id=1, source_target_pairs={{2,0},{4,2},{6,4},{8,6},{10,8},{12,10},{14,12},{16,14},{18,16},{20... | collective-permute-start | bytes 2654216 | tf_op jit(solution)/shard_map/ppermute | solution.py:489
  51.8 14.4 %collective-permute-start.12 = (f32[4,27,16,128]{3,2,1,0:T(8,128)S(1)}, f32[4,27,16,128]{3,2,1,0:T(8,128)S(1)}, u32[]{:S(2)}, u32[]{:S(2)}) collective-permute-start(f32[4,27,16,128]{3,2,1,0:T(8,128)S(1)} %get-tuple-element.43), channel_id=1, source_target_pairs={{0,2},{2,4},{4,6},{6,8},{8,10},{10,12},{12,14},{14,16},{16,18},{18... | collective-permute-start | bytes 2654216 | tf_op jit(solution)/shard_map/ppermute | solution.py:486
  54.2 18.0 %collective-permute-start.13 = (f32[4,27,16,128]{3,2,1,0:T(8,128)S(1)}, f32[4,27,16,128]{3,2,1,0:T(8,128)S(1)}, u32[]{:S(2)}, u32[]{:S(2)}) collective-permute-start(f32[4,27,16,128]{3,2,1,0:T(8,128)S(1)} %get-tuple-element.44), channel_id=1, source_target_pairs={{2,0},{4,2},{6,4},{8,6},{10,8},{12,10},{14,12},{16,14},{18,16},{20... | collective-permute-start | bytes 2654216 | tf_op jit(solution)/shard_map/ppermute | solution.py:489
  57.4 23.2 %collective-permute-start.2 = (f32[4,32,16,128]{3,2,1,0:T(8,128)S(1)}, f32[4,32,16,128]{3,2,1,0:T(8,128)S(1)}, u32[]{:S(2)}, u32[]{:S(2)}) collective-permute-start(f32[4,32,16,128]{3,2,1,0:T(8,128)S(1)} %collective-permute-done.1), channel_id=1, source_target_pairs={{17,1},{16,0},{7,3},{6,2},{77,125},{76,124},{115,127},{114,126}} | collective-permute-start | bytes 3145736 | tf_op jit(solution)/shard_map/ppermute | solution.py:511
  59.2 21.4 %collective-permute-start.4 = (f32[4,32,16,128]{3,2,1,0:T(8,128)S(1)}, f32[4,32,16,128]{3,2,1,0:T(8,128)S(1)}, u32[]{:S(2)}, u32[]{:S(2)}) collective-permute-start(f32[4,32,16,128]{3,2,1,0:T(8,128)S(1)} %collective-permute-done.3), channel_id=1, source_target_pairs={{49,1},{48,0},{15,3},{14,2},{109,125},{108,124},{123,127},{122,126}} | collective-permute-start | bytes 3145736 | tf_op jit(solution)/shard_map/ppermute | solution.py:511
  73.7 25.1 %collective-permute-start.15 = (f32[4,16,16,128]{3,2,1,0:T(8,128)S(1)}, f32[4,16,16,128]{3,2,1,0:T(8,128)S(1)}, u32[]{:S(2)}, u32[]{:S(2)}) collective-permute-start(f32[4,16,16,128]{3,2,1,0:T(8,128)S(1)} %get-tuple-element.50), channel_id=1, source_target_pairs={{0,1},{1,0},{2,3},{3,2},{4,5},{5,4},{6,7},{7,6},{8,9},{9,8},{10,11... | collective-permute-start | bytes 1572872 | tf_op jit(solution)/shard_map/ppermute | solution.py:580
  73.8 36.2 %collective-permute-start.14 = (f32[4,16,16,128]{3,2,1,0:T(8,128)S(1)}, f32[4,16,16,128]{3,2,1,0:T(8,128)S(1)}, u32[]{:S(2)}, u32[]{:S(2)}) collective-permute-start(f32[4,16,16,128]{3,2,1,0:T(8,128)S(1)} %get-tuple-element.49), channel_id=1, source_target_pairs={{0,1},{1,0},{2,3},{3,2},{4,5},{5,4},{6,7},{7,6},{8,9},{9,8},{10,11... | collective-permute-start | bytes 1572872 | tf_op jit(solution)/shard_map/ppermute | solution.py:580
  110.7 5.7 %collective-permute-start.16 = (f32[16,128]{1,0:T(8,128)S(1)}, f32[16,128]{1,0:T(8,128)S(1)}, u32[]{:S(2)}, u32[]{:S(2)}) collective-permute-start(f32[16,128]{1,0:T(8,128)S(1)} %gram_late.1), channel_id=1, source_target_pairs={{0,2},{2,0},{4,6},{6,4},{8,10},{10,8},{12,14},{14,12},{16,18},{18,... | collective-permute-start | bytes 24584 | tf_op jit(solution)/shard_map/ppermute | solution.py:457
  116.4 7.0 %collective-permute-start.17 = (f32[16,128]{1,0:T(8,128)S(1)}, f32[16,128]{1,0:T(8,128)S(1)}, u32[]{:S(2)}, u32[]{:S(2)}) collective-permute-start(f32[16,128]{1,0:T(8,128)S(1)} %add.64), channel_id=1, source_target_pairs={{0,64},{1,65},{2,66},{3,67},{4,68},{5,69},{6,70},{7,71},{8,72},{9,... | collective-permute-start | bytes 24584 | tf_op jit(solution)/shard_map/ppermute | solution.py:468
  116.4 7.0 %collective-permute-start.18 = (f32[16,128]{1,0:T(8,128)S(1)}, f32[16,128]{1,0:T(8,128)S(1)}, u32[]{:S(2)}, u32[]{:S(2)}) collective-permute-start(f32[16,128]{1,0:T(8,128)S(1)} %add.64), channel_id=1, source_target_pairs={{0,1},{1,0},{2,3},{3,2},{4,5},{5,4},{6,7},{7,6},{8,9},{9,8},{10,11... | collective-permute-start | bytes 24584 | tf_op jit(solution)/shard_map/ppermute | solution.py:468
  120.8 4.0 %collective-permute-start.19 = (f32[16,128]{1,0:T(8,128)S(1)}, f32[16,128]{1,0:T(8,128)S(1)}, u32[]{:S(2)}, u32[]{:S(2)}) collective-permute-start(f32[16,128]{1,0:T(8,128)S(1)} %add.64), channel_id=1, source_target_pairs={{0,65},{1,64},{2,67},{3,66},{4,69},{5,68},{6,71},{7,70},{8,73},{9,... | collective-permute-start | bytes 24584 | tf_op jit(solution)/shard_map/ppermute | solution.py:468
  124.8 6.7 %collective-permute-start.20 = (f32[16,128]{1,0:T(8,128)S(1)}, f32[16,128]{1,0:T(8,128)S(1)}, u32[]{:S(2)}, u32[]{:S(2)}) collective-permute-start(f32[16,128]{1,0:T(8,128)S(1)} %add_add_fusion.5), channel_id=1, source_target_pairs={{0,4},{2,6},{4,8},{6,10},{8,12},{10,14},{12,0},{14,2},{16,20},{18,... | collective-permute-start | bytes 24584 | tf_op jit(solution)/shard_map/ppermute | solution.py:457
  124.8 6.7 %collective-permute-start.21 = (f32[16,128]{1,0:T(8,128)S(1)}, f32[16,128]{1,0:T(8,128)S(1)}, u32[]{:S(2)}, u32[]{:S(2)}) collective-permute-start(f32[16,128]{1,0:T(8,128)S(1)} %add_add_fusion.5), channel_id=1, source_target_pairs={{0,8},{2,10},{4,12},{6,14},{8,0},{10,2},{12,4},{14,6},{16,24},{18,... | collective-permute-start | bytes 24584 | tf_op jit(solution)/shard_map/ppermute | solution.py:457
  126.4 5.2 %collective-permute-start.22 = (f32[16,128]{1,0:T(8,128)S(1)}, f32[16,128]{1,0:T(8,128)S(1)}, u32[]{:S(2)}, u32[]{:S(2)}) collective-permute-start(f32[16,128]{1,0:T(8,128)S(1)} %add_add_fusion.5), channel_id=1, source_target_pairs={{0,12},{2,14},{4,0},{6,2},{8,4},{10,6},{12,8},{14,10},{16,28},{18,... | collective-permute-start | bytes 24584 | tf_op jit(solution)/shard_map/ppermute | solution.py:457
  127.8 50.2 %collective-permute-start.36 = (f32[8,32,8,128]{3,2,1,0:T(8,128)S(1)}, f32[8,32,8,128]{3,2,1,0:T(8,128)S(1)}, u32[]{:S(2)}, u32[]{:S(2)}) collective-permute-start(f32[8,32,8,128]{3,2,1,0:T(8,128)S(1)} %get-tuple-element.58), channel_id=1, source_target_pairs={{0,1},{2,3},{4,5},{6,7},{8,9},{10,11},{12,13},{14,15},{16,17},{18,... | collective-permute-start | bytes 3145736 | tf_op jit(solution)/shard_map/ppermute | solution.py:603
  131.6 6.1 %collective-permute-start.23 = (f32[16,128]{1,0:T(8,128)S(1)}, f32[16,128]{1,0:T(8,128)S(1)}, u32[]{:S(2)}, u32[]{:S(2)}) collective-permute-start(f32[16,128]{1,0:T(8,128)S(1)} %add_add_fusion.4), channel_id=1, source_target_pairs={{0,16},{2,18},{4,20},{6,22},{8,24},{10,26},{12,28},{14,30},{16,32}... | collective-permute-start | bytes 24584 | tf_op jit(solution)/shard_map/ppermute | solution.py:457
  133.5 5.8 %collective-permute-start.24 = (f32[16,128]{1,0:T(8,128)S(1)}, f32[16,128]{1,0:T(8,128)S(1)}, u32[]{:S(2)}, u32[]{:S(2)}) collective-permute-start(f32[16,128]{1,0:T(8,128)S(1)} %add_add_fusion.4), channel_id=1, source_target_pairs={{0,32},{2,34},{4,36},{6,38},{8,40},{10,42},{12,44},{14,46},{16,48}... | collective-permute-start | bytes 24584 | tf_op jit(solution)/shard_map/ppermute | solution.py:457
  137.6 3.7 %collective-permute-start.25 = (f32[16,128]{1,0:T(8,128)S(1)}, f32[16,128]{1,0:T(8,128)S(1)}, u32[]{:S(2)}, u32[]{:S(2)}) collective-permute-start(f32[16,128]{1,0:T(8,128)S(1)} %add_add_fusion.4), channel_id=1, source_target_pairs={{0,48},{2,50},{4,52},{6,54},{8,56},{10,58},{12,60},{14,62},{16,0},... | collective-permute-start | bytes 24584 | tf_op jit(solution)/shard_map/ppermute | solution.py:457
  148.2 1.3 collective-permute-start.26
  149.5 4.9 %collective-permute-start.27 = (f32[16,128]{1,0:T(8,128)S(1)}, f32[16,128]{1,0:T(8,128)S(1)}, u32[]{:S(2)}, u32[]{:S(2)}) collective-permute-start(f32[16,128]{1,0:T(8,128)S(1)} %add.74), channel_id=1, source_target_pairs={{0,64},{1,65},{2,66},{3,67},{4,68},{5,69},{6,70},{7,71},{8,72},{9,... | collective-permute-start | bytes 24584 | tf_op jit(solution)/shard_map/ppermute | solution.py:468
  150.3 5.2 %collective-permute-start.28 = (f32[16,128]{1,0:T(8,128)S(1)}, f32[16,128]{1,0:T(8,128)S(1)}, u32[]{:S(2)}, u32[]{:S(2)}) collective-permute-start(f32[16,128]{1,0:T(8,128)S(1)} %add.74), channel_id=1, source_target_pairs={{0,1},{1,0},{2,3},{3,2},{4,5},{5,4},{6,7},{7,6},{8,9},{9,8},{10,11... | collective-permute-start | bytes 24584 | tf_op jit(solution)/shard_map/ppermute | solution.py:468
  153.1 3.7 %collective-permute-start.29 = (f32[16,128]{1,0:T(8,128)S(1)}, f32[16,128]{1,0:T(8,128)S(1)}, u32[]{:S(2)}, u32[]{:S(2)}) collective-permute-start(f32[16,128]{1,0:T(8,128)S(1)} %add.74), channel_id=1, source_target_pairs={{0,65},{1,64},{2,67},{3,66},{4,69},{5,68},{6,71},{7,70},{8,73},{9,... | collective-permute-start | bytes 24584 | tf_op jit(solution)/shard_map/ppermute | solution.py:468
  156.7 3.7 %collective-permute-start.30 = (f32[16,128]{1,0:T(8,128)S(1)}, f32[16,128]{1,0:T(8,128)S(1)}, u32[]{:S(2)}, u32[]{:S(2)}) collective-permute-start(f32[16,128]{1,0:T(8,128)S(1)} %add_add_fusion.2), channel_id=1, source_target_pairs={{0,4},{2,6},{4,8},{6,10},{8,12},{10,14},{12,0},{14,2},{16,20},{18,... | collective-permute-start | bytes 24584 | tf_op jit(solution)/shard_map/ppermute | solution.py:457
  157.8 5.2 %collective-permute-start.31 = (f32[16,128]{1,0:T(8,128)S(1)}, f32[16,128]{1,0:T(8,128)S(1)}, u32[]{:S(2)}, u32[]{:S(2)}) collective-permute-start(f32[16,128]{1,0:T(8,128)S(1)} %add_add_fusion.2), channel_id=1, source_target_pairs={{0,8},{2,10},{4,12},{6,14},{8,0},{10,2},{12,4},{14,6},{16,24},{18,... | collective-permute-start | bytes 24584 | tf_op jit(solution)/shard_map/ppermute | solution.py:457
  160.1 4.9 %collective-permute-start.32 = (f32[16,128]{1,0:T(8,128)S(1)}, f32[16,128]{1,0:T(8,128)S(1)}, u32[]{:S(2)}, u32[]{:S(2)}) collective-permute-start(f32[16,128]{1,0:T(8,128)S(1)} %add_add_fusion.2), channel_id=1, source_target_pairs={{0,12},{2,14},{4,0},{6,2},{8,4},{10,6},{12,8},{14,10},{16,28},{18,... | collective-permute-start | bytes 24584 | tf_op jit(solution)/shard_map/ppermute | solution.py:457
  165.0 4.9 %collective-permute-start.33 = (f32[16,128]{1,0:T(8,128)S(1)}, f32[16,128]{1,0:T(8,128)S(1)}, u32[]{:S(2)}, u32[]{:S(2)}) collective-permute-start(f32[16,128]{1,0:T(8,128)S(1)} %add_add_fusion.1), channel_id=1, source_target_pairs={{0,16},{2,18},{4,20},{6,22},{8,24},{10,26},{12,28},{14,30},{16,32}... | collective-permute-start | bytes 24584 | tf_op jit(solution)/shard_map/ppermute | solution.py:457
  166.0 5.2 %collective-permute-start.34 = (f32[16,128]{1,0:T(8,128)S(1)}, f32[16,128]{1,0:T(8,128)S(1)}, u32[]{:S(2)}, u32[]{:S(2)}) collective-permute-start(f32[16,128]{1,0:T(8,128)S(1)} %add_add_fusion.1), channel_id=1, source_target_pairs={{0,32},{2,34},{4,36},{6,38},{8,40},{10,42},{12,44},{14,46},{16,48}... | collective-permute-start | bytes 24584 | tf_op jit(solution)/shard_map/ppermute | solution.py:457
  168.7 3.7 %collective-permute-start.35 = (f32[16,128]{1,0:T(8,128)S(1)}, f32[16,128]{1,0:T(8,128)S(1)}, u32[]{:S(2)}, u32[]{:S(2)}) collective-permute-start(f32[16,128]{1,0:T(8,128)S(1)} %add_add_fusion.1), channel_id=1, source_target_pairs={{0,48},{2,50},{4,52},{6,54},{8,56},{10,58},{12,60},{14,62},{16,0},... | collective-permute-start | bytes 24584 | tf_op jit(solution)/shard_map/ppermute | solution.py:457

commit v5 on v4

--- a/solution.py
+++ b/solution.py
@@ -208,67 +208,54 @@
     lax.fori_loop(0, halves, plane, 0, unroll=4)
 
 
-def gram_kernel(early, own_x_ref, other_x_ref, *refs):
-    if early:
-        ys, (out_ref, late_ref, acc_ref) = refs[:2], refs[2:]
-        for place, ref in enumerate(ys):
-            late_ref[pl.ds(place * chunk, chunk)] = ref[...]
-    else:
-        ys, (before_ref, out_ref, acc_ref) = refs[:4], refs[4:]
+def gram_kernel(own_x_ref, other_x_ref, *refs):
+    ys, (out_ref, late_ref, acc_ref) = refs[:4], refs[4:]
+    for place, ref in enumerate(ys[2:]):
+        late_ref[pl.ds(place * chunk, chunk)] = ref[...]
     cols = own_x_ref.shape[0]
     tiles = own_x_ref.shape[1] // 2
-    group = chunk
     vec = lax.axis_index("vec")
     acc_ref[...] = jnp.zeros_like(acc_ref)
 
-    def load(kind, number, t):
-        if kind == "x":
-            ref = own_x_ref if number < 2 else other_x_ref
-            return [ref[(number % 2) * group + k, vec * tiles + t] for k in range(group)]
-        return [ys[number][k, t] for k in range(group)]
-
-    def block_of_pairs(slot, left_kind, left, right_kind, right):
-        same = left == right
-        pairs = [(i, j) for i in range(group) for j in range(group) if not (same and j < i)]
-
-        def step(t, accs):
-            a = load(left_kind, left, t)
-            b = a if same and left_kind == right_kind else load(right_kind, right, t)
-            return tuple(acc + a[i] * b[j] for (i, j), acc in zip(pairs, accs))
-
-        zero = tuple(jnp.zeros((8, 128), f32) for _ in pairs)
-        accs = lax.fori_loop(0, tiles, step, zero, unroll=4)
-        for (i, j), acc in zip(pairs, accs):
-            row = jnp.sum(acc, axis=0, keepdims=True)
-            gi = lax.rem(left * group + i + cols * vec, 2 * cols)
-            gj = lax.rem(right * group + j + cols * vec, 2 * cols)
-            acc_ref[slot, pl.ds(gi * 16 + gj, 1), :] = row
-            acc_ref[slot, pl.ds(gj * 16 + gi, 1), :] = row
+    def xs(number, tile):
+        ref = own_x_ref if number < 2 else other_x_ref
+        return [ref[(number % 2) * chunk + k, tile] for k in range(chunk)]
+
+    def place_of(number, k):
+        return lax.rem(number * chunk + k + cols * vec, 2 * cols)
 
     for left in range(4):
-        for right in range(left, 4):
-            if early:
-                block_of_pairs(0, "x", left, "x", right)
-            if (right < 2) == early:
-                if left // 2 == right // 2:
-                    block_of_pairs(1, "y", left, "x", right)
-            if left // 2 != right // 2:
-                if early:
-
-                    @pl.when(vec == 0)
-                    def _(left=left, right=right):
-                        block_of_pairs(1, "y", left, "x", right)
-
-                else:
-
-                    @pl.when(vec == 1)
-                    def _(left=left, right=right):
-                        block_of_pairs(1, "y", right, "x", left)
+        for right in range(4):
+            pairs = [(i, j) for i in range(chunk) for j in range(chunk)]
+            zero = tuple(jnp.zeros((8, 128), f32) for _ in pairs)
+            if right >= left:
+
+                def step(t, accs):
+                    a, b = xs(left, vec * tiles + t), xs(right, vec * tiles + t)
+                    return tuple(acc + a[i] * b[j] for (i, j), acc in zip(pairs, accs))
+
+                for (i, j), acc in zip(pairs, lax.fori_loop(0, tiles, step, zero, unroll=4)):
+                    row = jnp.sum(acc, axis=0, keepdims=True)
+                    gi, gj = place_of(left, i), place_of(right, j)
+                    acc_ref[0, pl.ds(gi * 16 + gj, 1), :] = row
+                    acc_ref[0, pl.ds(gj * 16 + gi, 1), :] = row
+            if left < 2:
+                accs = zero
+                for first, y_ref in (((1 - vec) * tiles, ys[left]), (vec * tiles, ys[2 + left])):
+
+                    def step_y(t, accs, first=first, y_ref=y_ref):
+                        b = xs(right, first + t)
+                        return tuple(acc + y_ref[i, t] * b[j] for (i, j), acc in zip(pairs, accs))
+
+                    accs = lax.fori_loop(0, tiles, step_y, accs, unroll=4)
+                for (i, j), acc in zip(pairs, accs):
+                    at = place_of(left, i) * 16 + place_of(right, j)
+                    acc_ref[1, pl.ds(at, 1), :] = jnp.sum(acc, axis=0, keepdims=True)
 
     lane = lax.broadcasted_iota(jnp.int32, (256, 128), 1)
     inner = lax.rem(lax.broadcasted_iota(jnp.int32, (256, 128), 0), 16)
-    total = jnp.zeros((16, 128), f32) if early else before_ref[...]
-    for slot in range(0 if early else 1, 2):
+    total = jnp.zeros((16, 128), f32)
+    for slot in range(2):
         sums = jnp.sum(acc_ref[slot], axis=1, keepdims=True)
         placed = jnp.where(lane == inner + 16 * slot, sums, 0.0)
         total = total + jnp.sum(placed.reshape(16, 16, 128), axis=1)
@@ -457,6 +444,9 @@
         return lax.ppermute(v, "brick", [(place[0], moved(place, dim, by)) for place in places()])
 
     value = value + permute(value, "core", 1)
+    for dim in ("y", "x"):
+        near = [permute(value, dim, by) for by in (1, 2, 3)]
+        value = (value + near[0]) + (near[1] + near[2])
     pairs = {}
     for by in (1, 2, 3):
         table = []
@@ -467,9 +457,6 @@
         pairs[by] = table
     near = [lax.ppermute(value, ("brick", "vec"), pairs[by]) for by in (1, 2, 3)]
     value = (value + near[0]) + (near[1] + near[2])
-    for dim in ("y", "x"):
-        near = [permute(value, dim, by) for by in (1, 2, 3)]
-        value = (value + near[0]) + (near[1] + near[2])
     return value
 
 
@@ -585,23 +572,20 @@
     def tiled(value):
         return value.reshape(value.shape[0], -1, 8, lanes) if value.shape[2] != 8 else value
 
-    def gram_call(early, *operands):
-        out = jax.ShapeDtypeStruct((2 * own_cols, 128), f32)
-        late = jax.ShapeDtypeStruct((own_cols, halves * rows // 8, 8, lanes), f32)
-        return pl.pallas_call(
-            functools.partial(gram_kernel, early),
-            out_shape=(out, late) if early else out,
-            in_specs=[VMEM] * len(operands),
-            out_specs=(VMEM, VMEM) if early else VMEM,
-            scratch_shapes=[pltpu.VMEM((2, 256, 128), f32)],
-            compiler_params=params(4),
-            name="gram_early" if early else "gram_late",
-        )(*operands)
-
     mine_tiled = [tiled(value) for value in (x_own, x_other, *y_mine)]
-    partial_gram, outgoing = gram_call(True, *mine_tiled)
+    gram, outgoing = pl.pallas_call(
+        gram_kernel,
+        out_shape=(
+            jax.ShapeDtypeStruct((2 * own_cols, 128), f32),
+            jax.ShapeDtypeStruct((own_cols, halves * rows // 8, 8, lanes), f32),
+        ),
+        in_specs=[VMEM] * 6,
+        out_specs=(VMEM, VMEM),
+        scratch_shapes=[pltpu.VMEM((2, 256, 128), f32)],
+        compiler_params=params(4),
+        name="gram",
+    )(*mine_tiled[:2], *map(tiled, y_theirs), *mine_tiled[2:])
     late = lax.ppermute(outgoing, "vec", [(0, 1)])
-    gram = gram_call(False, *mine_tiled, *map(tiled, y_other_mine), partial_gram)
     gram = sum_everywhere(gram)
 
     small = jax.ShapeDtypeStruct((16, 16), f32)

time: 182 us -> 194 us (1.066)
  the two profiles are of different devices: /device:TPU:24 before, /device:TPU:26 now
where the time goes in v5:
time: 194 us
  starting transfers between devices  92.3 us (48%)
  waiting for transfers between devices  60 us (31%)
  Pallas kernels  39.5 us (20%)
    ppermute x6, waiting for transfers between devices, sum_everywhere(): lax.ppermute(value, ('brick', 'vec'), pairs[by])  33.9 us
    ppermute x14, starting transfers between devices, permute(): lax.ppermute(v, 'brick', [(place[0], moved(place, dim, by)) for place in...  31.5 us
    ppermute x5, starting transfers between devices, up(): return lax.ppermute(value, 'brick', upward)  22.3 us
    ppermute x5, waiting for transfers between devices, up(): return lax.ppermute(value, 'brick', upward)  13 us
    ppermute x14, waiting for transfers between devices, permute(): lax.ppermute(v, 'brick', [(place[0], moved(place, dim, by)) for place in...  11.2 us
    ppermute x4, starting transfers between devices, down(): return lax.ppermute(value, 'brick', downward)  10.5 us
    ppermute x6, starting transfers between devices, sum_everywhere(): lax.ppermute(value, ('brick', 'vec'), pairs[by])  10.1 us
    pallas_call x2, Pallas kernels, combine(): pl.pallas_call(functools.partial(combine_kernel, mine), in_specs=[VMEM] *...  6.88 us
  transfers between devices with their start and end apart: 37, of which 18 were waited for; matrix products, arithmetic and copies ran while one was open for 0% of the time, Pallas kernels for 15%

profile of v5, /device:TPU:26, one launch (start us, length us, event | category | flops | bytes accessed | tf_op | source)
XLA Modules:
  0.0 193.7 jit_solution(13847417295174482069)
XLA Ops:
  0.6 1.9 %tail.1 = f32[40,16,128]{2,1,0:T(8,128)} custom-call(s32[12,32,16,128]{3,2,1,0:T(8,128)} %levels_ref.5), custom_call_target="tpu_custom_call" | custom-call | tf_op jit(solution)/shard_map/tail/pallas_call | solution.py:478
  2.6 1.9 collective-permute-start.5
  4.5 0.2 convert_element_type.3.start_ref.own_ref
  4.7 0.1 fusion
  4.9 0.9 collective-permute-start.1
  5.8 0.7 collective-permute-start.3
  6.5 4.7 %collective-permute-done.5.halo_ref = f32[40,16,128]{2,1,0:T(8,128)S(1)} collective-permute-done((f32[40,16,128]{2,1,0:T(8,128)}, f32[40,16,128]{2,1,0:T(8,128)S(1)}, u32[]{:S(2)}, u32[]{:S(2)}) %collective-permute-start.5) | collective-permute-done | bytes 327712 | tf_op jit(solution)/shard_map/ppermute | solution.py:473
  11.2 1.4 degree.1
  12.6 1.9 collective-permute-start.6
  14.6 3.6 %collective-permute-start.7 = (f32[4,27,16,128]{3,2,1,0:T(8,128)S(1)}, f32[4,27,16,128]{3,2,1,0:T(8,128)S(1)}, u32[]{:S(2)}, u32[]{:S(2)}) collective-permute-start(f32[4,27,16,128]{3,2,1,0:T(8,128)S(1)} %get-tuple-element.33), channel_id=1, source_target_pairs={{2,0},{4,2},{6,4},{8,6},{10,8},{12,10},{14,12},{16,14},{18,16},{20... | collective-permute-start | bytes 2654216 | tf_op jit(solution)/shard_map/ppermute | solution.py:476
  18.2 5.8 %collective-permute-start = (f32[8,32,16,128]{3,2,1,0:T(8,128)S(1)}, f32[8,32,16,128]{3,2,1,0:T(8,128)S(1)}, u32[]{:S(2)}, u32[]{:S(2)}) collective-permute-start(f32[8,32,16,128]{3,2,1,0:T(8,128)S(1)} %convert_element_type.3.start_ref.own_ref), channel_id=1, source_target_pairs={{4,5},{5,4},{6,7},{7,6},{8,9},{9,8},{10,11},{11,10},{12,13},{13,12... | collective-permute-start | bytes 6291464 | tf_op jit(solution)/shard_map/ppermute | solution.py:499
  24.0 3.0 %collective-permute-done.6 = f32[4,27,16,128]{3,2,1,0:T(8,128)S(1)} collective-permute-done((f32[4,27,16,128]{3,2,1,0:T(8,128)S(1)}, f32[4,27,16,128]{3,2,1,0:T(8,128)S(1)}, u32[]{:S(2)}, u32[]{:S(2)}) %collective-permute-start.6) | collective-permute-done | bytes 884768 | tf_op jit(solution)/shard_map/ppermute | solution.py:473
  27.0 2.8 %collective-permute-start.8 = (f32[4,27,16,128]{3,2,1,0:T(8,128)S(1)}, f32[4,27,16,128]{3,2,1,0:T(8,128)S(1)}, u32[]{:S(2)}, u32[]{:S(2)}) collective-permute-start(f32[4,27,16,128]{3,2,1,0:T(8,128)S(1)} %get-tuple-element.35), channel_id=1, source_target_pairs={{0,2},{2,4},{4,6},{6,8},{8,10},{10,12},{12,14},{14,16},{16,18},{18... | collective-permute-start | bytes 2654216 | tf_op jit(solution)/shard_map/ppermute | solution.py:473
  29.8 3.0 %collective-permute-start.9 = (f32[4,27,16,128]{3,2,1,0:T(8,128)S(1)}, f32[4,27,16,128]{3,2,1,0:T(8,128)S(1)}, u32[]{:S(2)}, u32[]{:S(2)}) collective-permute-start(f32[4,27,16,128]{3,2,1,0:T(8,128)S(1)} %get-tuple-element.36), channel_id=1, source_target_pairs={{2,0},{4,2},{6,4},{8,6},{10,8},{12,10},{14,12},{16,14},{18,16},{20... | collective-permute-start | bytes 2654216 | tf_op jit(solution)/shard_map/ppermute | solution.py:476
  32.9 1.4 weights.1.weight_ref
  34.2 3.1 %shard_map.49 = (f32[4,32,16,128]{3,2,1,0:T(8,128)S(1)}, f32[4,27,16,128]{3,2,1,0:T(8,128)S(1)}, f32[4,27,16,128]{3,2,1,0:T(8,128)S(1)}, f32[22,32,16,128]{3,2,1,0:T(8,128)S(1)}) custom-call(f32[22,32,16,128]{3,2,1,0:T(8,128)S(1)} %weights.1.weight_ref, f32[32,16,128]{2,1,0:T(8,128)S(1)} %get-tuple-element.31.root_ref, ...), custom_call_target="tpu_custom_call", output_to_operand_aliasing={{3}: (0, {})} | custom-call | tf_op jit(solution)/shard_map/pallas_call | solution.py:536
  37.4 5.7 %collective-permute-start.10 = (f32[4,27,16,128]{3,2,1,0:T(8,128)S(1)}, f32[4,27,16,128]{3,2,1,0:T(8,128)S(1)}, u32[]{:S(2)}, u32[]{:S(2)}) collective-permute-start(f32[4,27,16,128]{3,2,1,0:T(8,128)S(1)} %get-tuple-element.39), channel_id=1, source_target_pairs={{0,2},{2,4},{4,6},{6,8},{8,10},{10,12},{12,14},{14,16},{16,18},{18... | collective-permute-start | bytes 2654216 | tf_op jit(solution)/shard_map/ppermute | solution.py:473
  43.0 1.9 collective-permute-start.11
  45.0 0.7 collective-permute-start.2
  45.7 0.7 collective-permute-start.4
  46.5 3.1 %shard_map.50 = (f32[4,32,16,128]{3,2,1,0:T(8,128)S(1)}, f32[4,27,16,128]{3,2,1,0:T(8,128)S(1)}, f32[4,27,16,128]{3,2,1,0:T(8,128)S(1)}, f32[22,32,16,128]{3,2,1,0:T(8,128)S(1)}) custom-call(f32[22,32,16,128]{3,2,1,0:T(8,128)S(1)} %get-tuple-element.34.weight_ref, f32[32,16,128]{2,1,0:T(8,128)S(1)} %get-tuple-element.31.root_ref, ...), custom_call_target="tpu_custom_call", output_to_operand_aliasing={{3}: (0, {})} | custom-call | tf_op jit(solution)/shard_map/pallas_call | solution.py:536
  49.6 2.1 %collective-permute-done.10 = f32[4,27,16,128]{3,2,1,0:T(8,128)S(1)} collective-permute-done((f32[4,27,16,128]{3,2,1,0:T(8,128)S(1)}, f32[4,27,16,128]{3,2,1,0:T(8,128)S(1)}, u32[]{:S(2)}, u32[]{:S(2)}) %collective-permute-start.10) | collective-permute-done | bytes 884768 | tf_op jit(solution)/shard_map/ppermute | solution.py:473
  51.7 1.9 collective-permute-start.13
  53.6 1.9 collective-permute-done.11
  55.5 10.0 %collective-permute-start.12 = (f32[4,27,16,128]{3,2,1,0:T(8,128)S(1)}, f32[4,27,16,128]{3,2,1,0:T(8,128)S(1)}, u32[]{:S(2)}, u32[]{:S(2)}) collective-permute-start(f32[4,27,16,128]{3,2,1,0:T(8,128)S(1)} %get-tuple-element.44), channel_id=1, source_target_pairs={{0,2},{2,4},{4,6},{6,8},{8,10},{10,12},{12,14},{14,16},{16,18},{18... | collective-permute-start | bytes 2654216 | tf_op jit(solution)/shard_map/ppermute | solution.py:473
  65.6 1.6 shard_map.51
  67.2 3.2 %collective-permute-done.12 = f32[4,27,16,128]{3,2,1,0:T(8,128)S(1)} collective-permute-done((f32[4,27,16,128]{3,2,1,0:T(8,128)S(1)}, f32[4,27,16,128]{3,2,1,0:T(8,128)S(1)}, u32[]{:S(2)}, u32[]{:S(2)}) %collective-permute-start.12) | collective-permute-done | bytes 884768 | tf_op jit(solution)/shard_map/ppermute | solution.py:473
  70.3 1.6 shard_map.52
  71.9 1.6 shard_map.53
  73.5 1.6 shard_map.54
  75.2 0.3 maximum_add_fusion
  75.4 5.5 %gram.1 = (f32[16,128]{1,0:T(8,128)S(1)}, f32[8,32,8,128]{3,2,1,0:T(8,128)S(1)}) custom-call(f32[8,64,8,128]{3,2,1,0:T(8,128)S(1)} %bitcast.19, f32[8,64,8,128]{3,2,1,0:T(8,128)S(1)} %bitcast.23, f32[4,32,8,128]{3,2,1,0:T(8,128)S(1)} %bitcast.45, f32[4,32,8,128]{3,2,1,0:T(8,128)S(1)} %bitcast.47, f32[4,32,8,128]{3,2,1,0:T(8,128)S(1)} %bitcast.27, ...), custom_call_target="tpu_custom_call" | custom-call | tf_op jit(solution)/shard_map/gram/pallas_call | solution.py:576
  81.0 5.3 %collective-permute-start.14 = (f32[16,128]{1,0:T(8,128)S(1)}, f32[16,128]{1,0:T(8,128)S(1)}, u32[]{:S(2)}, u32[]{:S(2)}) collective-permute-start(f32[16,128]{1,0:T(8,128)S(1)} %get-tuple-element.51), channel_id=1, source_target_pairs={{0,2},{2,0},{4,6},{6,4},{8,10},{10,8},{12,14},{14,12},{16,18},{18,... | collective-permute-start | bytes 24584 | tf_op jit(solution)/shard_map/ppermute | solution.py:444
  86.3 0.8 collective-permute-done.14
  87.1 7.7 %collective-permute-start.15 = (f32[16,128]{1,0:T(8,128)S(1)}, f32[16,128]{1,0:T(8,128)S(1)}, u32[]{:S(2)}, u32[]{:S(2)}) collective-permute-start(f32[16,128]{1,0:T(8,128)S(1)} %add.64), channel_id=1, source_target_pairs={{0,4},{2,6},{4,8},{6,10},{8,12},{10,14},{12,0},{14,2},{16,20},{18,... | collective-permute-start | bytes 24584 | tf_op jit(solution)/shard_map/ppermute | solution.py:444
  94.8 0.9 collective-permute-start.17
  95.7 3.5 %collective-permute-start.25 = (f32[4,16,16,128]{3,2,1,0:T(8,128)S(1)}, f32[4,16,16,128]{3,2,1,0:T(8,128)S(1)}, u32[]{:S(2)}, u32[]{:S(2)}) collective-permute-start(f32[4,16,16,128]{3,2,1,0:T(8,128)S(1)} %get-tuple-element.46), channel_id=1, source_target_pairs={{0,1},{1,0},{2,3},{3,2},{4,5},{5,4},{6,7},{7,6},{8,9},{9,8},{10,11... | collective-permute-start | bytes 1572872 | tf_op jit(solution)/shard_map/ppermute | solution.py:567
  99.3 0.7 collective-permute-done.16
  100.1 5.2 %collective-permute-start.19 = (f32[16,128]{1,0:T(8,128)S(1)}, f32[16,128]{1,0:T(8,128)S(1)}, u32[]{:S(2)}, u32[]{:S(2)}) collective-permute-start(f32[16,128]{1,0:T(8,128)S(1)} %add_add_fusion.5), channel_id=1, source_target_pairs={{0,32},{2,34},{4,36},{6,38},{8,40},{10,42},{12,44},{14,46},{16,48}... | collective-permute-start | bytes 24584 | tf_op jit(solution)/shard_map/ppermute | solution.py:444
  105.3 1.2 collective-permute-start.20
  106.5 5.5 %collective-permute-start.36 = (f32[8,32,8,128]{3,2,1,0:T(8,128)S(1)}, f32[8,32,8,128]{3,2,1,0:T(8,128)S(1)}, u32[]{:S(2)}, u32[]{:S(2)}) collective-permute-start(f32[8,32,8,128]{3,2,1,0:T(8,128)S(1)} %get-tuple-element.58), channel_id=1, source_target_pairs={{0,1},{2,3},{4,5},{6,7},{8,9},{10,11},{12,13},{14,15},{16,17},{18,... | collective-permute-start | bytes 3145736 | tf_op jit(solution)/shard_map/ppermute | solution.py:588
  112.1 3.8 %collective-permute-start.21 = (f32[16,128]{1,0:T(8,128)S(1)}, f32[16,128]{1,0:T(8,128)S(1)}, u32[]{:S(2)}, u32[]{:S(2)}) collective-permute-start(f32[16,128]{1,0:T(8,128)S(1)} %add_add_fusion.4), channel_id=1, source_target_pairs={{0,64},{1,65},{2,66},{3,67},{4,68},{5,69},{6,70},{7,71},{8,72},{9,... | collective-permute-start | bytes 24584 | tf_op jit(solution)/shard_map/ppermute | solution.py:458
  115.9 2.2 %collective-permute-start.22 = (f32[16,128]{1,0:T(8,128)S(1)}, f32[16,128]{1,0:T(8,128)S(1)}, u32[]{:S(2)}, u32[]{:S(2)}) collective-permute-start(f32[16,128]{1,0:T(8,128)S(1)} %add_add_fusion.4), channel_id=1, source_target_pairs={{0,1},{1,0},{2,3},{3,2},{4,5},{5,4},{6,7},{7,6},{8,9},{9,8},{10,11... | collective-permute-start | bytes 24584 | tf_op jit(solution)/shard_map/ppermute | solution.py:458
  118.1 26.1 %collective-permute-done.21 = f32[16,128]{1,0:T(8,128)S(1)} collective-permute-done((f32[16,128]{1,0:T(8,128)S(1)}, f32[16,128]{1,0:T(8,128)S(1)}, u32[]{:S(2)}, u32[]{:S(2)}) %collective-permute-start.21) | collective-permute-done | bytes 8224 | tf_op jit(solution)/shard_map/ppermute | solution.py:458
  144.2 0.1 collective-permute-done.22
  144.3 4.0 %collective-permute-done.23 = f32[16,128]{1,0:T(8,128)S(1)} collective-permute-done((f32[16,128]{1,0:T(8,128)S(1)}, f32[16,128]{1,0:T(8,128)S(1)}, u32[]{:S(2)}, u32[]{:S(2)}) %collective-permute-start.23) | collective-permute-done | bytes 8224 | tf_op jit(solution)/shard_map/ppermute | solution.py:458
  148.3 2.7 %project.1 = (f32[16,16]{1,0:T(8,128)}, f32[16,16]{1,0:T(8,128)S(1)}, f32[16,16]{1,0:T(8,128)S(1)}, f32[16,16,128]{2,1,0:T(8,128)S(1)}) custom-call(f32[16,128]{1,0:T(8,128)S(1)} %add_add_fusion.3.gram_ref), custom_call_target="tpu_custom_call" | custom-call | tf_op jit(solution)/shard_map/project/pallas_call | solution.py:592
  151.0 4.3 %residual.1 = f32[16,128]{1,0:T(8,128)S(1)} custom-call(f32[16,16,128]{2,1,0:T(8,128)S(1)} %get-tuple-element.53.table_ref, f32[8,64,8,128]{3,2,1,0:T(8,128)S(1)} %bitcast.20, f32[8,64,8,128]{3,2,1,0:T(8,128)S(1)} %bitcast.24, f32[4,32,8,128]{3,2,1,0:T(8,128)S(1)} %bitcast.28, f32[4,32,8,128]{3,2,1,0:T(8,128)S(1)} %bitcast.31, ...), custom_call_target="tpu_custom_call" | custom-call | tf_op jit(solution)/shard_map/residual/pallas_call | solution.py:600
  155.4 0.1 collective-permute-start.26
  155.5 1.2 collective-permute-done.26
  156.6 2.4 %collective-permute-start.27 = (f32[16,128]{1,0:T(8,128)S(1)}, f32[16,128]{1,0:T(8,128)S(1)}, u32[]{:S(2)}, u32[]{:S(2)}) collective-permute-start(f32[16,128]{1,0:T(8,128)S(1)} %add.74), channel_id=1, source_target_pairs={{0,4},{2,6},{4,8},{6,10},{8,12},{10,14},{12,0},{14,2},{16,20},{18,... | collective-permute-start | bytes 24584 | tf_op jit(solution)/shard_map/ppermute | solution.py:444
  159.0 2.0 %collective-permute-start.28 = (f32[16,128]{1,0:T(8,128)S(1)}, f32[16,128]{1,0:T(8,128)S(1)}, u32[]{:S(2)}, u32[]{:S(2)}) collective-permute-start(f32[16,128]{1,0:T(8,128)S(1)} %add.74), channel_id=1, source_target_pairs={{0,8},{2,10},{4,12},{6,14},{8,0},{10,2},{12,4},{14,6},{16,24},{18,... | collective-permute-start | bytes 24584 | tf_op jit(solution)/shard_map/ppermute | solution.py:444
  161.0 3.1 %collective-permute-done.28 = f32[16,128]{1,0:T(8,128)S(1)} collective-permute-done((f32[16,128]{1,0:T(8,128)S(1)}, f32[16,128]{1,0:T(8,128)S(1)}, u32[]{:S(2)}, u32[]{:S(2)}) %collective-permute-start.28) | collective-permute-done | bytes 8224 | tf_op jit(solution)/shard_map/ppermute | solution.py:444
  164.2 1.7 collective-permute-done.29
  165.9 6.6 %collective-permute-start.31 = (f32[16,128]{1,0:T(8,128)S(1)}, f32[16,128]{1,0:T(8,128)S(1)}, u32[]{:S(2)}, u32[]{:S(2)}) collective-permute-start(f32[16,128]{1,0:T(8,128)S(1)} %add_add_fusion.2), channel_id=1, source_target_pairs={{0,32},{2,34},{4,36},{6,38},{8,40},{10,42},{12,44},{14,46},{16,48}... | collective-permute-start | bytes 24584 | tf_op jit(solution)/shard_map/ppermute | solution.py:444
  172.5 1.6 collective-permute-done.31
  174.1 2.0 %collective-permute-done.32 = f32[16,128]{1,0:T(8,128)S(1)} collective-permute-done((f32[16,128]{1,0:T(8,128)S(1)}, f32[16,128]{1,0:T(8,128)S(1)}, u32[]{:S(2)}, u32[]{:S(2)}) %collective-permute-start.32) | collective-permute-done | bytes 8224 | tf_op jit(solution)/shard_map/ppermute | solution.py:444
  176.2 4.1 %collective-permute-start.34 = (f32[16,128]{1,0:T(8,128)S(1)}, f32[16,128]{1,0:T(8,128)S(1)}, u32[]{:S(2)}, u32[]{:S(2)}) collective-permute-start(f32[16,128]{1,0:T(8,128)S(1)} %add_add_fusion.1), channel_id=1, source_target_pairs={{0,1},{1,0},{2,3},{3,2},{4,5},{5,4},{6,7},{7,6},{8,9},{9,8},{10,11... | collective-permute-start | bytes 24584 | tf_op jit(solution)/shard_map/ppermute | solution.py:458
  180.3 0.8 collective-permute-done.33
  181.0 0.9 collective-permute-done.34
  182.0 1.9 %collective-permute-done.35 = f32[16,128]{1,0:T(8,128)S(1)} collective-permute-done((f32[16,128]{1,0:T(8,128)S(1)}, f32[16,128]{1,0:T(8,128)S(1)}, u32[]{:S(2)}, u32[]{:S(2)}) %collective-permute-start.35) | collective-permute-done | bytes 8224 | tf_op jit(solution)/shard_map/ppermute | solution.py:458
  183.9 2.7 %algebra.1 = (f32[16,16]{1,0:T(8,128)}, f32[32,8,128]{2,1,0:T(8,128)S(1)}) custom-call(f32[16,128]{1,0:T(8,128)S(1)} %add_add_fusion.gram_ref, f32[16,16]{1,0:T(8,128)S(1)} %get-tuple-element.54.inverse_ref, f32[16,16]{1,0:T(8,128)S(1)} %get-tuple-element.55.mix_ref), custom_call_target="tpu_custom_call" | custom-call | tf_op jit(solution)/shard_map/algebra/pallas_call | solution.py:613
  186.6 3.3 %combine_mine.1.refs_3_ = f32[8,64,8,128]{3,2,1,0:T(8,128)} custom-call(f32[32,8,128]{2,1,0:T(8,128)S(1)} %get-tuple-element.57.table_ref, f32[8,64,8,128]{3,2,1,0:T(8,128)S(1)} %bitcast.21, f32[8,64,8,128]{3,2,1,0:T(8,128)S(1)} %bitcast.25, f32[4,32,8,128]{3,2,1,0:T(8,128)S(1)} %bitcast.29, f32[4,32,8,128]{3,2,1,0:T(8,128)S(1)} %bitcast.32, ...), custom_call_target="tpu_custom_call" | custom-call | tf_op jit(solution)/shard_map/combine_mine/pallas_call | solution.py:625
  189.9 3.6 %combine_theirs.1 = f32[8,64,8,128]{3,2,1,0:T(8,128)} custom-call(f32[32,8,128]{2,1,0:T(8,128)S(1)} %get-tuple-element.57.table_ref, f32[8,64,8,128]{3,2,1,0:T(8,128)S(1)} %bitcast.22, f32[8,64,8,128]{3,2,1,0:T(8,128)S(1)} %bitcast.26, f32[4,32,8,128]{3,2,1,0:T(8,128)S(1)} %bitcast.46, ...), custom_call_target="tpu_custom_call", output_to_operand_aliasing={{}: (6, {})} | custom-call | tf_op jit(solution)/shard_map/combine_theirs/pallas_call | solution.py:625
  (40 shorter events, 0.2 us)
Async XLA Ops:
  0.6 3.9 %copy-start.1 = (s32[8,32,16,128]{3,2,1,0:T(8,128)S(1)}, s32[8,32,16,128]{3,2,1,0:T(8,128)}, u32[]{:S(2)}) copy-start(s32[8,32,16,128]{3,2,1,0:T(8,128)} %param.3) | copy-start | bytes 6291460
  2.6 8.6 %collective-permute-start.5 = (f32[40,16,128]{2,1,0:T(8,128)}, f32[40,16,128]{2,1,0:T(8,128)S(1)}, u32[]{:S(2)}, u32[]{:S(2)}) collective-permute-start(f32[40,16,128]{2,1,0:T(8,128)} %tail.1), channel_id=1, source_target_pairs={{0,2},{2,4},{4,6},{6,8},{8,10},{10,12},{12,14},{14,16},{16,18},{18... | collective-permute-start | bytes 983048 | tf_op jit(solution)/shard_map/ppermute | solution.py:473
  4.7 6.5 %copy-start = (s32[12,32,16,128]{3,2,1,0:T(8,128)S(1)}, s32[12,32,16,128]{3,2,1,0:T(8,128)}, u32[]{:S(2)}) copy-start(s32[12,32,16,128]{3,2,1,0:T(8,128)} %levels_ref.5) | copy-start | bytes 9437188
  4.9 32.5 %collective-permute-start.1 = (f32[4,32,16,128]{3,2,1,0:T(8,128)S(1)}, f32[4,32,16,128]{3,2,1,0:T(8,128)S(1)}, u32[]{:S(2)}, u32[]{:S(2)}) collective-permute-start(f32[4,32,16,128]{3,2,1,0:T(8,128)S(1)} %get-tuple-element.59), channel_id=1, source_target_pairs={{0,17},{1,16},{2,7},{3,6},{124,77},{125,76},{126,115},{127,114}} | collective-permute-start | bytes 3145736 | tf_op jit(solution)/shard_map/ppermute | solution.py:497
  5.8 37.3 %collective-permute-start.3 = (f32[4,32,16,128]{3,2,1,0:T(8,128)S(1)}, f32[4,32,16,128]{3,2,1,0:T(8,128)S(1)}, u32[]{:S(2)}, u32[]{:S(2)}) collective-permute-start(f32[4,32,16,128]{3,2,1,0:T(8,128)S(1)} %get-tuple-element.60), channel_id=1, source_target_pairs={{0,49},{1,48},{2,15},{3,14},{124,109},{125,108},{126,123},{127,122}} | collective-permute-start | bytes 3145736 | tf_op jit(solution)/shard_map/ppermute | solution.py:497
  12.6 14.4 %collective-permute-start.6 = (f32[4,27,16,128]{3,2,1,0:T(8,128)S(1)}, f32[4,27,16,128]{3,2,1,0:T(8,128)S(1)}, u32[]{:S(2)}, u32[]{:S(2)}) collective-permute-start(f32[4,27,16,128]{3,2,1,0:T(8,128)S(1)} %get-tuple-element.32), channel_id=1, source_target_pairs={{0,2},{2,4},{4,6},{6,8},{8,10},{10,12},{12,14},{14,16},{16,18},{18... | collective-permute-start | bytes 2654216 | tf_op jit(solution)/shard_map/ppermute | solution.py:473
  14.6 15.2 %collective-permute-start.7 = (f32[4,27,16,128]{3,2,1,0:T(8,128)S(1)}, f32[4,27,16,128]{3,2,1,0:T(8,128)S(1)}, u32[]{:S(2)}, u32[]{:S(2)}) collective-permute-start(f32[4,27,16,128]{3,2,1,0:T(8,128)S(1)} %get-tuple-element.33), channel_id=1, source_target_pairs={{2,0},{4,2},{6,4},{8,6},{10,8},{12,10},{14,12},{16,14},{18,16},{20... | collective-permute-start | bytes 2654216 | tf_op jit(solution)/shard_map/ppermute | solution.py:476
  18.2 56.9 %collective-permute-start = (f32[8,32,16,128]{3,2,1,0:T(8,128)S(1)}, f32[8,32,16,128]{3,2,1,0:T(8,128)S(1)}, u32[]{:S(2)}, u32[]{:S(2)}) collective-permute-start(f32[8,32,16,128]{3,2,1,0:T(8,128)S(1)} %convert_element_type.3.start_ref.own_ref), channel_id=1, source_target_pairs={{4,5},{5,4},{6,7},{7,6},{8,9},{9,8},{10,11},{11,10},{12,13},{13,12... | collective-permute-start | bytes 6291464 | tf_op jit(solution)/shard_map/ppermute | solution.py:499
  27.0 18.0 %collective-permute-start.8 = (f32[4,27,16,128]{3,2,1,0:T(8,128)S(1)}, f32[4,27,16,128]{3,2,1,0:T(8,128)S(1)}, u32[]{:S(2)}, u32[]{:S(2)}) collective-permute-start(f32[4,27,16,128]{3,2,1,0:T(8,128)S(1)} %get-tuple-element.35), channel_id=1, source_target_pairs={{0,2},{2,4},{4,6},{6,8},{8,10},{10,12},{12,14},{14,16},{16,18},{18... | collective-permute-start | bytes 2654216 | tf_op jit(solution)/shard_map/ppermute | solution.py:473
  29.8 15.9 %collective-permute-start.9 = (f32[4,27,16,128]{3,2,1,0:T(8,128)S(1)}, f32[4,27,16,128]{3,2,1,0:T(8,128)S(1)}, u32[]{:S(2)}, u32[]{:S(2)}) collective-permute-start(f32[4,27,16,128]{3,2,1,0:T(8,128)S(1)} %get-tuple-element.36), channel_id=1, source_target_pairs={{2,0},{4,2},{6,4},{8,6},{10,8},{12,10},{14,12},{16,14},{18,16},{20... | collective-permute-start | bytes 2654216 | tf_op jit(solution)/shard_map/ppermute | solution.py:476
  37.4 14.4 %collective-permute-start.10 = (f32[4,27,16,128]{3,2,1,0:T(8,128)S(1)}, f32[4,27,16,128]{3,2,1,0:T(8,128)S(1)}, u32[]{:S(2)}, u32[]{:S(2)}) collective-permute-start(f32[4,27,16,128]{3,2,1,0:T(8,128)S(1)} %get-tuple-element.39), channel_id=1, source_target_pairs={{0,2},{2,4},{4,6},{6,8},{8,10},{10,12},{12,14},{14,16},{16,18},{18... | collective-permute-start | bytes 2654216 | tf_op jit(solution)/shard_map/ppermute | solution.py:473
  43.0 12.5 %collective-permute-start.11 = (f32[4,27,16,128]{3,2,1,0:T(8,128)S(1)}, f32[4,27,16,128]{3,2,1,0:T(8,128)S(1)}, u32[]{:S(2)}, u32[]{:S(2)}) collective-permute-start(f32[4,27,16,128]{3,2,1,0:T(8,128)S(1)} %get-tuple-element.40), channel_id=1, source_target_pairs={{2,0},{4,2},{6,4},{8,6},{10,8},{12,10},{14,12},{16,14},{18,16},{20... | collective-permute-start | bytes 2654216 | tf_op jit(solution)/shard_map/ppermute | solution.py:476
  45.0 30.2 %collective-permute-start.2 = (f32[4,32,16,128]{3,2,1,0:T(8,128)S(1)}, f32[4,32,16,128]{3,2,1,0:T(8,128)S(1)}, u32[]{:S(2)}, u32[]{:S(2)}) collective-permute-start(f32[4,32,16,128]{3,2,1,0:T(8,128)S(1)} %collective-permute-done.1), channel_id=1, source_target_pairs={{17,1},{16,0},{7,3},{6,2},{77,125},{76,124},{115,127},{114,126}} | collective-permute-start | bytes 3145736 | tf_op jit(solution)/shard_map/ppermute | solution.py:498
  45.7 29.4 %collective-permute-start.4 = (f32[4,32,16,128]{3,2,1,0:T(8,128)S(1)}, f32[4,32,16,128]{3,2,1,0:T(8,128)S(1)}, u32[]{:S(2)}, u32[]{:S(2)}) collective-permute-start(f32[4,32,16,128]{3,2,1,0:T(8,128)S(1)} %collective-permute-done.3), channel_id=1, source_target_pairs={{49,1},{48,0},{15,3},{14,2},{109,125},{108,124},{123,127},{122,126}} | collective-permute-start | bytes 3145736 | tf_op jit(solution)/shard_map/ppermute | solution.py:498
  51.7 15.4 %collective-permute-start.13 = (f32[4,27,16,128]{3,2,1,0:T(8,128)S(1)}, f32[4,27,16,128]{3,2,1,0:T(8,128)S(1)}, u32[]{:S(2)}, u32[]{:S(2)}) collective-permute-start(f32[4,27,16,128]{3,2,1,0:T(8,128)S(1)} %get-tuple-element.45), channel_id=1, source_target_pairs={{2,0},{4,2},{6,4},{8,6},{10,8},{12,10},{14,12},{16,14},{18,16},{20... | collective-permute-start | bytes 2654216 | tf_op jit(solution)/shard_map/ppermute | solution.py:476
  55.5 14.8 %collective-permute-start.12 = (f32[4,27,16,128]{3,2,1,0:T(8,128)S(1)}, f32[4,27,16,128]{3,2,1,0:T(8,128)S(1)}, u32[]{:S(2)}, u32[]{:S(2)}) collective-permute-start(f32[4,27,16,128]{3,2,1,0:T(8,128)S(1)} %get-tuple-element.44), channel_id=1, source_target_pairs={{0,2},{2,4},{4,6},{6,8},{8,10},{10,12},{12,14},{14,16},{16,18},{18... | collective-permute-start | bytes 2654216 | tf_op jit(solution)/shard_map/ppermute | solution.py:473
  81.0 6.1 %collective-permute-start.14 = (f32[16,128]{1,0:T(8,128)S(1)}, f32[16,128]{1,0:T(8,128)S(1)}, u32[]{:S(2)}, u32[]{:S(2)}) collective-permute-start(f32[16,128]{1,0:T(8,128)S(1)} %get-tuple-element.51), channel_id=1, source_target_pairs={{0,2},{2,0},{4,6},{6,4},{8,10},{10,8},{12,14},{14,12},{16,18},{18,... | collective-permute-start | bytes 24584 | tf_op jit(solution)/shard_map/ppermute | solution.py:444
  87.1 12.2 %collective-permute-start.15 = (f32[16,128]{1,0:T(8,128)S(1)}, f32[16,128]{1,0:T(8,128)S(1)}, u32[]{:S(2)}, u32[]{:S(2)}) collective-permute-start(f32[16,128]{1,0:T(8,128)S(1)} %add.64), channel_id=1, source_target_pairs={{0,4},{2,6},{4,8},{6,10},{8,12},{10,14},{12,0},{14,2},{16,20},{18,... | collective-permute-start | bytes 24584 | tf_op jit(solution)/shard_map/ppermute | solution.py:444
  94.8 5.2 %collective-permute-start.16 = (f32[16,128]{1,0:T(8,128)S(1)}, f32[16,128]{1,0:T(8,128)S(1)}, u32[]{:S(2)}, u32[]{:S(2)}) collective-permute-start(f32[16,128]{1,0:T(8,128)S(1)} %add.64), channel_id=1, source_target_pairs={{0,8},{2,10},{4,12},{6,14},{8,0},{10,2},{12,4},{14,6},{16,24},{18,... | collective-permute-start | bytes 24584 | tf_op jit(solution)/shard_map/ppermute | solution.py:444
  94.8 5.2 %collective-permute-start.17 = (f32[16,128]{1,0:T(8,128)S(1)}, f32[16,128]{1,0:T(8,128)S(1)}, u32[]{:S(2)}, u32[]{:S(2)}) collective-permute-start(f32[16,128]{1,0:T(8,128)S(1)} %add.64), channel_id=1, source_target_pairs={{0,12},{2,14},{4,0},{6,2},{8,4},{10,6},{12,8},{14,10},{16,28},{18,... | collective-permute-start | bytes 24584 | tf_op jit(solution)/shard_map/ppermute | solution.py:444
  95.7 55.3 %collective-permute-start.25 = (f32[4,16,16,128]{3,2,1,0:T(8,128)S(1)}, f32[4,16,16,128]{3,2,1,0:T(8,128)S(1)}, u32[]{:S(2)}, u32[]{:S(2)}) collective-permute-start(f32[4,16,16,128]{3,2,1,0:T(8,128)S(1)} %get-tuple-element.46), channel_id=1, source_target_pairs={{0,1},{1,0},{2,3},{3,2},{4,5},{5,4},{6,7},{7,6},{8,9},{9,8},{10,11... | collective-permute-start | bytes 1572872 | tf_op jit(solution)/shard_map/ppermute | solution.py:567
  99.2 51.8 %collective-permute-start.24 = (f32[4,16,16,128]{3,2,1,0:T(8,128)S(1)}, f32[4,16,16,128]{3,2,1,0:T(8,128)S(1)}, u32[]{:S(2)}, u32[]{:S(2)}) collective-permute-start(f32[4,16,16,128]{3,2,1,0:T(8,128)S(1)} %get-tuple-element.41), channel_id=1, source_target_pairs={{0,1},{1,0},{2,3},{3,2},{4,5},{5,4},{6,7},{7,6},{8,9},{9,8},{10,11... | collective-permute-start | bytes 1572872 | tf_op jit(solution)/shard_map/ppermute | solution.py:567
  100.0 6.5 %collective-permute-start.18 = (f32[16,128]{1,0:T(8,128)S(1)}, f32[16,128]{1,0:T(8,128)S(1)}, u32[]{:S(2)}, u32[]{:S(2)}) collective-permute-start(f32[16,128]{1,0:T(8,128)S(1)} %add_add_fusion.5), channel_id=1, source_target_pairs={{0,16},{2,18},{4,20},{6,22},{8,24},{10,26},{12,28},{14,30},{16,32}... | collective-permute-start | bytes 24584 | tf_op jit(solution)/shard_map/ppermute | solution.py:444
  100.1 12.0 %collective-permute-start.19 = (f32[16,128]{1,0:T(8,128)S(1)}, f32[16,128]{1,0:T(8,128)S(1)}, u32[]{:S(2)}, u32[]{:S(2)}) collective-permute-start(f32[16,128]{1,0:T(8,128)S(1)} %add_add_fusion.5), channel_id=1, source_target_pairs={{0,32},{2,34},{4,36},{6,38},{8,40},{10,42},{12,44},{14,46},{16,48}... | collective-permute-start | bytes 24584 | tf_op jit(solution)/shard_map/ppermute | solution.py:444
  105.3 6.8 %collective-permute-start.20 = (f32[16,128]{1,0:T(8,128)S(1)}, f32[16,128]{1,0:T(8,128)S(1)}, u32[]{:S(2)}, u32[]{:S(2)}) collective-permute-start(f32[16,128]{1,0:T(8,128)S(1)} %add_add_fusion.5), channel_id=1, source_target_pairs={{0,48},{2,50},{4,52},{6,54},{8,56},{10,58},{12,60},{14,62},{16,0},... | collective-permute-start | bytes 24584 | tf_op jit(solution)/shard_map/ppermute | solution.py:444
  106.5 83.4 %collective-permute-start.36 = (f32[8,32,8,128]{3,2,1,0:T(8,128)S(1)}, f32[8,32,8,128]{3,2,1,0:T(8,128)S(1)}, u32[]{:S(2)}, u32[]{:S(2)}) collective-permute-start(f32[8,32,8,128]{3,2,1,0:T(8,128)S(1)} %get-tuple-element.58), channel_id=1, source_target_pairs={{0,1},{2,3},{4,5},{6,7},{8,9},{10,11},{12,13},{14,15},{16,17},{18,... | collective-permute-start | bytes 3145736 | tf_op jit(solution)/shard_map/ppermute | solution.py:588
  112.1 32.1 %collective-permute-start.21 = (f32[16,128]{1,0:T(8,128)S(1)}, f32[16,128]{1,0:T(8,128)S(1)}, u32[]{:S(2)}, u32[]{:S(2)}) collective-permute-start(f32[16,128]{1,0:T(8,128)S(1)} %add_add_fusion.4), channel_id=1, source_target_pairs={{0,64},{1,65},{2,66},{3,67},{4,68},{5,69},{6,70},{7,71},{8,72},{9,... | collective-permute-start | bytes 24584 | tf_op jit(solution)/shard_map/ppermute | solution.py:458
  115.9 28.4 %collective-permute-start.22 = (f32[16,128]{1,0:T(8,128)S(1)}, f32[16,128]{1,0:T(8,128)S(1)}, u32[]{:S(2)}, u32[]{:S(2)}) collective-permute-start(f32[16,128]{1,0:T(8,128)S(1)} %add_add_fusion.4), channel_id=1, source_target_pairs={{0,1},{1,0},{2,3},{3,2},{4,5},{5,4},{6,7},{7,6},{8,9},{9,8},{10,11... | collective-permute-start | bytes 24584 | tf_op jit(solution)/shard_map/ppermute | solution.py:458
  144.2 4.1 %collective-permute-start.23 = (f32[16,128]{1,0:T(8,128)S(1)}, f32[16,128]{1,0:T(8,128)S(1)}, u32[]{:S(2)}, u32[]{:S(2)}) collective-permute-start(f32[16,128]{1,0:T(8,128)S(1)} %add_add_fusion.4), channel_id=1, source_target_pairs={{0,65},{1,64},{2,67},{3,66},{4,69},{5,68},{6,71},{7,70},{8,73},{9,... | collective-permute-start | bytes 24584 | tf_op jit(solution)/shard_map/ppermute | solution.py:458
  155.4 1.3 collective-permute-start.26
  156.6 4.4 %collective-permute-start.27 = (f32[16,128]{1,0:T(8,128)S(1)}, f32[16,128]{1,0:T(8,128)S(1)}, u32[]{:S(2)}, u32[]{:S(2)}) collective-permute-start(f32[16,128]{1,0:T(8,128)S(1)} %add.74), channel_id=1, source_target_pairs={{0,4},{2,6},{4,8},{6,10},{8,12},{10,14},{12,0},{14,2},{16,20},{18,... | collective-permute-start | bytes 24584 | tf_op jit(solution)/shard_map/ppermute | solution.py:444
  159.0 5.2 %collective-permute-start.28 = (f32[16,128]{1,0:T(8,128)S(1)}, f32[16,128]{1,0:T(8,128)S(1)}, u32[]{:S(2)}, u32[]{:S(2)}) collective-permute-start(f32[16,128]{1,0:T(8,128)S(1)} %add.74), channel_id=1, source_target_pairs={{0,8},{2,10},{4,12},{6,14},{8,0},{10,2},{12,4},{14,6},{16,24},{18,... | collective-permute-start | bytes 24584 | tf_op jit(solution)/shard_map/ppermute | solution.py:444
  161.0 4.9 %collective-permute-start.29 = (f32[16,128]{1,0:T(8,128)S(1)}, f32[16,128]{1,0:T(8,128)S(1)}, u32[]{:S(2)}, u32[]{:S(2)}) collective-permute-start(f32[16,128]{1,0:T(8,128)S(1)} %add.74), channel_id=1, source_target_pairs={{0,12},{2,14},{4,0},{6,2},{8,4},{10,6},{12,8},{14,10},{16,28},{18,... | collective-permute-start | bytes 24584 | tf_op jit(solution)/shard_map/ppermute | solution.py:444
  165.9 6.6 %collective-permute-start.30 = (f32[16,128]{1,0:T(8,128)S(1)}, f32[16,128]{1,0:T(8,128)S(1)}, u32[]{:S(2)}, u32[]{:S(2)}) collective-permute-start(f32[16,128]{1,0:T(8,128)S(1)} %add_add_fusion.2), channel_id=1, source_target_pairs={{0,16},{2,18},{4,20},{6,22},{8,24},{10,26},{12,28},{14,30},{16,32}... | collective-permute-start | bytes 24584 | tf_op jit(solution)/shard_map/ppermute | solution.py:444
  165.9 8.2 %collective-permute-start.31 = (f32[16,128]{1,0:T(8,128)S(1)}, f32[16,128]{1,0:T(8,128)S(1)}, u32[]{:S(2)}, u32[]{:S(2)}) collective-permute-start(f32[16,128]{1,0:T(8,128)S(1)} %add_add_fusion.2), channel_id=1, source_target_pairs={{0,32},{2,34},{4,36},{6,38},{8,40},{10,42},{12,44},{14,46},{16,48}... | collective-permute-start | bytes 24584 | tf_op jit(solution)/shard_map/ppermute | solution.py:444
  172.5 3.7 %collective-permute-start.32 = (f32[16,128]{1,0:T(8,128)S(1)}, f32[16,128]{1,0:T(8,128)S(1)}, u32[]{:S(2)}, u32[]{:S(2)}) collective-permute-start(f32[16,128]{1,0:T(8,128)S(1)} %add_add_fusion.2), channel_id=1, source_target_pairs={{0,48},{2,50},{4,52},{6,54},{8,56},{10,58},{12,60},{14,62},{16,0},... | collective-permute-start | bytes 24584 | tf_op jit(solution)/shard_map/ppermute | solution.py:444
  176.2 4.9 %collective-permute-start.33 = (f32[16,128]{1,0:T(8,128)S(1)}, f32[16,128]{1,0:T(8,128)S(1)}, u32[]{:S(2)}, u32[]{:S(2)}) collective-permute-start(f32[16,128]{1,0:T(8,128)S(1)} %add_add_fusion.1), channel_id=1, source_target_pairs={{0,64},{1,65},{2,66},{3,67},{4,68},{5,69},{6,70},{7,71},{8,72},{9,... | collective-permute-start | bytes 24584 | tf_op jit(solution)/shard_map/ppermute | solution.py:458
  176.2 5.8 %collective-permute-start.34 = (f32[16,128]{1,0:T(8,128)S(1)}, f32[16,128]{1,0:T(8,128)S(1)}, u32[]{:S(2)}, u32[]{:S(2)}) collective-permute-start(f32[16,128]{1,0:T(8,128)S(1)} %add_add_fusion.1), channel_id=1, source_target_pairs={{0,1},{1,0},{2,3},{3,2},{4,5},{5,4},{6,7},{7,6},{8,9},{9,8},{10,11... | collective-permute-start | bytes 24584 | tf_op jit(solution)/shard_map/ppermute | solution.py:458
  180.3 3.7 %collective-permute-start.35 = (f32[16,128]{1,0:T(8,128)S(1)}, f32[16,128]{1,0:T(8,128)S(1)}, u32[]{:S(2)}, u32[]{:S(2)}) collective-permute-start(f32[16,128]{1,0:T(8,128)S(1)} %add_add_fusion.1), channel_id=1, source_target_pairs={{0,65},{1,64},{2,67},{3,66},{4,69},{5,68},{6,71},{7,70},{8,73},{9,... | collective-permute-start | bytes 24584 | tf_op jit(solution)/shard_map/ppermute | solution.py:458
